TPU v7x, 32 devices: a whole 2x2x4 slice. The times are simulated.
32 devices in a mesh: section: 4 (over y, core), dom: 8 (over z, x).
Axes of the slice: x: 2, y: 2, z: 4, core: 2. Of those that a mesh axis runs over, the one named last changes fastest.
Arguments:
- initial_feat: bfloat16 [2, 2048, 1024], P(None, 'dom'), may hold values from -6 to 6
- layer_weight: bfloat16 [4, 1024, 1024], P('section'), may hold values from -1.35 to 1.35
- tile_column: int32 [8, 2, 2, 4], P('dom'), may hold values from 0 to 1, as said below
- tile_values: bfloat16 [8, 2, 2, 4, 128, 128], P('dom'), may hold values from 0 to 0.05625, as said below
- send_rows: int32 [8, 2, 8, 16], P('dom'), may hold values from 0 to 255
Outputs:
- activations: bfloat16 [4, 2, 2048, 1024], P('section', None, 'dom')
Inputs may be any that keep to these rules, and one draw needn't show every extreme that they name: `tile_column`: each of the two column blocks appears in at least one of the 4 tiles of every partition, node batch and row block. `tile_values`: each row of a tile has a few nonzero weights; the weights of one row over all tiles of its row block sum to about one.
All inputs are finite; a program needn't handle non-finite values.
Results may differ from a plain program's by a relative error of at most 0.006.
Values may be sent and summed in bfloat16 or wider, within the bound.
No kernel may reach another device: no remote copies, remote signals or barrier semaphores. Data moves between devices by JAX's collectives and lax.ppermute only.
A program may use at most 64 MiB of HBM per device.

v0:
```python
import jax
import jax.numpy as jnp
from jax import lax
from jax.sharding import PartitionSpec as P

restart = 0.1
strength = 0.5


def passed_along(x, axis, by):
    devices = lax.axis_size(axis)
    pairs = [(i, i + by) for i in range(devices) if 0 <= i + by < devices]
    return lax.ppermute(x, axis, pairs)


def take_rows(matrix, indices):
    picked = jnp.take(matrix, indices.reshape(-1), axis=0)
    return picked.reshape(indices.shape + (matrix.shape[-1],))


def combine_tiles(current, boundary, tile_weights, tile_block):
    block_count = tile_weights.shape[0]
    side = tile_weights.shape[-1]
    width = current.shape[-1]
    row_blocks = current.reshape(block_count, side, width)
    is_own = (tile_block == 0)[:, :, None, None]
    gathered = jnp.where(is_own, row_blocks[:, None], boundary[None, None])
    summed = jnp.einsum(
        "rtij,rtjf->rif", tile_weights, gathered, preferred_element_type=jnp.float32
    )
    return summed.reshape(block_count * side, width)


def gcn_layer(current, boundary, initial, tile_weights, tile_block, weight_now, beta_mix):
    aggregate = combine_tiles(current, boundary, tile_weights, tile_block)
    mixed_in = ((1.0 - restart) * aggregate + restart * initial.astype(jnp.float32)).astype(
        jnp.bfloat16
    )
    product = jnp.dot(mixed_in, weight_now, preferred_element_type=jnp.float32)
    return jax.nn.relu((1.0 - beta_mix) * mixed_in.astype(jnp.float32) + beta_mix * product).astype(
        jnp.bfloat16
    )


def on_device(initial_feat, layer_weight, tile_column, tile_values, send_rows):
    section_count = lax.axis_size("section")
    section_pos = lax.axis_index("section")
    batch_count = initial_feat.shape[0]
    width = initial_feat.shape[-1]
    side = tile_values.shape[-1]
    layer_pos = (section_pos + 1).astype(jnp.float32)
    beta_mix = jnp.log(strength / layer_pos + 1.0)
    weight_now = layer_weight[0]
    block_all = tile_column[0]
    weights_all = tile_values[0]
    sends_all = send_rows[0]
    tick_count = section_count + batch_count - 1
    stored = jnp.zeros_like(initial_feat)

    def batch_inputs(tick_num):
        batch_num = tick_num - section_pos
        active_now = (batch_num >= 0) & (batch_num < batch_count)
        batch_id = jnp.clip(batch_num, 0, batch_count - 1)
        initial = lax.dynamic_index_in_dim(initial_feat, batch_id, 0, keepdims=False)
        tile_weights = lax.dynamic_index_in_dim(weights_all, batch_id, 0, keepdims=False)
        tile_block = lax.dynamic_index_in_dim(block_all, batch_id, 0, keepdims=False)
        send_now = lax.dynamic_index_in_dim(sends_all, batch_id, 0, keepdims=False)
        return (active_now, batch_id, initial, tile_weights, tile_block, send_now)

    def apply_layer(
        active_now, batch_id, current, boundary, initial, tile_weights, tile_block, stored
    ):

        def compute(operand):
            output = gcn_layer(
                current, boundary, initial, tile_weights, tile_block, weight_now, beta_mix
            )
            return (output, lax.dynamic_update_index_in_dim(stored, output, batch_id, 0))

        def skipped(operand):
            return (jnp.zeros_like(current), stored)

        return lax.cond(active_now, compute, skipped, current)

    def tick_step(tick_num, carry):
        received, stored = carry
        active_now, batch_id, initial, tile_weights, tile_block, send_now = batch_inputs(tick_num)
        current = jnp.where(section_pos == 0, initial, received)
        outgoing = take_rows(current, send_now)
        boundary = lax.all_to_all(outgoing, "dom", split_axis=0, concat_axis=0, tiled=True).reshape(
            side, width
        )
        output, stored = apply_layer(
            active_now, batch_id, current, boundary, initial, tile_weights, tile_block, stored
        )
        received = passed_along(output, "section", 1)
        return (received, stored)

    start_rows = jnp.zeros(initial_feat.shape[1:], jnp.bfloat16)
    finished = lax.fori_loop(0, tick_count, tick_step, (start_rows, stored))
    stored = finished[1]
    return stored[None]


def solution(mesh):
    in_specs = (
        P(None, "dom", None),
        P("section", None, None),
        P("dom", None, None, None),
        P("dom", None, None, None, None, None),
        P("dom", None, None, None),
    )
    out_specs = P("section", None, "dom", None)
    return jax.shard_map(
        on_device, mesh=mesh, in_specs=in_specs, out_specs=out_specs, check_vma=False
    )
```

profile of v0, /device:TPU:1, one launch (start us, length us, event | category | flops | bytes accessed | tf_op | source)
XLA Modules:
  0.0 138.1 jit_solution(13990132352387187109)
XLA Ops:
  0.1 0.1 broadcast.81
  0.2 0.1 broadcast_in_dim.67
  0.3 136.9 %while.19 = (s32[]{:T(128)}, bf16[256,1024]{1,0:T(8,128)(2,1)S(1)}, bf16[2,256,1024]{2,1,0:T(8,128)(2,1)S(1)}, s32[]{:T(128)}, pred[]{:T(512)}, /*index=5*/bf16[...) while((s32[]{:T(128)}, bf16[256,1024]{1,0:T(8,128)(2,1)S(1)}, ...), condition=%wide.region_3.4_spmd, body=%wide.region_0.3_spmd.sunk | while | flops 809633920 | bytes 24913448 | solution.py:100
  0.3 0.7 compare_and_fusion.2
  1.0 0.1 reshape.89
  1.1 1.1 broadcast_select_fusion.4
  2.2 0.9 gather_fusion
  3.1 0.8 broadcast_select_fusion.5
  3.9 6.3 %all-to-all-start = ((bf16[8,16,1024]{2,1,0:T(8,128)(2,1)}), bf16[8,16,1024]{2,1,0:T(8,128)(2,1)S(1)}, u32[]{:S(2)}, u32[]{:S(2)}) async-start(bf16[8,16,1024]{2,1,0:T(8,128)(2,1)} %broadcast_select_fusion.5), calls=%async_computation | async-start | bytes 524288 | tf_op jit(solution)/shard_map/while/body/eval_jaxpr/all_to_all | solution.py:90
  10.2 7.4 %all-to-all-done = bf16[8,16,1024]{2,1,0:T(8,128)(2,1)S(1)} async-done(((bf16[8,16,1024]{2,1,0:T(8,128)(2,1)}), bf16[8,16,1024]{2,1,0:T(8,128)(2,1)S(1)}, u32[]{:S(2)}, u32[]{:S(2)}) %all-to-all-start) | async-done | bytes 262176 | tf_op jit(solution)/shard_map/while/body/eval_jaxpr/all_to_all | solution.py:90
  17.7 0.1 conditional.2
  17.7 0.1 broadcast.76
  17.7 5.5 %collective-permute-start = (bf16[256,1024]{1,0:T(8,128)(2,1)S(1)}, bf16[256,1024]{1,0:T(8,128)(2,1)S(1)}, u32[]{:S(2)}, u32[]{:S(2)}) collective-permute-start(bf16[256,1024]{1,0:T(8,128)(2,1)S(1)} %get-tuple-element.407), channel_id=1, source_target_pairs={{0,8},{8,16},{16,24},{1,9},{9,17},{17,25},{2,10},{10,18},{18,26},{... | collective-permute-start | bytes 1572872 | tf_op jit(solution)/shard_map/while/body/eval_jaxpr/ppermute | solution.py:13
  23.2 6.1 %collective-permute-done = bf16[256,1024]{1,0:T(8,128)(2,1)S(1)} collective-permute-done((bf16[256,1024]{1,0:T(8,128)(2,1)S(1)}, bf16[256,1024]{1,0:T(8,128)(2,1)S(1)}, u32[]{:S(2)}, u32[]{:S(2)}) %collective-permute-start) | collective-permute-done | bytes 524320 | tf_op jit(solution)/shard_map/while/body/eval_jaxpr/ppermute | solution.py:13
  29.3 0.7 compare_and_fusion.2
  30.0 0.1 reshape.89
  30.1 1.1 broadcast_select_fusion.4
  31.3 0.9 gather_fusion
  32.1 0.8 broadcast_select_fusion.5
  32.9 3.4 %all-to-all-start = ((bf16[8,16,1024]{2,1,0:T(8,128)(2,1)}), bf16[8,16,1024]{2,1,0:T(8,128)(2,1)S(1)}, u32[]{:S(2)}, u32[]{:S(2)}) async-start(bf16[8,16,1024]{2,1,0:T(8,128)(2,1)} %broadcast_select_fusion.5), calls=%async_computation | async-start | bytes 524288 | tf_op jit(solution)/shard_map/while/body/eval_jaxpr/all_to_all | solution.py:90
  36.4 7.0 %all-to-all-done = bf16[8,16,1024]{2,1,0:T(8,128)(2,1)S(1)} async-done(((bf16[8,16,1024]{2,1,0:T(8,128)(2,1)}), bf16[8,16,1024]{2,1,0:T(8,128)(2,1)S(1)}, u32[]{:S(2)}, u32[]{:S(2)}) %all-to-all-start) | async-done | bytes 262176 | tf_op jit(solution)/shard_map/while/body/eval_jaxpr/all_to_all | solution.py:90
  43.4 2.4 %conditional.2 = (bf16[256,1024]{1,0:T(8,128)(2,1)S(1)}, bf16[2,256,1024]{2,1,0:T(8,128)(2,1)S(1)}) conditional(s32[]{:T(128)} %convert_element_type.37, bf16[2,256,1024]{2,1,0:T(8,128)(2,1)S(1)} %get-tuple-element.429, (f32[]{:T(128)}, bf16[2,2,4,128,128]{4,3,2,1,0:T(8,128)(2,1)S(1)}, s32[]{:T(128)}, s32[2,2,4]{2,1,0:T(2,128)S(1)}, ...), branch_computations={%region_1.1_spmd, %region_2.2_spmd} | conditional | flops 809238528 | bytes 16777878 | solution.py:83
  43.4 0.5 fusion.8
  43.9 0.2 fusion.12
  44.1 0.9 copy-done.2
  45.0 0.7 bitcast_dynamic-update-slice_fusion
  45.7 3.5 %collective-permute-start = (bf16[256,1024]{1,0:T(8,128)(2,1)S(1)}, bf16[256,1024]{1,0:T(8,128)(2,1)S(1)}, u32[]{:S(2)}, u32[]{:S(2)}) collective-permute-start(bf16[256,1024]{1,0:T(8,128)(2,1)S(1)} %get-tuple-element.407), channel_id=1, source_target_pairs={{0,8},{8,16},{16,24},{1,9},{9,17},{17,25},{2,10},{10,18},{18,26},{... | collective-permute-start | bytes 1572872 | tf_op jit(solution)/shard_map/while/body/eval_jaxpr/ppermute | solution.py:13
  49.2 6.1 %collective-permute-done = bf16[256,1024]{1,0:T(8,128)(2,1)S(1)} collective-permute-done((bf16[256,1024]{1,0:T(8,128)(2,1)S(1)}, bf16[256,1024]{1,0:T(8,128)(2,1)S(1)}, u32[]{:S(2)}, u32[]{:S(2)}) %collective-permute-start) | collective-permute-done | bytes 524320 | tf_op jit(solution)/shard_map/while/body/eval_jaxpr/ppermute | solution.py:13
  55.3 0.7 compare_and_fusion.2
  56.0 0.1 reshape.89
  56.1 1.1 broadcast_select_fusion.4
  57.3 0.9 gather_fusion
  58.1 0.8 broadcast_select_fusion.5
  58.9 3.4 %all-to-all-start = ((bf16[8,16,1024]{2,1,0:T(8,128)(2,1)}), bf16[8,16,1024]{2,1,0:T(8,128)(2,1)S(1)}, u32[]{:S(2)}, u32[]{:S(2)}) async-start(bf16[8,16,1024]{2,1,0:T(8,128)(2,1)} %broadcast_select_fusion.5), calls=%async_computation | async-start | bytes 524288 | tf_op jit(solution)/shard_map/while/body/eval_jaxpr/all_to_all | solution.py:90
  62.3 7.0 %all-to-all-done = bf16[8,16,1024]{2,1,0:T(8,128)(2,1)S(1)} async-done(((bf16[8,16,1024]{2,1,0:T(8,128)(2,1)}), bf16[8,16,1024]{2,1,0:T(8,128)(2,1)S(1)}, u32[]{:S(2)}, u32[]{:S(2)}) %all-to-all-start) | async-done | bytes 262176 | tf_op jit(solution)/shard_map/while/body/eval_jaxpr/all_to_all | solution.py:90
  69.3 2.4 %conditional.2 = (bf16[256,1024]{1,0:T(8,128)(2,1)S(1)}, bf16[2,256,1024]{2,1,0:T(8,128)(2,1)S(1)}) conditional(s32[]{:T(128)} %convert_element_type.37, bf16[2,256,1024]{2,1,0:T(8,128)(2,1)S(1)} %get-tuple-element.429, (f32[]{:T(128)}, bf16[2,2,4,128,128]{4,3,2,1,0:T(8,128)(2,1)S(1)}, s32[]{:T(128)}, s32[2,2,4]{2,1,0:T(2,128)S(1)}, ...), branch_computations={%region_1.1_spmd, %region_2.2_spmd} | conditional | flops 809238528 | bytes 16777878 | solution.py:83
  69.4 0.5 fusion.8
  69.9 0.2 fusion.12
  70.1 0.9 copy-done.2
  71.0 0.7 bitcast_dynamic-update-slice_fusion
  71.7 5.5 %collective-permute-start = (bf16[256,1024]{1,0:T(8,128)(2,1)S(1)}, bf16[256,1024]{1,0:T(8,128)(2,1)S(1)}, u32[]{:S(2)}, u32[]{:S(2)}) collective-permute-start(bf16[256,1024]{1,0:T(8,128)(2,1)S(1)} %get-tuple-element.407), channel_id=1, source_target_pairs={{0,8},{8,16},{16,24},{1,9},{9,17},{17,25},{2,10},{10,18},{18,26},{... | collective-permute-start | bytes 1572872 | tf_op jit(solution)/shard_map/while/body/eval_jaxpr/ppermute | solution.py:13
  77.3 6.1 %collective-permute-done = bf16[256,1024]{1,0:T(8,128)(2,1)S(1)} collective-permute-done((bf16[256,1024]{1,0:T(8,128)(2,1)S(1)}, bf16[256,1024]{1,0:T(8,128)(2,1)S(1)}, u32[]{:S(2)}, u32[]{:S(2)}) %collective-permute-start) | collective-permute-done | bytes 524320 | tf_op jit(solution)/shard_map/while/body/eval_jaxpr/ppermute | solution.py:13
  83.4 0.7 compare_and_fusion.2
  84.1 0.1 reshape.89
  84.1 1.1 broadcast_select_fusion.4
  85.3 0.9 gather_fusion
  86.2 0.8 broadcast_select_fusion.5
  86.9 3.4 %all-to-all-start = ((bf16[8,16,1024]{2,1,0:T(8,128)(2,1)}), bf16[8,16,1024]{2,1,0:T(8,128)(2,1)S(1)}, u32[]{:S(2)}, u32[]{:S(2)}) async-start(bf16[8,16,1024]{2,1,0:T(8,128)(2,1)} %broadcast_select_fusion.5), calls=%async_computation | async-start | bytes 524288 | tf_op jit(solution)/shard_map/while/body/eval_jaxpr/all_to_all | solution.py:90
  90.4 7.0 %all-to-all-done = bf16[8,16,1024]{2,1,0:T(8,128)(2,1)S(1)} async-done(((bf16[8,16,1024]{2,1,0:T(8,128)(2,1)}), bf16[8,16,1024]{2,1,0:T(8,128)(2,1)S(1)}, u32[]{:S(2)}, u32[]{:S(2)}) %all-to-all-start) | async-done | bytes 262176 | tf_op jit(solution)/shard_map/while/body/eval_jaxpr/all_to_all | solution.py:90
  97.4 0.1 conditional.2
  97.4 0.1 broadcast.76
  97.5 7.8 %collective-permute-start = (bf16[256,1024]{1,0:T(8,128)(2,1)S(1)}, bf16[256,1024]{1,0:T(8,128)(2,1)S(1)}, u32[]{:S(2)}, u32[]{:S(2)}) collective-permute-start(bf16[256,1024]{1,0:T(8,128)(2,1)S(1)} %get-tuple-element.407), channel_id=1, source_target_pairs={{0,8},{8,16},{16,24},{1,9},{9,17},{17,25},{2,10},{10,18},{18,26},{... | collective-permute-start | bytes 1572872 | tf_op jit(solution)/shard_map/while/body/eval_jaxpr/ppermute | solution.py:13
  105.3 6.1 %collective-permute-done = bf16[256,1024]{1,0:T(8,128)(2,1)S(1)} collective-permute-done((bf16[256,1024]{1,0:T(8,128)(2,1)S(1)}, bf16[256,1024]{1,0:T(8,128)(2,1)S(1)}, u32[]{:S(2)}, u32[]{:S(2)}) %collective-permute-start) | collective-permute-done | bytes 524320 | tf_op jit(solution)/shard_map/while/body/eval_jaxpr/ppermute | solution.py:13
  111.4 0.7 compare_and_fusion.2
  112.1 0.1 reshape.89
  112.2 1.1 broadcast_select_fusion.4
  113.3 0.9 gather_fusion
  114.2 0.8 broadcast_select_fusion.5
  115.0 3.4 %all-to-all-start = ((bf16[8,16,1024]{2,1,0:T(8,128)(2,1)}), bf16[8,16,1024]{2,1,0:T(8,128)(2,1)S(1)}, u32[]{:S(2)}, u32[]{:S(2)}) async-start(bf16[8,16,1024]{2,1,0:T(8,128)(2,1)} %broadcast_select_fusion.5), calls=%async_computation | async-start | bytes 524288 | tf_op jit(solution)/shard_map/while/body/eval_jaxpr/all_to_all | solution.py:90
  118.4 7.0 %all-to-all-done = bf16[8,16,1024]{2,1,0:T(8,128)(2,1)S(1)} async-done(((bf16[8,16,1024]{2,1,0:T(8,128)(2,1)}), bf16[8,16,1024]{2,1,0:T(8,128)(2,1)S(1)}, u32[]{:S(2)}, u32[]{:S(2)}) %all-to-all-start) | async-done | bytes 262176 | tf_op jit(solution)/shard_map/while/body/eval_jaxpr/all_to_all | solution.py:90
  125.4 0.1 conditional.2
  125.5 5.5 %collective-permute-start = (bf16[256,1024]{1,0:T(8,128)(2,1)S(1)}, bf16[256,1024]{1,0:T(8,128)(2,1)S(1)}, u32[]{:S(2)}, u32[]{:S(2)}) collective-permute-start(bf16[256,1024]{1,0:T(8,128)(2,1)S(1)} %get-tuple-element.407), channel_id=1, source_target_pairs={{0,8},{8,16},{16,24},{1,9},{9,17},{17,25},{2,10},{10,18},{18,26},{... | collective-permute-start | bytes 1572872 | tf_op jit(solution)/shard_map/while/body/eval_jaxpr/ppermute | solution.py:13
  131.0 6.1 %collective-permute-done = bf16[256,1024]{1,0:T(8,128)(2,1)S(1)} collective-permute-done((bf16[256,1024]{1,0:T(8,128)(2,1)S(1)}, bf16[256,1024]{1,0:T(8,128)(2,1)S(1)}, u32[]{:S(2)}, u32[]{:S(2)}) %collective-permute-start) | collective-permute-done | bytes 524320 | tf_op jit(solution)/shard_map/while/body/eval_jaxpr/ppermute | solution.py:13
  137.1 1.0 copy-done
  (36 shorter events, 0.2 us)
Async XLA Ops:
  2.2 15.4 %copy-start.1 = (s32[2,2,4]{2,1,0:T(2,128)S(1)}, s32[2,2,4]{2,1,0:T(2,128)}, u32[]{:S(2)}) copy-start(s32[2,2,4]{2,1,0:T(2,128)} %get-tuple-element.450) | copy-start | bytes 196 | tf_op jit(solution)/shard_map/while
  2.2 15.4 %copy-start.3 = (bf16[2,2,4,128,128]{4,3,2,1,0:T(8,128)(2,1)S(1)}, bf16[2,2,4,128,128]{4,3,2,1,0:T(8,128)(2,1)}, u32[]{:S(2)}) copy-start(bf16[2,2,4,128,128]{4,3,2,1,0:T(8,128)(2,1)} %get-tuple-element.449) | copy-start | bytes 1572868 | tf_op jit(solution)/shard_map/while
  3.9 13.8 %all-to-all-start = ((bf16[8,16,1024]{2,1,0:T(8,128)(2,1)}), bf16[8,16,1024]{2,1,0:T(8,128)(2,1)S(1)}, u32[]{:S(2)}, u32[]{:S(2)}) async-start(bf16[8,16,1024]{2,1,0:T(8,128)(2,1)} %broadcast_select_fusion.5), calls=%async_computation | async-start | bytes 524288 | tf_op jit(solution)/shard_map/while/body/eval_jaxpr/all_to_all | solution.py:90
  17.7 11.6 %collective-permute-start = (bf16[256,1024]{1,0:T(8,128)(2,1)S(1)}, bf16[256,1024]{1,0:T(8,128)(2,1)S(1)}, u32[]{:S(2)}, u32[]{:S(2)}) collective-permute-start(bf16[256,1024]{1,0:T(8,128)(2,1)S(1)} %get-tuple-element.407), channel_id=1, source_target_pairs={{0,8},{8,16},{16,24},{1,9},{9,17},{17,25},{2,10},{10,18},{18,26},{... | collective-permute-start | bytes 1572872 | tf_op jit(solution)/shard_map/while/body/eval_jaxpr/ppermute | solution.py:13
  31.2 12.1 %copy-start.1 = (s32[2,2,4]{2,1,0:T(2,128)S(1)}, s32[2,2,4]{2,1,0:T(2,128)}, u32[]{:S(2)}) copy-start(s32[2,2,4]{2,1,0:T(2,128)} %get-tuple-element.450) | copy-start | bytes 196 | tf_op jit(solution)/shard_map/while
  31.3 12.1 %copy-start.3 = (bf16[2,2,4,128,128]{4,3,2,1,0:T(8,128)(2,1)S(1)}, bf16[2,2,4,128,128]{4,3,2,1,0:T(8,128)(2,1)}, u32[]{:S(2)}) copy-start(bf16[2,2,4,128,128]{4,3,2,1,0:T(8,128)(2,1)} %get-tuple-element.449) | copy-start | bytes 1572868 | tf_op jit(solution)/shard_map/while
  32.9 10.4 %all-to-all-start = ((bf16[8,16,1024]{2,1,0:T(8,128)(2,1)}), bf16[8,16,1024]{2,1,0:T(8,128)(2,1)S(1)}, u32[]{:S(2)}, u32[]{:S(2)}) async-start(bf16[8,16,1024]{2,1,0:T(8,128)(2,1)} %broadcast_select_fusion.5), calls=%async_computation | async-start | bytes 524288 | tf_op jit(solution)/shard_map/while/body/eval_jaxpr/all_to_all | solution.py:90
  43.4 1.6 %copy-start.2 = (bf16[1024,1024]{1,0:T(8,128)(2,1)S(1)}, bf16[1024,1024]{1,0:T(8,128)(2,1)}, u32[]{:S(2)}) copy-start(bf16[1024,1024]{1,0:T(8,128)(2,1)} %get-tuple-element.284) | copy-start | bytes 6291460 | tf_op jit(solution)/shard_map/while/body/eval_jaxpr/cond
  45.7 9.6 %collective-permute-start = (bf16[256,1024]{1,0:T(8,128)(2,1)S(1)}, bf16[256,1024]{1,0:T(8,128)(2,1)S(1)}, u32[]{:S(2)}, u32[]{:S(2)}) collective-permute-start(bf16[256,1024]{1,0:T(8,128)(2,1)S(1)} %get-tuple-element.407), channel_id=1, source_target_pairs={{0,8},{8,16},{16,24},{1,9},{9,17},{17,25},{2,10},{10,18},{18,26},{... | collective-permute-start | bytes 1572872 | tf_op jit(solution)/shard_map/while/body/eval_jaxpr/ppermute | solution.py:13
  57.2 12.1 %copy-start.1 = (s32[2,2,4]{2,1,0:T(2,128)S(1)}, s32[2,2,4]{2,1,0:T(2,128)}, u32[]{:S(2)}) copy-start(s32[2,2,4]{2,1,0:T(2,128)} %get-tuple-element.450) | copy-start | bytes 196 | tf_op jit(solution)/shard_map/while
  57.2 12.1 %copy-start.3 = (bf16[2,2,4,128,128]{4,3,2,1,0:T(8,128)(2,1)S(1)}, bf16[2,2,4,128,128]{4,3,2,1,0:T(8,128)(2,1)}, u32[]{:S(2)}) copy-start(bf16[2,2,4,128,128]{4,3,2,1,0:T(8,128)(2,1)} %get-tuple-element.449) | copy-start | bytes 1572868 | tf_op jit(solution)/shard_map/while
  58.9 10.4 %all-to-all-start = ((bf16[8,16,1024]{2,1,0:T(8,128)(2,1)}), bf16[8,16,1024]{2,1,0:T(8,128)(2,1)S(1)}, u32[]{:S(2)}, u32[]{:S(2)}) async-start(bf16[8,16,1024]{2,1,0:T(8,128)(2,1)} %broadcast_select_fusion.5), calls=%async_computation | async-start | bytes 524288 | tf_op jit(solution)/shard_map/while/body/eval_jaxpr/all_to_all | solution.py:90
  69.4 1.6 %copy-start.2 = (bf16[1024,1024]{1,0:T(8,128)(2,1)S(1)}, bf16[1024,1024]{1,0:T(8,128)(2,1)}, u32[]{:S(2)}) copy-start(bf16[1024,1024]{1,0:T(8,128)(2,1)} %get-tuple-element.284) | copy-start | bytes 6291460 | tf_op jit(solution)/shard_map/while/body/eval_jaxpr/cond
  71.7 11.6 %collective-permute-start = (bf16[256,1024]{1,0:T(8,128)(2,1)S(1)}, bf16[256,1024]{1,0:T(8,128)(2,1)S(1)}, u32[]{:S(2)}, u32[]{:S(2)}) collective-permute-start(bf16[256,1024]{1,0:T(8,128)(2,1)S(1)} %get-tuple-element.407), channel_id=1, source_target_pairs={{0,8},{8,16},{16,24},{1,9},{9,17},{17,25},{2,10},{10,18},{18,26},{... | collective-permute-start | bytes 1572872 | tf_op jit(solution)/shard_map/while/body/eval_jaxpr/ppermute | solution.py:13
  85.3 12.1 %copy-start.1 = (s32[2,2,4]{2,1,0:T(2,128)S(1)}, s32[2,2,4]{2,1,0:T(2,128)}, u32[]{:S(2)}) copy-start(s32[2,2,4]{2,1,0:T(2,128)} %get-tuple-element.450) | copy-start | bytes 196 | tf_op jit(solution)/shard_map/while
  85.3 12.1 %copy-start.3 = (bf16[2,2,4,128,128]{4,3,2,1,0:T(8,128)(2,1)S(1)}, bf16[2,2,4,128,128]{4,3,2,1,0:T(8,128)(2,1)}, u32[]{:S(2)}) copy-start(bf16[2,2,4,128,128]{4,3,2,1,0:T(8,128)(2,1)} %get-tuple-element.449) | copy-start | bytes 1572868 | tf_op jit(solution)/shard_map/while
  86.9 10.4 %all-to-all-start = ((bf16[8,16,1024]{2,1,0:T(8,128)(2,1)}), bf16[8,16,1024]{2,1,0:T(8,128)(2,1)S(1)}, u32[]{:S(2)}, u32[]{:S(2)}) async-start(bf16[8,16,1024]{2,1,0:T(8,128)(2,1)} %broadcast_select_fusion.5), calls=%async_computation | async-start | bytes 524288 | tf_op jit(solution)/shard_map/while/body/eval_jaxpr/all_to_all | solution.py:90
  97.5 13.9 %collective-permute-start = (bf16[256,1024]{1,0:T(8,128)(2,1)S(1)}, bf16[256,1024]{1,0:T(8,128)(2,1)S(1)}, u32[]{:S(2)}, u32[]{:S(2)}) collective-permute-start(bf16[256,1024]{1,0:T(8,128)(2,1)S(1)} %get-tuple-element.407), channel_id=1, source_target_pairs={{0,8},{8,16},{16,24},{1,9},{9,17},{17,25},{2,10},{10,18},{18,26},{... | collective-permute-start | bytes 1572872 | tf_op jit(solution)/shard_map/while/body/eval_jaxpr/ppermute | solution.py:13
  113.3 12.1 %copy-start.1 = (s32[2,2,4]{2,1,0:T(2,128)S(1)}, s32[2,2,4]{2,1,0:T(2,128)}, u32[]{:S(2)}) copy-start(s32[2,2,4]{2,1,0:T(2,128)} %get-tuple-element.450) | copy-start | bytes 196 | tf_op jit(solution)/shard_map/while
  113.3 12.1 %copy-start.3 = (bf16[2,2,4,128,128]{4,3,2,1,0:T(8,128)(2,1)S(1)}, bf16[2,2,4,128,128]{4,3,2,1,0:T(8,128)(2,1)}, u32[]{:S(2)}) copy-start(bf16[2,2,4,128,128]{4,3,2,1,0:T(8,128)(2,1)} %get-tuple-element.449) | copy-start | bytes 1572868 | tf_op jit(solution)/shard_map/while
  115.0 10.4 %all-to-all-start = ((bf16[8,16,1024]{2,1,0:T(8,128)(2,1)}), bf16[8,16,1024]{2,1,0:T(8,128)(2,1)S(1)}, u32[]{:S(2)}, u32[]{:S(2)}) async-start(bf16[8,16,1024]{2,1,0:T(8,128)(2,1)} %broadcast_select_fusion.5), calls=%async_computation | async-start | bytes 524288 | tf_op jit(solution)/shard_map/while/body/eval_jaxpr/all_to_all | solution.py:90
  125.5 11.7 %collective-permute-start = (bf16[256,1024]{1,0:T(8,128)(2,1)S(1)}, bf16[256,1024]{1,0:T(8,128)(2,1)S(1)}, u32[]{:S(2)}, u32[]{:S(2)}) collective-permute-start(bf16[256,1024]{1,0:T(8,128)(2,1)S(1)} %get-tuple-element.407), channel_id=1, source_target_pairs={{0,8},{8,16},{16,24},{1,9},{9,17},{17,25},{2,10},{10,18},{18,26},{... | collective-permute-start | bytes 1572872 | tf_op jit(solution)/shard_map/while/body/eval_jaxpr/ppermute | solution.py:13
  137.1 1.0 copy-start
where the time goes:
time: 139 us; the launch traced here: 138 us
  waiting for transfers between devices  65.9 us (47%)
  starting transfers between devices  47.9 us (34%)
  other arithmetic  13.4 us (10%)
  local copies, waits for them, and re-layouts  7.81 us (6%)
  matrix products  2.58 us (2%)
    all_to_all x5, waiting for transfers between devices, tick_step(): lax.all_to_all(outgoing, 'dom', split_axis=0, concat_axis=0, tiled=True)  35.4 us
    ppermute x5, waiting for transfers between devices, passed_along(): return lax.ppermute(x, axis, pairs)  30.5 us
    ppermute x5, starting transfers between devices, passed_along(): return lax.ppermute(x, axis, pairs)  27.9 us
    all_to_all x5, starting transfers between devices, tick_step(): lax.all_to_all(outgoing, 'dom', split_axis=0, concat_axis=0, tiled=True)  20 us
    select_n x5, other arithmetic, tick_step(): current = jnp.where(section_pos == 0, initial, received)  5.59 us
    gather x5, local copies, waits for them, and re-layouts, take_rows(): picked = jnp.take(matrix, indices.reshape(-1), axis=0)  4.31 us
    select_n x10, other arithmetic, take_rows(): picked = jnp.take(matrix, indices.reshape(-1), axis=0)  4.02 us
    and x5, other arithmetic, take_rows(): picked = jnp.take(matrix, indices.reshape(-1), axis=0)  3.47 us
  transfers between devices with their start and end apart: 10, of which 10 were waited for; matrix products, arithmetic and copies ran while one was open for 0% of the time, Pallas kernels for 0%

commit v1 on v0

v1 whole, which is shorter than its diff:
```python
import functools
import math

import jax
import jax.numpy as jnp
from jax import lax
from jax.experimental import pallas as pl
from jax.experimental.pallas import tpu as pltpu
from jax.sharding import PartitionSpec as P

restart = 0.1
strength = 0.5
VMEM = pl.BlockSpec(memory_space=pltpu.VMEM)
SMEM = pl.BlockSpec(memory_space=pltpu.SMEM)


def params():
    return pltpu.CompilerParams(vmem_limit_bytes=24 * 1024 * 1024)


def pick_matrix(send, rows):
    parts, each = send.shape
    total = parts * each
    line = lax.broadcasted_iota(jnp.int32, (total, parts), 0) // each
    part = lax.broadcasted_iota(jnp.int32, (total, parts), 1)
    spread = jnp.dot(
        (line == part).astype(jnp.float32),
        send.astype(jnp.float32),
        precision=lax.Precision.HIGHEST,
        preferred_element_type=jnp.float32,
    )
    slot = lax.broadcasted_iota(jnp.int32, (total, each), 0) % each
    lane = lax.broadcasted_iota(jnp.int32, (total, each), 1)
    row = jnp.sum(jnp.where(slot == lane, spread, 0.0), axis=1, keepdims=True)
    local = lax.broadcasted_iota(jnp.int32, (total, rows), 1).astype(jnp.float32)
    return (local == row).astype(jnp.bfloat16)


def tile_sums(block_ref, tiles_ref, batch, r):
    own = far = None
    for t in range(tiles_ref.shape[3]):
        tile = tiles_ref[0, batch, r, t].astype(jnp.float32)
        is_own = block_ref[0, batch, r, t] == 0
        own_t = tile * jnp.where(is_own, 1.0, 0.0)
        far_t = tile * jnp.where(is_own, 0.0, 1.0)
        own = own_t if own is None else own + own_t
        far = far_t if far is None else far + far_t
    return jnp.concatenate([own, far], axis=1).astype(jnp.bfloat16)


def first_kernel(group, send_ref, init_ref, pick_ref, out_ref):
    batch = lax.axis_index("section") % group
    pick = pick_matrix(send_ref[0, batch], init_ref.shape[1])
    pick_ref[...] = pick
    out_ref[...] = jnp.dot(
        pick, init_ref[batch], preferred_element_type=jnp.float32
    ).astype(jnp.bfloat16)


def layer_kernel(group, step, from_init, last, *refs):
    block_ref, tiles_ref, init_ref, pick_ref, bound_ref = refs[:5]
    weights = refs[5 : 5 + group]
    rest = refs[5 + group :]
    if from_init:
        current_ref = None
    else:
        current_ref, rest = rest[0], rest[1:]
    if last:
        x_ref, mixed_ref = rest
        out_ref = None
    else:
        x_ref, out_ref, mixed_ref = rest
    section = lax.axis_index("section")
    batch = section % group
    row_blocks, side = tiles_ref.shape[2], tiles_ref.shape[4]
    boundary = bound_ref[...]
    for r in range(row_blocks):
        rows = pl.ds(r * side, side)
        own = init_ref[batch, rows, :] if from_init else current_ref[rows, :]
        both = jnp.concatenate([own, boundary], axis=0)
        aggregate = jnp.dot(
            tile_sums(block_ref, tiles_ref, batch, r), both, preferred_element_type=jnp.float32
        )
        initial = init_ref[batch, rows, :].astype(jnp.float32)
        mixed_ref[rows, :] = ((1.0 - restart) * aggregate + restart * initial).astype(jnp.bfloat16)

    layer = (section // group) * group + step + 1
    beta = jnp.float32(0.0)
    for number in range(step + 1, lax.axis_size("section") + 1, group):
        beta = jnp.where(layer == number, jnp.float32(math.log(strength / number + 1.0)), beta)

    for shift in range(group):

        @pl.when((batch + shift) % group == step)
        def _(weight_ref=weights[shift]):
            mixed = mixed_ref[...]
            product = jnp.dot(mixed, weight_ref[...], preferred_element_type=jnp.float32)
            x = (1.0 - beta) * mixed.astype(jnp.float32) + beta * product
            x_ref[...] = jnp.maximum(x, 0.0).astype(jnp.bfloat16)

    if not last:
        out_ref[...] = jnp.dot(
            pick_ref[...], x_ref[...], preferred_element_type=jnp.float32
        ).astype(jnp.bfloat16)


def on_device(initial_feat, layer_weight, tile_column, tile_values, send_rows):
    section_count = lax.axis_size("section")
    batches, rows, width = initial_feat.shape
    group = batches
    stages = section_count // group
    section = lax.axis_index("section")
    member = section % group
    mine = section // group
    sent = send_rows.shape[2] * send_rows.shape[3]
    bf16 = jnp.bfloat16

    def shifted(x, by):
        pairs = [
            (s, (s // group) * group + (s - by) % group) for s in range(section_count)
        ]
        return lax.ppermute(x, "section", pairs)

    def crossed(x):
        pairs = [(s, s + group) for s in range(section_count - group)]
        return lax.ppermute(x, "section", pairs)

    def exchanged(x):
        return lax.all_to_all(x, "dom", split_axis=0, concat_axis=0, tiled=True)

    own_weight = layer_weight[0]
    weights = [own_weight] + [shifted(own_weight, by) for by in range(1, group)]

    pick, outgoing = pl.pallas_call(
        functools.partial(first_kernel, group),
        out_shape=[
            jax.ShapeDtypeStruct((sent, rows), bf16),
            jax.ShapeDtypeStruct((sent, width), bf16),
        ],
        in_specs=[VMEM, VMEM],
        out_specs=[VMEM, VMEM],
        compiler_params=params(),
        name="first_rows",
    )(send_rows, initial_feat)

    def layer(step, current, boundary, last):
        from_init = current is None
        outs = [jax.ShapeDtypeStruct((rows, width), bf16)]
        if not last:
            outs.append(jax.ShapeDtypeStruct((sent, width), bf16))
        operands = [tile_column, tile_values, initial_feat, pick, boundary] + weights
        if not from_init:
            operands.append(current)
        return pl.pallas_call(
            functools.partial(layer_kernel, group, step, from_init, last),
            out_shape=outs,
            in_specs=[SMEM] + [VMEM] * (len(operands) - 1),
            out_specs=[VMEM] * len(outs),
            scratch_shapes=[pltpu.VMEM((rows, width), bf16)],
            compiler_params=params(),
            name="layer",
        )(*operands)

    boundary = exchanged(outgoing)
    current = None
    kept = None
    for stage in range(stages):
        outs = []
        for step in range(group):
            last = stage == stages - 1 and step == group - 1
            result = layer(step, current, boundary, last)
            current = result[0]
            outs.append(current)
            if last:
                break
            boundary = exchanged(result[1])
        kept = outs if kept is None else [
            jnp.where(mine == stage, new, old) for new, old in zip(outs, kept)
        ]
        if stage < stages - 1:
            current = crossed(current)
            boundary = crossed(boundary)

    stack = jnp.stack(kept)
    pieces = []
    for by in range(group):
        wanted = lax.dynamic_index_in_dim(stack, (member - by) % group, 0, keepdims=False)
        pieces.append(wanted if by == 0 else shifted(wanted, by))
    order = [
        lax.select_n((b - member) % group, *pieces) for b in range(group)
    ]
    return jnp.stack(order)[None]


def solution(mesh):
    in_specs = (
        P(None, "dom", None),
        P("section", None, None),
        P("dom", None, None, None),
        P("dom", None, None, None, None, None),
        P("dom", None, None, None),
    )
    out_specs = P("section", None, "dom", None)
    return jax.shard_map(
        on_device, mesh=mesh, in_specs=in_specs, out_specs=out_specs, check_vma=False
    )
```

time: 139 us -> 94.6 us (0.68)
  waiting for transfers between devices: 65.9 us -> 18.7 us
  starting transfers between devices: 47.9 us -> 20.6 us
  blocking collectives: 0 us -> 26.9 us
  other arithmetic: 13.4 us -> 3.46 us
  Pallas kernels: 0 us -> 8.93 us
  local copies, waits for them, and re-layouts: 7.81 us -> 14.6 us
  matrix products: 2.58 us -> 0 us
    all_to_all x0 -> x2, blocking collectives: none -> 26.9 us  [exchanged(): return lax.all_to_all(x, 'dom', split_axis=0, concat_axis=0, tiled=True)]
    all_to_all x5 -> x2, waiting for transfers between devices: 35.4 us -> 8.52 us  [exchanged(): return lax.all_to_all(x, 'dom', split_axis=0, concat_axis=0, tiled=True)]
    ppermute x5 -> x4, waiting for transfers between devices: 30.5 us -> 10.1 us  [the longest x2 8.6 us: crossed(): return lax.ppermute(x, 'section', pairs)]
    ppermute x5 -> x4, starting transfers between devices: 27.9 us -> 10.9 us  [the longest x2 7.08 us: crossed(): return lax.ppermute(x, 'section', pairs)]
    unnamed x2 -> x42, local copies, waits for them, and re-layouts: 0.97 us -> 14.6 us
    all_to_all x5 -> x2, starting transfers between devices: 20 us -> 9.69 us  [exchanged(): return lax.all_to_all(x, 'dom', split_axis=0, concat_axis=0, tiled=True)]
    select_n x15 -> x0, other arithmetic: 9.6 us -> none  [the longest x5 5.59 us: tick_step(): current = jnp.where(section_pos == 0, initial, received)]
    pallas_call x0 -> x5, Pallas kernels: none -> 8.93 us  [the longest x4 8.41 us: layer(): pl.pallas_call(functools.partial(layer_kernel, group, step, from_init, la...]
  transfers between devices with their start and end apart: 10 -> 6, of which waited for: 10 -> 5; matrix products, arithmetic and copies ran while one was open for 0% -> 2% of each run, Pallas kernels for 0% -> 1%
where the time goes in v1:
time: 94.6 us; the launch traced here: 93.3 us
  blocking collectives  26.9 us (28%)
  starting transfers between devices  20.6 us (22%)
  waiting for transfers between devices  18.7 us (20%)
  local copies, waits for them, and re-layouts  14.6 us (15%)
  Pallas kernels  8.93 us (9%)
  other arithmetic  3.46 us (4%)
    all_to_all x2, blocking collectives, exchanged(): return lax.all_to_all(x, 'dom', split_axis=0, concat_axis=0, tiled=True)  26.9 us
    unnamed x42, local copies, waits for them, and re-layouts  14.6 us
    all_to_all x2, starting transfers between devices, exchanged(): return lax.all_to_all(x, 'dom', split_axis=0, concat_axis=0, tiled=True)  9.69 us
    ppermute x2, waiting for transfers between devices, crossed(): return lax.ppermute(x, 'section', pairs)  8.6 us
    all_to_all x2, waiting for transfers between devices, exchanged(): return lax.all_to_all(x, 'dom', split_axis=0, concat_axis=0, tiled=True)  8.52 us
    pallas_call x4, Pallas kernels, layer(): pl.pallas_call(functools.partial(layer_kernel, group, step, from_init, la...  8.41 us
    ppermute x2, starting transfers between devices, crossed(): return lax.ppermute(x, 'section', pairs)  7.08 us
    ppermute x2, starting transfers between devices, shifted(): return lax.ppermute(x, 'section', pairs)  3.84 us
  transfers between devices with their start and end apart: 6, of which 5 were waited for; matrix products, arithmetic and copies ran while one was open for 2% of the time, Pallas kernels for 1%

profile of v1, /device:TPU:1, one launch (start us, length us, event | category | flops | bytes accessed | tf_op | source)
XLA Modules:
  0.0 93.3 jit_solution(2324933225813790074)
XLA Ops:
  0.0 0.0 collective-permute-start
  0.0 0.0 copy-start.5
  0.0 1.2 %copy-done.5 = bf16[2,256,1024]{2,1,0:T(8,128)(2,1)S(1)} copy-done((bf16[2,256,1024]{2,1,0:T(8,128)(2,1)S(1)}, bf16[2,256,1024]{2,1,0:T(8,128)(2,1)}, u32[]{:S(2)}) %copy-start.5) | copy-done | bytes 1048600
  1.2 0.0 copy-start.18
  1.2 0.7 copy-done.18
  1.9 0.0 copy-start.6
  1.9 0.5 first_rows.1
  2.5 15.0 %all_to_all.45 = bf16[8,16,1024]{2,1,0:T(8,128)(2,1)S(1)} all-to-all(bf16[8,16,1024]{2,1,0:T(8,128)(2,1)S(1)} %bitcast.37), channel_id=1, replica_groups=mesh['section'=4,'dom'=8] {'dom'}, dimensions={0} | all-to-all | bytes 524288 | tf_op jit(solution)/shard_map/all_to_all | solution.py:129
  17.5 0.0 collective-permute-done.refs_6_
  17.5 0.0 copy-start.2
  17.5 0.0 copy-done.6
  17.5 0.0 copy-start
  17.5 2.3 %copy-done = bf16[1,1024,1024]{2,1,0:T(8,128)(2,1)S(1)} copy-done((bf16[1,1024,1024]{2,1,0:T(8,128)(2,1)S(1)}, bf16[1,1024,1024]{2,1,0:T(8,128)(2,1)}, u32[]{:S(2)}) %copy-start) | copy-done | bytes 2097176
  19.8 0.0 copy-start.7
  19.8 1.0 %copy-done.7 = bf16[1,2,2,4,128,128]{5,4,3,2,1,0:T(8,128)(2,1)S(1)} copy-done((bf16[1,2,2,4,128,128]{5,4,3,2,1,0:T(8,128)(2,1)S(1)}, bf16[1,2,2,4,128,128]{5,4,3,2,1,0:T(8,128)(2,1)}, u32[]{:S(2)}) %copy-start.7) | copy-done | bytes 524312
  20.9 0.0 copy-start.16
  20.9 0.7 copy-done.16
  21.5 0.0 copy-start.1
  21.5 1.9 %layer.4 = (bf16[256,1024]{1,0:T(8,128)(2,1)S(1)}, bf16[128,1024]{1,0:T(8,128)(2,1)S(1)}) custom-call(s32[1,2,2,4]{3,2,1,0:T(2,128)S(1)} %copy-done.16, bf16[1,2,2,4,128,128]{5,4,3,2,1,0:T(8,128)(2,1)S(1)} %copy-done.7, bf16[2,256,1024]{2,1,0:T(8,128)(2,1)S(1)} %copy-done.6, bf16[128,256]{1,0:T(8,128)(2,1)S(1)} %get-tuple-element.13.refs_3_, ...), custom_call_target="tpu_custom_call" | custom-call | tf_op jit(solution)/shard_map/layer/pallas_call | solution.py:154
  23.4 0.0 copy-start.10
  23.4 11.9 %all_to_all.46 = bf16[8,16,1024]{2,1,0:T(8,128)(2,1)S(1)} all-to-all(bf16[8,16,1024]{2,1,0:T(8,128)(2,1)S(1)} %bitcast.36), channel_id=1, replica_groups=mesh['section'=4,'dom'=8] {'dom'}, dimensions={0} | all-to-all | bytes 524288 | tf_op jit(solution)/shard_map/all_to_all | solution.py:129
  35.4 0.0 copy-done.2
  35.4 0.0 copy-done.1
  35.4 0.0 copy-start.17
  35.4 2.6 %layer.5 = (bf16[256,1024]{1,0:T(8,128)(2,1)S(1)}, bf16[128,1024]{1,0:T(8,128)(2,1)}) custom-call(s32[1,2,2,4]{3,2,1,0:T(2,128)S(1)} %copy-done.16, bf16[1,2,2,4,128,128]{5,4,3,2,1,0:T(8,128)(2,1)S(1)} %copy-done.7, bf16[2,256,1024]{2,1,0:T(8,128)(2,1)S(1)} %copy-done.6, bf16[128,256]{1,0:T(8,128)(2,1)S(1)} %get-tuple-element.13.refs_3_, ...), custom_call_target="tpu_custom_call" | custom-call | tf_op jit(solution)/shard_map/layer/pallas_call | solution.py:154
  37.9 0.0 copy-done.10
  37.9 0.0 copy-start.13
  38.0 0.8 copy-done.13
  38.7 4.5 %all-to-all-start.2 = ((bf16[8,16,1024]{2,1,0:T(8,128)(2,1)}), bf16[8,16,1024]{2,1,0:T(8,128)(2,1)S(1)}, u32[]{:S(2)}, u32[]{:S(2)}) async-start(bf16[8,16,1024]{2,1,0:T(8,128)(2,1)} %bitcast.5), calls=%async_computation.2 | async-start | bytes 524288 | tf_op jit(solution)/shard_map/all_to_all | solution.py:129
  43.3 3.9 %collective-permute-start.2 = (bf16[256,1024]{1,0:T(8,128)(2,1)}, bf16[256,1024]{1,0:T(8,128)(2,1)}, u32[]{:S(2)}, u32[]{:S(2)}) collective-permute-start(bf16[256,1024]{1,0:T(8,128)(2,1)} %copy-done.13), channel_id=1, source_target_pairs={{0,16},{8,24},{1,17},{9,25},{2,18},{10,26},{3,19},{11,27},{4,20},{... | collective-permute-start | bytes 1572872 | tf_op jit(solution)/shard_map/ppermute | solution.py:126
  47.2 3.3 %all-to-all-done.2 = bf16[8,16,1024]{2,1,0:T(8,128)(2,1)S(1)} async-done(((bf16[8,16,1024]{2,1,0:T(8,128)(2,1)}), bf16[8,16,1024]{2,1,0:T(8,128)(2,1)S(1)}, u32[]{:S(2)}, u32[]{:S(2)}) %all-to-all-start.2) | async-done | bytes 262176 | tf_op jit(solution)/shard_map/all_to_all | solution.py:129
  50.5 3.1 %collective-permute-start.1 = (bf16[128,1024]{1,0:T(8,128)(2,1)S(1)}, bf16[128,1024]{1,0:T(8,128)(2,1)S(1)}, u32[]{:S(2)}, u32[]{:S(2)}) collective-permute-start(bf16[128,1024]{1,0:T(8,128)(2,1)S(1)} %bitcast.38), channel_id=1, source_target_pairs={{0,16},{8,24},{1,17},{9,25},{2,18},{10,26},{3,19},{11,27},{4,20},{... | collective-permute-start | bytes 786440 | tf_op jit(solution)/shard_map/ppermute | solution.py:126
  53.6 3.1 %collective-permute-done.2.refs_7_ = bf16[256,1024]{1,0:T(8,128)(2,1)} collective-permute-done((bf16[256,1024]{1,0:T(8,128)(2,1)}, bf16[256,1024]{1,0:T(8,128)(2,1)}, u32[]{:S(2)}, u32[]{:S(2)}) %collective-permute-start.2) | collective-permute-done | bytes 524320 | tf_op jit(solution)/shard_map/ppermute | solution.py:126
  56.7 5.5 %collective-permute-done.1.refs_4_ = bf16[128,1024]{1,0:T(8,128)(2,1)S(1)} collective-permute-done((bf16[128,1024]{1,0:T(8,128)(2,1)S(1)}, bf16[128,1024]{1,0:T(8,128)(2,1)S(1)}, u32[]{:S(2)}, u32[]{:S(2)}) %collective-permute-start.1) | collective-permute-done | bytes 262176 | tf_op jit(solution)/shard_map/ppermute | solution.py:126
  62.2 0.0 copy-done.17
  62.2 0.0 copy-start.3
  62.2 1.6 %copy-done.3 = bf16[1024,1024]{1,0:T(8,128)(2,1)S(1)} copy-done((bf16[1024,1024]{1,0:T(8,128)(2,1)S(1)}, bf16[1024,1024]{1,0:T(8,128)(2,1)}, u32[]{:S(2)}) %copy-start.3) | copy-done | bytes 2097176
  63.8 0.0 copy-start.8
  63.8 1.0 %copy-done.8 = bf16[1,2,2,4,128,128]{5,4,3,2,1,0:T(8,128)(2,1)S(1)} copy-done((bf16[1,2,2,4,128,128]{5,4,3,2,1,0:T(8,128)(2,1)S(1)}, bf16[1,2,2,4,128,128]{5,4,3,2,1,0:T(8,128)(2,1)}, u32[]{:S(2)}) %copy-start.8) | copy-done | bytes 524312
  64.8 2.3 %layer.6 = (bf16[256,1024]{1,0:T(8,128)(2,1)S(1)}, bf16[128,1024]{1,0:T(8,128)(2,1)S(1)}) custom-call(s32[1,2,2,4]{3,2,1,0:T(2,128)S(1)} %copy-done.17, bf16[1,2,2,4,128,128]{5,4,3,2,1,0:T(8,128)(2,1)S(1)} %copy-done.8, bf16[2,256,1024]{2,1,0:T(8,128)(2,1)S(1)} %copy-done.6, bf16[128,256]{1,0:T(8,128)(2,1)S(1)} %get-tuple-element.13.refs_3_, ...), custom_call_target="tpu_custom_call" | custom-call | tf_op jit(solution)/shard_map/layer/pallas_call | solution.py:154
  67.2 0.0 copy-start.11
  67.2 0.8 copy-done.11
  68.0 0.0 copy-start.15
  68.0 0.7 copy-done.15
  68.7 5.2 %all-to-all-start.3 = ((bf16[8,16,1024]{2,1,0:T(8,128)(2,1)}), bf16[8,16,1024]{2,1,0:T(8,128)(2,1)S(1)}, u32[]{:S(2)}, u32[]{:S(2)}) async-start(bf16[8,16,1024]{2,1,0:T(8,128)(2,1)} %bitcast.35), calls=%async_computation.3 | async-start | bytes 524288 | tf_op jit(solution)/shard_map/all_to_all | solution.py:129
  73.8 1.9 %select_bitcast_fusion.3 = bf16[1,256,1024]{2,1,0:T(8,128)(2,1)} fusion(bf16[256,1024]{1,0:T(8,128)(2,1)} %copy-done.11, bf16[256,1024]{1,0:T(8,128)(2,1)} %copy-done.10, pred[]{:T(512)S(6)} %eq.10), kind=kLoop, calls=%fused_computation.12 | loop fusion | flops 262144 | bytes 1572865 | tf_op jit(solution)/shard_map/stack | solution.py:184
  75.7 5.3 %all-to-all-done.3 = bf16[8,16,1024]{2,1,0:T(8,128)(2,1)S(1)} async-done(((bf16[8,16,1024]{2,1,0:T(8,128)(2,1)}), bf16[8,16,1024]{2,1,0:T(8,128)(2,1)S(1)}, u32[]{:S(2)}, u32[]{:S(2)}) %all-to-all-start.3) | async-done | bytes 262176 | tf_op jit(solution)/shard_map/all_to_all | solution.py:129
  81.0 0.0 copy-start.4
  81.0 1.6 %copy-done.4 = bf16[1024,1024]{1,0:T(8,128)(2,1)S(1)} copy-done((bf16[1024,1024]{1,0:T(8,128)(2,1)S(1)}, bf16[1024,1024]{1,0:T(8,128)(2,1)}, u32[]{:S(2)}) %copy-start.4) | copy-done | bytes 2097176
  82.6 0.0 copy-start.9
  82.6 1.0 %copy-done.9 = bf16[1,2,2,4,128,128]{5,4,3,2,1,0:T(8,128)(2,1)S(1)} copy-done((bf16[1,2,2,4,128,128]{5,4,3,2,1,0:T(8,128)(2,1)S(1)}, bf16[1,2,2,4,128,128]{5,4,3,2,1,0:T(8,128)(2,1)}, u32[]{:S(2)}) %copy-start.9) | copy-done | bytes 524312
  83.6 0.0 copy-start.12
  83.7 1.0 %copy-done.12 = bf16[256,1024]{1,0:T(8,128)(2,1)S(1)} copy-done((bf16[256,1024]{1,0:T(8,128)(2,1)S(1)}, bf16[256,1024]{1,0:T(8,128)(2,1)}, u32[]{:S(2)}) %copy-start.12) | copy-done | bytes 524312
  84.7 1.6 %layer.7 = bf16[256,1024]{1,0:T(8,128)(2,1)S(1)} custom-call(s32[1,2,2,4]{3,2,1,0:T(2,128)S(1)} %copy-done.17, bf16[1,2,2,4,128,128]{5,4,3,2,1,0:T(8,128)(2,1)S(1)} %copy-done.9, bf16[2,256,1024]{2,1,0:T(8,128)(2,1)S(1)} %copy-done.6, bf16[128,256]{1,0:T(8,128)(2,1)S(1)} %get-tuple-element.13.refs_3_, bf16[128,1024]{1,0:T(8,128)(2,1)S(1)} %bitcast.34, ...), custom_call_target="tpu_custom_call" | custom-call | tf_op jit(solution)/shard_map/layer/pallas_call | solution.py:154
  86.3 0.0 copy-done.14
  86.3 0.0 copy-start.20
  86.4 0.1 select_bitcast_fusion.2
  86.4 0.0 copy-done.19
  86.4 0.2 fusion.1
  86.6 3.8 %collective-permute-start.3 = (bf16[256,1024]{1,0:T(8,128)(2,1)S(1)}, bf16[256,1024]{1,0:T(8,128)(2,1)S(1)}, u32[]{:S(2)}, u32[]{:S(2)}) collective-permute-start(bf16[256,1024]{1,0:T(8,128)(2,1)S(1)} %fusion.1), channel_id=1, source_target_pairs={{0,8},{8,0},{16,24},{24,16},{1,9},{9,1},{17,25},{25,17},{2,10},{10... | collective-permute-start | bytes 1572872 | tf_op jit(solution)/shard_map/ppermute | solution.py:122
  90.5 1.5 %collective-permute-done.3 = bf16[256,1024]{1,0:T(8,128)(2,1)S(1)} collective-permute-done((bf16[256,1024]{1,0:T(8,128)(2,1)S(1)}, bf16[256,1024]{1,0:T(8,128)(2,1)S(1)}, u32[]{:S(2)}, u32[]{:S(2)}) %collective-permute-start.3) | collective-permute-done | bytes 524320 | tf_op jit(solution)/shard_map/ppermute | solution.py:122
  92.0 0.0 copy-done.20
  92.0 0.2 select_bitcast_fusion.1
  92.2 1.1 %maximum_bitcast_fusion = bf16[1,2,256,1024]{3,2,1,0:T(8,128)(2,1)} fusion(bf16[1,256,1024]{2,1,0:T(8,128)(2,1)S(1)} %get-tuple-element.22, bf16[1,256,1024]{2,1,0:T(8,128)(2,1)S(1)} %get-tuple-element.21), kind=kLoop, calls=%fused_computation.4 | loop fusion | flops 524288 | bytes 2097152 | tf_op jit(solution)/shard_map/broadcast_in_dim | solution.py:192
  (2 shorter events, 0.0 us)
Async XLA Ops:
  0.0 17.5 %collective-permute-start = (bf16[1024,1024]{1,0:T(8,128)(2,1)}, bf16[1024,1024]{1,0:T(8,128)(2,1)S(1)}, u32[]{:S(2)}, u32[]{:S(2)}) collective-permute-start(bf16[1024,1024]{1,0:T(8,128)(2,1)} %bitcast.27), channel_id=1, source_target_pairs={{0,8},{8,0},{16,24},{24,16},{1,9},{9,1},{17,25},{25,17},{2,10},{10... | collective-permute-start | bytes 6291464 | tf_op jit(solution)/shard_map/ppermute | solution.py:122
  0.0 1.2 %copy-start.5 = (bf16[2,256,1024]{2,1,0:T(8,128)(2,1)S(1)}, bf16[2,256,1024]{2,1,0:T(8,128)(2,1)}, u32[]{:S(2)}) copy-start(bf16[2,256,1024]{2,1,0:T(8,128)(2,1)} %refs_2_.7) | copy-start | bytes 3145732
  1.2 0.7 copy-start.18
  1.9 15.5 %copy-start.6 = (bf16[2,256,1024]{2,1,0:T(8,128)(2,1)S(1)}, bf16[2,256,1024]{2,1,0:T(8,128)(2,1)}, u32[]{:S(2)}) copy-start(bf16[2,256,1024]{2,1,0:T(8,128)(2,1)} %refs_2_.7) | copy-start | bytes 3145732
  17.5 17.9 %copy-start.2 = (bf16[1024,1024]{1,0:T(8,128)(2,1)}, bf16[1024,1024]{1,0:T(8,128)(2,1)S(1)}, u32[]{:S(2)}) copy-start(bf16[1024,1024]{1,0:T(8,128)(2,1)S(1)} %collective-permute-done.refs_6_) | copy-start | bytes 6291460
  17.5 2.4 %copy-start = (bf16[1,1024,1024]{2,1,0:T(8,128)(2,1)S(1)}, bf16[1,1024,1024]{2,1,0:T(8,128)(2,1)}, u32[]{:S(2)}) copy-start(bf16[1,1024,1024]{2,1,0:T(8,128)(2,1)} %param.6) | copy-start | bytes 6291460
  19.8 1.0 %copy-start.7 = (bf16[1,2,2,4,128,128]{5,4,3,2,1,0:T(8,128)(2,1)S(1)}, bf16[1,2,2,4,128,128]{5,4,3,2,1,0:T(8,128)(2,1)}, u32[]{:S(2)}) copy-start(bf16[1,2,2,4,128,128]{5,4,3,2,1,0:T(8,128)(2,1)} %refs_1_.7) | copy-start | bytes 1572868
  20.9 0.7 copy-start.16
  21.5 13.8 %copy-start.1 = (bf16[1,1024,1024]{2,1,0:T(8,128)(2,1)S(1)}, bf16[1,1024,1024]{2,1,0:T(8,128)(2,1)}, u32[]{:S(2)}) copy-start(bf16[1,1024,1024]{2,1,0:T(8,128)(2,1)} %param.6) | copy-start | bytes 6291460
  23.4 14.5 %copy-start.10 = (bf16[256,1024]{1,0:T(8,128)(2,1)}, bf16[256,1024]{1,0:T(8,128)(2,1)S(1)}, u32[]{:S(2)}) copy-start(bf16[256,1024]{1,0:T(8,128)(2,1)S(1)} %get-tuple-element.16.refs_7_) | copy-start | bytes 1572868
  35.4 26.8 %copy-start.17 = (s32[1,2,2,4]{3,2,1,0:T(2,128)S(1)}, s32[1,2,2,4]{3,2,1,0:T(2,128)}, u32[]{:S(2)}) copy-start(s32[1,2,2,4]{3,2,1,0:T(2,128)} %refs_0_.7) | copy-start | bytes 196
  37.9 0.8 copy-start.13
  38.7 11.7 %all-to-all-start.2 = ((bf16[8,16,1024]{2,1,0:T(8,128)(2,1)}), bf16[8,16,1024]{2,1,0:T(8,128)(2,1)S(1)}, u32[]{:S(2)}, u32[]{:S(2)}) async-start(bf16[8,16,1024]{2,1,0:T(8,128)(2,1)} %bitcast.5), calls=%async_computation.2 | async-start | bytes 524288 | tf_op jit(solution)/shard_map/all_to_all | solution.py:129
  43.3 13.4 %collective-permute-start.2 = (bf16[256,1024]{1,0:T(8,128)(2,1)}, bf16[256,1024]{1,0:T(8,128)(2,1)}, u32[]{:S(2)}, u32[]{:S(2)}) collective-permute-start(bf16[256,1024]{1,0:T(8,128)(2,1)} %copy-done.13), channel_id=1, source_target_pairs={{0,16},{8,24},{1,17},{9,25},{2,18},{10,26},{3,19},{11,27},{4,20},{... | collective-permute-start | bytes 1572872 | tf_op jit(solution)/shard_map/ppermute | solution.py:126
  50.5 11.8 %collective-permute-start.1 = (bf16[128,1024]{1,0:T(8,128)(2,1)S(1)}, bf16[128,1024]{1,0:T(8,128)(2,1)S(1)}, u32[]{:S(2)}, u32[]{:S(2)}) collective-permute-start(bf16[128,1024]{1,0:T(8,128)(2,1)S(1)} %bitcast.38), channel_id=1, source_target_pairs={{0,16},{8,24},{1,17},{9,25},{2,18},{10,26},{3,19},{11,27},{4,20},{... | collective-permute-start | bytes 786440 | tf_op jit(solution)/shard_map/ppermute | solution.py:126
  62.2 1.6 %copy-start.3 = (bf16[1024,1024]{1,0:T(8,128)(2,1)S(1)}, bf16[1024,1024]{1,0:T(8,128)(2,1)}, u32[]{:S(2)}) copy-start(bf16[1024,1024]{1,0:T(8,128)(2,1)} %copy-done.2) | copy-start | bytes 6291460
  63.8 1.0 %copy-start.8 = (bf16[1,2,2,4,128,128]{5,4,3,2,1,0:T(8,128)(2,1)S(1)}, bf16[1,2,2,4,128,128]{5,4,3,2,1,0:T(8,128)(2,1)}, u32[]{:S(2)}) copy-start(bf16[1,2,2,4,128,128]{5,4,3,2,1,0:T(8,128)(2,1)} %refs_1_.7) | copy-start | bytes 1572868
  67.2 0.8 copy-start.11
  68.0 0.7 copy-start.15
  68.7 12.3 %all-to-all-start.3 = ((bf16[8,16,1024]{2,1,0:T(8,128)(2,1)}), bf16[8,16,1024]{2,1,0:T(8,128)(2,1)S(1)}, u32[]{:S(2)}, u32[]{:S(2)}) async-start(bf16[8,16,1024]{2,1,0:T(8,128)(2,1)} %bitcast.35), calls=%async_computation.3 | async-start | bytes 524288 | tf_op jit(solution)/shard_map/all_to_all | solution.py:129
  81.0 1.6 %copy-start.4 = (bf16[1024,1024]{1,0:T(8,128)(2,1)S(1)}, bf16[1024,1024]{1,0:T(8,128)(2,1)}, u32[]{:S(2)}) copy-start(bf16[1024,1024]{1,0:T(8,128)(2,1)} %copy-done.2) | copy-start | bytes 6291460
  82.6 1.0 %copy-start.9 = (bf16[1,2,2,4,128,128]{5,4,3,2,1,0:T(8,128)(2,1)S(1)}, bf16[1,2,2,4,128,128]{5,4,3,2,1,0:T(8,128)(2,1)}, u32[]{:S(2)}) copy-start(bf16[1,2,2,4,128,128]{5,4,3,2,1,0:T(8,128)(2,1)} %refs_1_.7) | copy-start | bytes 1572868
  83.6 1.0 %copy-start.12 = (bf16[256,1024]{1,0:T(8,128)(2,1)S(1)}, bf16[256,1024]{1,0:T(8,128)(2,1)}, u32[]{:S(2)}) copy-start(bf16[256,1024]{1,0:T(8,128)(2,1)} %copy-done.11) | copy-start | bytes 1572868
  84.7 1.6 %copy-start.14 = (bf16[256,1024]{1,0:T(8,128)(2,1)S(1)}, bf16[256,1024]{1,0:T(8,128)(2,1)}, u32[]{:S(2)}) copy-start(bf16[256,1024]{1,0:T(8,128)(2,1)} %copy-done.13) | copy-start | bytes 1572868
  84.7 1.7 %copy-start.19 = (bf16[1,256,1024]{2,1,0:T(8,128)(2,1)S(1)}, bf16[1,256,1024]{2,1,0:T(8,128)(2,1)}, u32[]{:S(2)}) copy-start(bf16[1,256,1024]{2,1,0:T(8,128)(2,1)} %select_bitcast_fusion.3) | copy-start | bytes 1572868
  86.3 5.7 %copy-start.20 = (bf16[1,256,1024]{2,1,0:T(8,128)(2,1)S(1)}, bf16[1,256,1024]{2,1,0:T(8,128)(2,1)}, u32[]{:S(2)}) copy-start(bf16[1,256,1024]{2,1,0:T(8,128)(2,1)} %select_bitcast_fusion.3) | copy-start | bytes 1572868
  86.6 5.4 %collective-permute-start.3 = (bf16[256,1024]{1,0:T(8,128)(2,1)S(1)}, bf16[256,1024]{1,0:T(8,128)(2,1)S(1)}, u32[]{:S(2)}, u32[]{:S(2)}) collective-permute-start(bf16[256,1024]{1,0:T(8,128)(2,1)S(1)} %fusion.1), channel_id=1, source_target_pairs={{0,8},{8,0},{16,24},{24,16},{1,9},{9,1},{17,25},{25,17},{2,10},{10... | collective-permute-start | bytes 1572872 | tf_op jit(solution)/shard_map/ppermute | solution.py:122

commit v2 on v1

v2 whole, which is shorter than its diff:
```python
import functools
import math

import jax
import jax.numpy as jnp
from jax import lax
from jax.experimental import pallas as pl
from jax.experimental.pallas import tpu as pltpu
from jax.sharding import PartitionSpec as P

restart = 0.1
strength = 0.5
VMEM = pl.BlockSpec(memory_space=pltpu.VMEM)
HBM = pl.BlockSpec(memory_space=pltpu.HBM)
bf16 = jnp.bfloat16
f32 = jnp.float32
MIB = 1024 * 1024


def call(kernel, outs, in_specs, out_specs, scratch=(), aliases=None, cost=None):
    return pl.pallas_call(
        kernel,
        out_shape=[jax.ShapeDtypeStruct(shape, bf16) for shape in outs],
        in_specs=in_specs,
        out_specs=out_specs,
        scratch_shapes=list(scratch),
        input_output_aliases=aliases or {},
        cost_estimate=cost,
        compiler_params=pltpu.CompilerParams(vmem_limit_bytes=16 * MIB),
    )


def pick_matrix(send, rows):
    parts, each = send.shape
    total = parts * each
    line = lax.broadcasted_iota(jnp.int32, (total, parts), 0) // each
    part = lax.broadcasted_iota(jnp.int32, (total, parts), 1)
    spread = jnp.dot(
        (line == part).astype(f32),
        send.astype(f32),
        precision=lax.Precision.HIGHEST,
        preferred_element_type=f32,
    )
    slot = lax.broadcasted_iota(jnp.int32, (total, each), 0) % each
    lane = lax.broadcasted_iota(jnp.int32, (total, each), 1)
    row = jnp.sum(jnp.where(slot == lane, spread, 0.0), axis=1, keepdims=True)
    local = lax.broadcasted_iota(jnp.int32, (total, rows), 1).astype(f32)
    return (local == row).astype(bf16)


def first_kernel(
    group,
    send_hbm,
    block_hbm,
    init_hbm,
    tiles_hbm,
    weight_hbm,
    out_ref,
    pick_ref,
    mix_ref,
    init_ref,
    weight_ref,
    send_ref,
    block_ref,
    tiles_ref,
    sems,
):
    batch = lax.axis_index("section") % group
    copies = [
        pltpu.make_async_copy(source, target, sems.at[i])
        for i, (source, target) in enumerate(
            [
                (send_hbm.at[0, batch], send_ref),
                (init_hbm.at[batch], init_ref),
                (block_hbm.at[0, batch], block_ref),
                (tiles_hbm.at[0, batch], tiles_ref),
            ]
        )
    ]
    count = sems.shape[0] - len(copies)
    part = weight_ref.shape[0] // count
    for i in range(count):
        rows = pl.ds(i * part, part)
        copies.append(
            pltpu.make_async_copy(
                weight_hbm.at[0, rows], weight_ref.at[rows], sems.at[4 + i]
            )
        )
    for copy in copies:
        copy.start()
    copies[0].wait()
    pick = pick_matrix(send_ref[...], init_ref.shape[0])
    pick_ref[...] = pick
    copies[1].wait()
    out_ref[...] = jnp.dot(pick, init_ref[...], preferred_element_type=f32).astype(bf16)
    copies[2].wait()
    copies[3].wait()
    row_blocks, tiles = tiles_ref.shape[:2]
    for r in range(row_blocks):
        own = far = None
        for t in range(tiles):
            tile = tiles_ref[r, t].astype(f32)
            is_own = block_ref[r, t] == 0
            own_t = tile * jnp.where(is_own, 1.0, 0.0)
            far_t = tile * jnp.where(is_own, 0.0, 1.0)
            own = own_t if own is None else own + own_t
            far = far_t if far is None else far + far_t
        mix_ref[r] = jnp.concatenate([own, far], axis=1).astype(bf16)
    for copy in copies[4:]:
        copy.wait()


def layer_kernel(group, stage, step, has_current, has_old, has_x, *refs):
    refs = list(refs)
    mix_ref, init_ref, pick_ref, bound_ref = refs[:4]
    weights = refs[4 : 4 + group]
    refs = refs[4 + group :]
    current_ref = refs.pop(0) if has_current else init_ref
    end = step == group - 1
    earlier = [refs.pop(0) for _ in range(group - 2)] if end else []
    old = [refs.pop(0) for _ in range(group)] if has_old else []
    mixed_ref = refs.pop()
    spare = None if has_x else refs.pop()
    picked = [refs.pop() for _ in range(group)][::-1] if end else []
    if has_x:
        x_ref, out_ref = refs
    else:
        x_ref, out_ref = spare, None

    section = lax.axis_index("section")
    member = section % group
    row_blocks, side = mix_ref.shape[:2]
    boundary = bound_ref[...]
    for r in range(row_blocks):
        rows = pl.ds(r * side, side)
        both = jnp.concatenate([current_ref[rows, :], boundary], axis=0)
        aggregate = jnp.dot(mix_ref[r], both, preferred_element_type=f32)
        initial = init_ref[rows, :].astype(f32)
        mixed_ref[rows, :] = ((1.0 - restart) * aggregate + restart * initial).astype(bf16)

    layer = (section // group) * group + step + 1
    beta = f32(0.0)
    for number in range(step + 1, lax.axis_size("section") + 1, group):
        beta = jnp.where(layer == number, f32(math.log(strength / number + 1.0)), beta)

    for shift in range(group):

        @pl.when((member + shift) % group == step)
        def _(weight_ref=weights[shift]):
            mixed = mixed_ref[...]
            product = jnp.dot(mixed, weight_ref[...], preferred_element_type=f32)
            x = (1.0 - beta) * mixed.astype(f32) + beta * product
            x_ref[...] = jnp.maximum(x, 0.0).astype(bf16)

    if out_ref is not None:
        out_ref[...] = jnp.dot(
            pick_ref[...], x_ref[...], preferred_element_type=f32
        ).astype(bf16)

    if end:
        layers = earlier + ([current_ref] if group > 1 else []) + [x_ref]

        def pick_from(sources):
            for target, source in zip(picked, sources):
                target[...] = source[...]

        for value in range(group):
            here = member == value
            if old:
                here = here & (section // group == stage)

            @pl.when(here)
            def _(value=value):
                pick_from([layers[(value - by) % group] for by in range(group)])

        if old:

            @pl.when(section // group != stage)
            def _():
                pick_from(old)


def write_kernel(group, shifts, *refs):
    pieces = refs[: len(shifts)]
    target, sems = refs[-2:]
    member = lax.axis_index("section") % group
    copies = [
        pltpu.make_async_copy(piece, target.at[0, (member + by) % group], sems.at[i])
        for i, (by, piece) in enumerate(zip(shifts, pieces))
    ]
    for copy in copies:
        copy.start()
    for copy in copies:
        copy.wait()


def on_device(initial_feat, layer_weight, tile_column, tile_values, send_rows):
    section_count = lax.axis_size("section")
    batches, rows, width = initial_feat.shape
    group = batches
    stages = section_count // group
    row_blocks, tiles, side = tile_values.shape[2:5]
    sent = send_rows.shape[2] * send_rows.shape[3]

    def shifted(x, by):
        pairs = [(s, (s // group) * group + (s - by) % group) for s in range(section_count)]
        return lax.ppermute(x, "section", pairs)

    def crossed(x):
        pairs = [(s, s + group) for s in range(section_count - group)]
        return lax.ppermute(x, "section", pairs)

    def exchanged(x):
        return lax.all_to_all(x, "dom", split_axis=0, concat_axis=0, tiled=True)

    def first():
        chunks = 4
        return call(
            functools.partial(first_kernel, group),
            [
                (sent, width),
                (sent, rows),
                (row_blocks, side, 2 * side),
                (rows, width),
                layer_weight.shape[1:],
            ],
            [HBM] * 5,
            [VMEM] * 5,
            [
                pltpu.VMEM(send_rows.shape[2:], jnp.int32),
                pltpu.SMEM((row_blocks, tiles), jnp.int32),
                pltpu.VMEM(tile_values.shape[2:], bf16),
                pltpu.SemaphoreType.DMA((4 + chunks,)),
            ],
        )(
            *[
                pltpu.with_memory_space_constraint(x, pltpu.HBM)
                for x in (send_rows, tile_column, initial_feat, tile_values, layer_weight)
            ]
        )

    def layer(stage, step, shared, boundary, weights, currents, old):
        end = step == group - 1
        has_x = not (end and stage == stages - 1)
        has_current = bool(currents)
        operands = list(shared) + [boundary] + weights
        if has_current:
            operands.append(currents[-1])
        if end:
            operands += currents[-group + 1 : -1]
            operands += old
        outs = [(rows, width), (sent, width)] if has_x else []
        if end:
            outs += [(rows, width)] * group
        scratch = [] if has_x else [pltpu.VMEM((rows, width), bf16)]
        scratch.append(pltpu.VMEM((rows, width), bf16))
        flops = 2 * width * rows * (2 * side + width) + 2 * width * rows * sent
        moved = 2 * width * (width + 3 * rows)
        return call(
            functools.partial(
                layer_kernel, group, stage, step, has_current, end and bool(old), has_x
            ),
            outs,
            [VMEM] * len(operands),
            [VMEM] * len(outs),
            scratch,
            cost=pl.CostEstimate(flops=flops, bytes_accessed=moved, transcendentals=0),
        )(*operands)

    outgoing, pick, mix, init, own_weight = first()
    weights = [own_weight] + [shifted(own_weight, by) for by in range(1, group)]
    boundary = exchanged(outgoing)
    shared = [mix, init, pick]
    current = None
    picked = []
    for stage in range(stages):
        currents = [] if stage == 0 else [current]
        for step in range(group):
            result = layer(stage, step, shared, boundary, weights, currents, picked)
            if step < group - 1:
                currents.append(result[0])
                boundary = exchanged(result[1])
            else:
                picked = result[-group:]
        if stage < stages - 1:
            rows_sent = crossed(result[1])
            current = crossed(result[0])
            boundary = exchanged(rows_sent)

    pieces = [shifted(picked[by], by) for by in range(1, group)]
    shape = (1, batches, rows, width)
    target = call(
        functools.partial(write_kernel, group, [0]),
        [shape],
        [VMEM],
        [HBM],
        [pltpu.SemaphoreType.DMA((1,))],
        cost=pl.CostEstimate(flops=0, bytes_accessed=4 * rows * width, transcendentals=0),
    )(picked[0])[0]
    if group == 1:
        return target
    return call(
        lambda *refs: write_kernel(
            group, range(1, group), *refs[: group - 1], *refs[group:]
        ),
        [shape],
        [VMEM] * (group - 1) + [HBM],
        [HBM],
        [pltpu.SemaphoreType.DMA((group - 1,))],
        aliases={group - 1: 0},
    )(*pieces, target)[0]


def solution(mesh):
    in_specs = (
        P(None, "dom", None),
        P("section", None, None),
        P("dom", None, None, None),
        P("dom", None, None, None, None, None),
        P("dom", None, None, None),
    )
    out_specs = P("section", None, "dom", None)
    return jax.shard_map(
        on_device, mesh=mesh, in_specs=in_specs, out_specs=out_specs, check_vma=False
    )
```

time: 94.6 us -> 77.3 us (0.82)
  local copies, waits for them, and re-layouts: 14.6 us -> 3.23 us
  blocking collectives: 26.9 us -> 38.1 us
  waiting for transfers between devices: 18.7 us -> 8.41 us
  starting transfers between devices: 20.6 us -> 16.4 us
  other arithmetic: 3.46 us -> 0 us
  Pallas kernels: 8.93 us -> 10.4 us
    unnamed x42 -> x12, local copies, waits for them, and re-layouts: 14.6 us -> 3.23 us
    all_to_all x2 -> x3, blocking collectives: 26.9 us -> 38.1 us  [exchanged(): return lax.all_to_all(x, 'dom', split_axis=0, concat_axis=0, tiled=True)]
    all_to_all x2 -> x1, waiting for transfers between devices: 8.52 us -> 1.6 us  [exchanged(): return lax.all_to_all(x, 'dom', split_axis=0, concat_axis=0, tiled=True)]
    all_to_all x2 -> x1, starting transfers between devices: 9.69 us -> 5.87 us  [exchanged(): return lax.all_to_all(x, 'dom', split_axis=0, concat_axis=0, tiled=True)]
    ppermute x2, waiting for transfers between devices: 8.6 us -> 6.08 us  [crossed(): return lax.ppermute(x, 'section', pairs)]
    another operation x3 -> x0, other arithmetic: 2.19 us -> none  [the longest x2 1.96 us: on_device(): stack = jnp.stack(kept)]
    pallas_call x5 -> x7, Pallas kernels: 8.93 us -> 10.4 us  [the longest x4 6.96 us: layer(): call(functools.partial(layer_kernel, group, stage, step, has_current, end...]
    ppermute x2, starting transfers between devices: 7.08 us -> 5.92 us  [crossed(): return lax.ppermute(x, 'section', pairs)]
  transfers between devices with their start and end apart: 6 -> 5, of which waited for: 5 -> 4; matrix products, arithmetic and copies ran while one was open for 2% -> 0% of each run, Pallas kernels for 1% -> 1%
where the time goes in v2:
time: 77.3 us; the launch traced here: 76.5 us
  blocking collectives  38.1 us (49%)
  starting transfers between devices  16.4 us (21%)
  Pallas kernels  10.4 us (13%)
  waiting for transfers between devices  8.41 us (11%)
  local copies, waits for them, and re-layouts  3.23 us (4%)
    all_to_all x3, blocking collectives, exchanged(): return lax.all_to_all(x, 'dom', split_axis=0, concat_axis=0, tiled=True)  38.1 us
    pallas_call x4, Pallas kernels, layer(): call(functools.partial(layer_kernel, group, stage, step, has_current, end...  6.96 us
    ppermute x2, waiting for transfers between devices, crossed(): return lax.ppermute(x, 'section', pairs)  6.08 us
    ppermute x2, starting transfers between devices, crossed(): return lax.ppermute(x, 'section', pairs)  5.92 us
    all_to_all x1, starting transfers between devices, exchanged(): return lax.all_to_all(x, 'dom', split_axis=0, concat_axis=0, tiled=True)  5.87 us
    ppermute x2, starting transfers between devices, shifted(): return lax.ppermute(x, 'section', pairs)  4.58 us
    unnamed x12, local copies, waits for them, and re-layouts  3.23 us
    pallas_call x1, Pallas kernels, first(): call(functools.partial(first_kernel, group), [(sent, width), (sent, rows)...  1.84 us
  transfers between devices with their start and end apart: 5, of which 4 were waited for; matrix products, arithmetic and copies ran while one was open for 0% of the time, Pallas kernels for 1%

profile of v2, /device:TPU:1, one launch (start us, length us, event | category | flops | bytes accessed | tf_op | source)
XLA Modules:
  0.0 76.5 jit_solution(7038324307359067158)
XLA Ops:
  0.0 1.8 %shard_map.55 = (bf16[128,1024]{1,0:T(8,128)(2,1)S(1)}, bf16[128,256]{1,0:T(8,128)(2,1)S(1)}, bf16[2,128,256]{2,1,0:T(8,128)(2,1)S(1)}, bf16[256,1024]{1,0:T(8,128)(2,1)S(1)}, bf16[1024,1024]{1,0:T(8,128)(2,1)S(1)}) custom-call(s32[1,2,8,16]{3,2,1,0:T(8,128)} %send_hbm.1, s32[1,2,2,4]{3,2,1,0:T(2,128)} %block_hbm.1, bf16[2,256,1024]{2,1,0:T(8,128)(2,1)} %init_hbm.1, ...), custom_call_target="tpu_custom_call" | custom-call | tf_op jit(solution)/shard_map/pallas_call | solution.py:218
  1.8 0.1 collective-permute-start
  1.9 14.9 %all_to_all.44 = bf16[8,16,1024]{2,1,0:T(8,128)(2,1)S(1)} all-to-all(bf16[8,16,1024]{2,1,0:T(8,128)(2,1)S(1)} %bitcast.12), channel_id=1, replica_groups=mesh['section'=4,'dom'=8] {'dom'}, dimensions={0} | all-to-all | bytes 524288 | tf_op jit(solution)/shard_map/all_to_all | solution.py:214
  16.9 0.0 collective-permute-done.refs_5_
  16.9 0.0 copy-start
  16.9 1.3 %shard_map.56 = (bf16[256,1024]{1,0:T(8,128)(2,1)S(1)}, bf16[128,1024]{1,0:T(8,128)(2,1)S(1)}) custom-call(bf16[2,128,256]{2,1,0:T(8,128)(2,1)S(1)} %get-tuple-element.20.refs_0_, bf16[256,1024]{1,0:T(8,128)(2,1)S(1)} %get-tuple-element.21.refs_1_, bf16[128,256]{1,0:T(8,128)(2,1)S(1)} %get-tuple-element.22.refs_2_, bf16[128,1024]{1,0:T(8,128)(2,1)S(1)} %bitcast.10, ...), custom_call_target="tpu_custom_call" | custom-call | flops 738197504 | bytes 3670016 | tf_op jit(solution)/shard_map/pallas_call | solution.py:259
  18.2 12.0 %all_to_all.45 = bf16[8,16,1024]{2,1,0:T(8,128)(2,1)S(1)} all-to-all(bf16[8,16,1024]{2,1,0:T(8,128)(2,1)S(1)} %bitcast.14), channel_id=1, replica_groups=mesh['section'=4,'dom'=8] {'dom'}, dimensions={0} | all-to-all | bytes 524288 | tf_op jit(solution)/shard_map/all_to_all | solution.py:214
  30.1 0.0 copy-done
  30.1 2.1 %shard_map.57 = (bf16[256,1024]{1,0:T(8,128)(2,1)}, bf16[128,1024]{1,0:T(8,128)(2,1)S(1)}, bf16[256,1024]{1,0:T(8,128)(2,1)S(1)}, bf16[256,1024]{1,0:T(8,128)(2,1)S(1)}) custom-call(bf16[2,128,256]{2,1,0:T(8,128)(2,1)S(1)} %get-tuple-element.20.refs_0_, bf16[256,1024]{1,0:T(8,128)(2,1)S(1)} %get-tuple-element.21.refs_1_, ...), custom_call_target="tpu_custom_call" | custom-call | flops 738197504 | bytes 3670016 | tf_op jit(solution)/shard_map/pallas_call | solution.py:259
  32.3 0.0 copy-start.2
  32.3 0.8 %copy-done.2 = bf16[256,1024]{1,0:T(8,128)(2,1)} copy-done((bf16[256,1024]{1,0:T(8,128)(2,1)}, bf16[256,1024]{1,0:T(8,128)(2,1)S(1)}, u32[]{:S(2)}) %copy-start.2) | copy-done | bytes 524312
  33.1 0.0 copy-start.4
  33.1 0.8 %copy-done.4 = bf16[256,1024]{1,0:T(8,128)(2,1)} copy-done((bf16[256,1024]{1,0:T(8,128)(2,1)}, bf16[256,1024]{1,0:T(8,128)(2,1)S(1)}, u32[]{:S(2)}) %copy-start.4) | copy-done | bytes 524312
  33.9 3.8 %collective-permute-start.1 = (bf16[128,1024]{1,0:T(8,128)(2,1)S(1)}, bf16[128,1024]{1,0:T(8,128)(2,1)}, u32[]{:S(2)}, u32[]{:S(2)}) collective-permute-start(bf16[128,1024]{1,0:T(8,128)(2,1)S(1)} %get-tuple-element.27), channel_id=1, source_target_pairs={{0,16},{8,24},{1,17},{9,25},{2,18},{10,26},{3,19},{11,27},{4,20},{... | collective-permute-start | bytes 786440 | tf_op jit(solution)/shard_map/ppermute | solution.py:211
  37.8 2.1 %collective-permute-start.2 = (bf16[256,1024]{1,0:T(8,128)(2,1)}, bf16[256,1024]{1,0:T(8,128)(2,1)}, u32[]{:S(2)}, u32[]{:S(2)}) collective-permute-start(bf16[256,1024]{1,0:T(8,128)(2,1)} %get-tuple-element.28), channel_id=1, source_target_pairs={{0,16},{8,24},{1,17},{9,25},{2,18},{10,26},{3,19},{11,27},{4,20},{... | collective-permute-start | bytes 1572872 | tf_op jit(solution)/shard_map/ppermute | solution.py:211
  39.8 0.5 collective-permute-done.1
  40.3 5.9 %all-to-all-start.2 = ((bf16[8,16,1024]{2,1,0:T(8,128)(2,1)}), bf16[8,16,1024]{2,1,0:T(8,128)(2,1)S(1)}, u32[]{:S(2)}, u32[]{:S(2)}) async-start(bf16[8,16,1024]{2,1,0:T(8,128)(2,1)} %bitcast.4), calls=%async_computation.2 | async-start | bytes 524288 | tf_op jit(solution)/shard_map/all_to_all | solution.py:214
  46.2 5.6 %collective-permute-done.2.refs_6_ = bf16[256,1024]{1,0:T(8,128)(2,1)} collective-permute-done((bf16[256,1024]{1,0:T(8,128)(2,1)}, bf16[256,1024]{1,0:T(8,128)(2,1)}, u32[]{:S(2)}, u32[]{:S(2)}) %collective-permute-start.2) | collective-permute-done | bytes 524320 | tf_op jit(solution)/shard_map/ppermute | solution.py:211
  51.8 1.6 %all-to-all-done.2 = bf16[8,16,1024]{2,1,0:T(8,128)(2,1)S(1)} async-done(((bf16[8,16,1024]{2,1,0:T(8,128)(2,1)}), bf16[8,16,1024]{2,1,0:T(8,128)(2,1)S(1)}, u32[]{:S(2)}, u32[]{:S(2)}) %all-to-all-start.2) | async-done | bytes 262176 | tf_op jit(solution)/shard_map/all_to_all | solution.py:214
  53.4 0.0 copy-start.1
  53.4 1.6 %copy-done.1 = bf16[1024,1024]{1,0:T(8,128)(2,1)S(1)} copy-done((bf16[1024,1024]{1,0:T(8,128)(2,1)S(1)}, bf16[1024,1024]{1,0:T(8,128)(2,1)}, u32[]{:S(2)}) %copy-start.1) | copy-done | bytes 2097176
  55.0 0.0 copy-start.3
  55.0 0.0 copy-start.5
  55.0 2.4 %shard_map.58 = (bf16[256,1024]{1,0:T(8,128)(2,1)S(1)}, bf16[128,1024]{1,0:T(8,128)(2,1)S(1)}) custom-call(bf16[2,128,256]{2,1,0:T(8,128)(2,1)S(1)} %get-tuple-element.20.refs_0_, bf16[256,1024]{1,0:T(8,128)(2,1)S(1)} %get-tuple-element.21.refs_1_, bf16[128,256]{1,0:T(8,128)(2,1)S(1)} %get-tuple-element.22.refs_2_, bf16[128,1024]{1,0:T(8,128)(2,1)S(1)} %bitcast.8, ...), custom_call_target="tpu_custom_call" | custom-call | flops 738197504 | bytes 3670016 | tf_op jit(solution)/shard_map/pallas_call | solution.py:259
  57.4 11.1 %all_to_all.46 = bf16[8,16,1024]{2,1,0:T(8,128)(2,1)S(1)} all-to-all(bf16[8,16,1024]{2,1,0:T(8,128)(2,1)S(1)} %bitcast.13), channel_id=1, replica_groups=mesh['section'=4,'dom'=8] {'dom'}, dimensions={0} | all-to-all | bytes 524288 | tf_op jit(solution)/shard_map/all_to_all | solution.py:214
  68.5 0.0 copy-done.3
  68.5 0.0 copy-done.5
  68.5 1.1 %shard_map.59 = (bf16[256,1024]{1,0:T(8,128)(2,1)S(1)}, bf16[256,1024]{1,0:T(8,128)(2,1)S(1)}) custom-call(bf16[2,128,256]{2,1,0:T(8,128)(2,1)S(1)} %get-tuple-element.20.refs_0_, bf16[256,1024]{1,0:T(8,128)(2,1)S(1)} %get-tuple-element.21.refs_1_, bf16[128,256]{1,0:T(8,128)(2,1)S(1)} %get-tuple-element.22.refs_2_, bf16[128,1024]{1,0:T(8,128)(2,1)S(1)} %bitcast.9, ...), custom_call_target="tpu_custom_call" | custom-call | flops 738197504 | bytes 3670016 | tf_op jit(solution)/shard_map/pallas_call | solution.py:259
  69.7 4.5 %collective-permute-start.3 = (bf16[256,1024]{1,0:T(8,128)(2,1)S(1)}, bf16[256,1024]{1,0:T(8,128)(2,1)S(1)}, u32[]{:S(2)}, u32[]{:S(2)}) collective-permute-start(bf16[256,1024]{1,0:T(8,128)(2,1)S(1)} %get-tuple-element.33), channel_id=1, source_target_pairs={{0,8},{8,0},{16,24},{24,16},{1,9},{9,1},{17,25},{25,17},{2,10},{10... | collective-permute-start | bytes 1572872 | tf_op jit(solution)/shard_map/ppermute | solution.py:207
  74.2 0.8 %shard_map.60.refs_1_ = bf16[1,2,256,1024]{3,2,1,0:T(8,128)(2,1)} custom-call(bf16[256,1024]{1,0:T(8,128)(2,1)S(1)} %get-tuple-element.34.refs_0_), custom_call_target="tpu_custom_call" | custom-call | bytes 1048576 | tf_op jit(solution)/shard_map/pallas_call | solution.py:292
  75.0 0.7 collective-permute-done.3.refs_0_
  75.7 0.8 %shard_map.61 = bf16[1,2,256,1024]{3,2,1,0:T(8,128)(2,1)} custom-call(bf16[256,1024]{1,0:T(8,128)(2,1)S(1)} %collective-permute-done.3.refs_0_, bf16[1,2,256,1024]{3,2,1,0:T(8,128)(2,1)} %shard_map.60.refs_1_), custom_call_target="tpu_custom_call", output_to_operand_aliasing={{}: (1, {})} | custom-call | tf_op jit(solution)/shard_map/pallas_call | solution.py:302
Async XLA Ops:
  1.8 15.0 %collective-permute-start = (bf16[1024,1024]{1,0:T(8,128)(2,1)S(1)}, bf16[1024,1024]{1,0:T(8,128)(2,1)S(1)}, u32[]{:S(2)}, u32[]{:S(2)}) collective-permute-start(bf16[1024,1024]{1,0:T(8,128)(2,1)S(1)} %get-tuple-element.24.refs_4_), channel_id=1, source_target_pairs={{0,8},{8,0},{16,24},{24,16},{1,9},{9,1},{17,25},{25,17},{2,10},{10... | collective-permute-start | bytes 6291464 | tf_op jit(solution)/shard_map/ppermute | solution.py:207
  16.9 13.3 %copy-start = (bf16[1024,1024]{1,0:T(8,128)(2,1)}, bf16[1024,1024]{1,0:T(8,128)(2,1)S(1)}, u32[]{:S(2)}) copy-start(bf16[1024,1024]{1,0:T(8,128)(2,1)S(1)} %collective-permute-done.refs_5_) | copy-start | bytes 6291460
  32.3 0.8 %copy-start.2 = (bf16[256,1024]{1,0:T(8,128)(2,1)}, bf16[256,1024]{1,0:T(8,128)(2,1)S(1)}, u32[]{:S(2)}) copy-start(bf16[256,1024]{1,0:T(8,128)(2,1)S(1)} %get-tuple-element.31.refs_7_) | copy-start | bytes 1572868
  33.1 0.8 %copy-start.4 = (bf16[256,1024]{1,0:T(8,128)(2,1)}, bf16[256,1024]{1,0:T(8,128)(2,1)S(1)}, u32[]{:S(2)}) copy-start(bf16[256,1024]{1,0:T(8,128)(2,1)S(1)} %get-tuple-element.32.refs_8_) | copy-start | bytes 1572868
  33.9 6.4 %collective-permute-start.1 = (bf16[128,1024]{1,0:T(8,128)(2,1)S(1)}, bf16[128,1024]{1,0:T(8,128)(2,1)}, u32[]{:S(2)}, u32[]{:S(2)}) collective-permute-start(bf16[128,1024]{1,0:T(8,128)(2,1)S(1)} %get-tuple-element.27), channel_id=1, source_target_pairs={{0,16},{8,24},{1,17},{9,25},{2,18},{10,26},{3,19},{11,27},{4,20},{... | collective-permute-start | bytes 786440 | tf_op jit(solution)/shard_map/ppermute | solution.py:211
  37.8 14.0 %collective-permute-start.2 = (bf16[256,1024]{1,0:T(8,128)(2,1)}, bf16[256,1024]{1,0:T(8,128)(2,1)}, u32[]{:S(2)}, u32[]{:S(2)}) collective-permute-start(bf16[256,1024]{1,0:T(8,128)(2,1)} %get-tuple-element.28), channel_id=1, source_target_pairs={{0,16},{8,24},{1,17},{9,25},{2,18},{10,26},{3,19},{11,27},{4,20},{... | collective-permute-start | bytes 1572872 | tf_op jit(solution)/shard_map/ppermute | solution.py:211
  40.3 13.0 %all-to-all-start.2 = ((bf16[8,16,1024]{2,1,0:T(8,128)(2,1)}), bf16[8,16,1024]{2,1,0:T(8,128)(2,1)S(1)}, u32[]{:S(2)}, u32[]{:S(2)}) async-start(bf16[8,16,1024]{2,1,0:T(8,128)(2,1)} %bitcast.4), calls=%async_computation.2 | async-start | bytes 524288 | tf_op jit(solution)/shard_map/all_to_all | solution.py:214
  53.4 1.6 %copy-start.1 = (bf16[1024,1024]{1,0:T(8,128)(2,1)S(1)}, bf16[1024,1024]{1,0:T(8,128)(2,1)}, u32[]{:S(2)}) copy-start(bf16[1024,1024]{1,0:T(8,128)(2,1)} %copy-done) | copy-start | bytes 6291460
  55.0 13.6 %copy-start.3 = (bf16[256,1024]{1,0:T(8,128)(2,1)S(1)}, bf16[256,1024]{1,0:T(8,128)(2,1)}, u32[]{:S(2)}) copy-start(bf16[256,1024]{1,0:T(8,128)(2,1)} %copy-done.2) | copy-start | bytes 1572868
  55.0 13.6 %copy-start.5 = (bf16[256,1024]{1,0:T(8,128)(2,1)S(1)}, bf16[256,1024]{1,0:T(8,128)(2,1)}, u32[]{:S(2)}) copy-start(bf16[256,1024]{1,0:T(8,128)(2,1)} %copy-done.4) | copy-start | bytes 1572868
  69.7 6.0 %collective-permute-start.3 = (bf16[256,1024]{1,0:T(8,128)(2,1)S(1)}, bf16[256,1024]{1,0:T(8,128)(2,1)S(1)}, u32[]{:S(2)}, u32[]{:S(2)}) collective-permute-start(bf16[256,1024]{1,0:T(8,128)(2,1)S(1)} %get-tuple-element.33), channel_id=1, source_target_pairs={{0,8},{8,0},{16,24},{24,16},{1,9},{9,1},{17,25},{25,17},{2,10},{10... | collective-permute-start | bytes 1572872 | tf_op jit(solution)/shard_map/ppermute | solution.py:207

commit v3 on v2

--- a/solution.py
+++ b/solution.py
@@ -3,6 +3,7 @@
 
 import jax
 import jax.numpy as jnp
+import numpy as np
 from jax import lax
 from jax.experimental import pallas as pl
 from jax.experimental.pallas import tpu as pltpu
@@ -30,10 +31,22 @@
     )
 
 
+def partner_order(count):
+    return [int(i) for i in np.random.RandomState(2756).permutation(count)]
+
+
+def looked_up(index, table):
+    result = jnp.zeros_like(index)
+    for i, value in enumerate(table):
+        result = jnp.where(index == i, value, result)
+    return result
+
+
 def pick_matrix(send, rows):
     parts, each = send.shape
     total = parts * each
     line = lax.broadcasted_iota(jnp.int32, (total, parts), 0) // each
+    line = looked_up(line, partner_order(parts))
     part = lax.broadcasted_iota(jnp.int32, (total, parts), 1)
     spread = jnp.dot(
         (line == part).astype(f32),
@@ -46,6 +59,13 @@
     row = jnp.sum(jnp.where(slot == lane, spread, 0.0), axis=1, keepdims=True)
     local = lax.broadcasted_iota(jnp.int32, (total, rows), 1).astype(f32)
     return (local == row).astype(bf16)
+
+
+def arrival_matrix(parts, each):
+    total = parts * each
+    here = lax.broadcasted_iota(jnp.int32, (total, total), 1)
+    source = looked_up(here // each, partner_order(parts)) * each + here % each
+    return (lax.broadcasted_iota(jnp.int32, (total, total), 0) == source).astype(bf16)
 
 
 def first_kernel(
@@ -96,6 +116,7 @@
     copies[2].wait()
     copies[3].wait()
     row_blocks, tiles = tiles_ref.shape[:2]
+    arrival = arrival_matrix(*send_ref.shape)
     for r in range(row_blocks):
         own = far = None
         for t in range(tiles):
@@ -105,6 +126,7 @@
             far_t = tile * jnp.where(is_own, 0.0, 1.0)
             own = own_t if own is None else own + own_t
             far = far_t if far is None else far + far_t
+        far = jnp.dot(far.astype(bf16), arrival, preferred_element_type=f32)
         mix_ref[r] = jnp.concatenate([own, far], axis=1).astype(bf16)
     for copy in copies[4:]:
         copy.wait()
@@ -210,8 +232,19 @@
         pairs = [(s, s + group) for s in range(section_count - group)]
         return lax.ppermute(x, "section", pairs)
 
+    parts = lax.axis_size("dom")
+    order = partner_order(parts)
+    groups = [[s * parts + p for p in order] for s in range(section_count)]
+
     def exchanged(x):
-        return lax.all_to_all(x, "dom", split_axis=0, concat_axis=0, tiled=True)
+        return lax.all_to_all(
+            x,
+            ("section", "dom"),
+            split_axis=0,
+            concat_axis=0,
+            axis_index_groups=groups,
+            tiled=True,
+        )
 
     def first():
         chunks = 4

time: 77.3 us -> 70.4 us (0.911)
  blocking collectives: 38.1 us -> 32.2 us
  waiting for transfers between devices: 8.41 us -> 5.36 us
  starting transfers between devices: 16.4 us -> 18.1 us
    all_to_all x3, blocking collectives: 38.1 us -> 32.2 us  [exchanged(): lax.all_to_all(x, ('section', 'dom'), split_axis=0, concat_axis=0, axis_i...]
    ppermute x2, waiting for transfers between devices: 6.08 us -> 4.13 us  [crossed(): return lax.ppermute(x, 'section', pairs)]
    ppermute x2, starting transfers between devices: 4.58 us -> 5.88 us  [shifted(): return lax.ppermute(x, 'section', pairs)]
    all_to_all x1, waiting for transfers between devices: 1.6 us -> 0.5 us  [exchanged(): lax.all_to_all(x, ('section', 'dom'), split_axis=0, concat_axis=0, axis_i...]
where the time goes in v3:
time: 70.4 us; the launch traced here: 69.4 us
  blocking collectives  32.2 us (46%)
  starting transfers between devices  18.1 us (26%)
  Pallas kernels  10.4 us (15%)
  waiting for transfers between devices  5.36 us (8%)
  local copies, waits for them, and re-layouts  3.23 us (5%)
    all_to_all x3, blocking collectives, exchanged(): lax.all_to_all(x, ('section', 'dom'), split_axis=0, concat_axis=0, axis_i...  32.2 us
    pallas_call x4, Pallas kernels, layer(): call(functools.partial(layer_kernel, group, stage, step, has_current, end...  6.97 us
    all_to_all x1, starting transfers between devices, exchanged(): lax.all_to_all(x, ('section', 'dom'), split_axis=0, concat_axis=0, axis_i...  6.34 us
    ppermute x2, starting transfers between devices, crossed(): return lax.ppermute(x, 'section', pairs)  5.92 us
    ppermute x2, starting transfers between devices, shifted(): return lax.ppermute(x, 'section', pairs)  5.88 us
    ppermute x2, waiting for transfers between devices, crossed(): return lax.ppermute(x, 'section', pairs)  4.13 us
    unnamed x12, local copies, waits for them, and re-layouts  3.23 us
    pallas_call x1, Pallas kernels, first(): call(functools.partial(first_kernel, group), [(sent, width), (sent, rows)...  1.84 us
  transfers between devices with their start and end apart: 5, of which 4 were waited for; matrix products, arithmetic and copies ran while one was open for 0% of the time, Pallas kernels for 1%

profile of v3, /device:TPU:1, one launch (start us, length us, event | category | flops | bytes accessed | tf_op | source)
XLA Modules:
  0.0 69.4 jit_solution(13449361692912652534)
XLA Ops:
  0.0 1.8 %shard_map.55 = (bf16[128,1024]{1,0:T(8,128)(2,1)S(1)}, bf16[128,256]{1,0:T(8,128)(2,1)S(1)}, bf16[2,128,256]{2,1,0:T(8,128)(2,1)S(1)}, bf16[256,1024]{1,0:T(8,128)(2,1)S(1)}, bf16[1024,1024]{1,0:T(8,128)(2,1)S(1)}) custom-call(s32[1,2,8,16]{3,2,1,0:T(8,128)} %send_hbm.1, s32[1,2,2,4]{3,2,1,0:T(2,128)} %block_hbm.1, bf16[2,256,1024]{2,1,0:T(8,128)(2,1)} %init_hbm.1, ...), custom_call_target="tpu_custom_call" | custom-call | tf_op jit(solution)/shard_map/pallas_call | solution.py:251
  1.8 0.1 collective-permute-start
  1.9 13.3 %all_to_all.44 = bf16[8,16,1024]{2,1,0:T(8,128)(2,1)S(1)} all-to-all(bf16[8,16,1024]{2,1,0:T(8,128)(2,1)S(1)} %bitcast.12), channel_id=1, replica_groups={{5,0,2,3,6,1,4,7},{13,8,10,11,14,9,12,15},{21,16,18,19,22,17,20,23},{29..., dimensions={0} | all-to-all | bytes 524288 | tf_op jit(solution)/shard_map/all_to_all | solution.py:240
  15.2 0.0 collective-permute-done.refs_5_
  15.2 0.0 copy-start
  15.2 1.3 %shard_map.56 = (bf16[256,1024]{1,0:T(8,128)(2,1)S(1)}, bf16[128,1024]{1,0:T(8,128)(2,1)S(1)}) custom-call(bf16[2,128,256]{2,1,0:T(8,128)(2,1)S(1)} %get-tuple-element.20.refs_0_, bf16[256,1024]{1,0:T(8,128)(2,1)S(1)} %get-tuple-element.21.refs_1_, bf16[128,256]{1,0:T(8,128)(2,1)S(1)} %get-tuple-element.22.refs_2_, bf16[128,1024]{1,0:T(8,128)(2,1)S(1)} %bitcast.10, ...), custom_call_target="tpu_custom_call" | custom-call | flops 738197504 | bytes 3670016 | tf_op jit(solution)/shard_map/pallas_call | solution.py:292
  16.5 8.2 %all_to_all.45 = bf16[8,16,1024]{2,1,0:T(8,128)(2,1)S(1)} all-to-all(bf16[8,16,1024]{2,1,0:T(8,128)(2,1)S(1)} %bitcast.14), channel_id=1, replica_groups={{5,0,2,3,6,1,4,7},{13,8,10,11,14,9,12,15},{21,16,18,19,22,17,20,23},{29..., dimensions={0} | all-to-all | bytes 524288 | tf_op jit(solution)/shard_map/all_to_all | solution.py:240
  24.7 0.0 copy-done
  24.7 2.1 %shard_map.57 = (bf16[256,1024]{1,0:T(8,128)(2,1)}, bf16[128,1024]{1,0:T(8,128)(2,1)S(1)}, bf16[256,1024]{1,0:T(8,128)(2,1)S(1)}, bf16[256,1024]{1,0:T(8,128)(2,1)S(1)}) custom-call(bf16[2,128,256]{2,1,0:T(8,128)(2,1)S(1)} %get-tuple-element.20.refs_0_, bf16[256,1024]{1,0:T(8,128)(2,1)S(1)} %get-tuple-element.21.refs_1_, ...), custom_call_target="tpu_custom_call" | custom-call | flops 738197504 | bytes 3670016 | tf_op jit(solution)/shard_map/pallas_call | solution.py:292
  26.8 0.0 copy-start.2
  26.8 0.8 %copy-done.2 = bf16[256,1024]{1,0:T(8,128)(2,1)} copy-done((bf16[256,1024]{1,0:T(8,128)(2,1)}, bf16[256,1024]{1,0:T(8,128)(2,1)S(1)}, u32[]{:S(2)}) %copy-start.2) | copy-done | bytes 524312
  27.6 0.0 copy-start.4
  27.6 0.8 %copy-done.4 = bf16[256,1024]{1,0:T(8,128)(2,1)} copy-done((bf16[256,1024]{1,0:T(8,128)(2,1)}, bf16[256,1024]{1,0:T(8,128)(2,1)S(1)}, u32[]{:S(2)}) %copy-start.4) | copy-done | bytes 524312
  28.4 3.8 %collective-permute-start.1 = (bf16[128,1024]{1,0:T(8,128)(2,1)S(1)}, bf16[128,1024]{1,0:T(8,128)(2,1)}, u32[]{:S(2)}, u32[]{:S(2)}) collective-permute-start(bf16[128,1024]{1,0:T(8,128)(2,1)S(1)} %get-tuple-element.27), channel_id=1, source_target_pairs={{0,16},{8,24},{1,17},{9,25},{2,18},{10,26},{3,19},{11,27},{4,20},{... | collective-permute-start | bytes 786440 | tf_op jit(solution)/shard_map/ppermute | solution.py:233
  32.3 2.1 %collective-permute-start.2 = (bf16[256,1024]{1,0:T(8,128)(2,1)}, bf16[256,1024]{1,0:T(8,128)(2,1)}, u32[]{:S(2)}, u32[]{:S(2)}) collective-permute-start(bf16[256,1024]{1,0:T(8,128)(2,1)} %get-tuple-element.28), channel_id=1, source_target_pairs={{0,16},{8,24},{1,17},{9,25},{2,18},{10,26},{3,19},{11,27},{4,20},{... | collective-permute-start | bytes 1572872 | tf_op jit(solution)/shard_map/ppermute | solution.py:233
  34.4 0.5 collective-permute-done.1
  34.9 6.3 %all-to-all-start.2 = ((bf16[8,16,1024]{2,1,0:T(8,128)(2,1)}), bf16[8,16,1024]{2,1,0:T(8,128)(2,1)S(1)}, u32[]{:S(2)}, u32[]{:S(2)}) async-start(bf16[8,16,1024]{2,1,0:T(8,128)(2,1)} %bitcast.4), calls=%async_computation.2 | async-start | bytes 524288 | tf_op jit(solution)/shard_map/all_to_all | solution.py:240
  41.2 3.6 %collective-permute-done.2.refs_6_ = bf16[256,1024]{1,0:T(8,128)(2,1)} collective-permute-done((bf16[256,1024]{1,0:T(8,128)(2,1)}, bf16[256,1024]{1,0:T(8,128)(2,1)}, u32[]{:S(2)}, u32[]{:S(2)}) %collective-permute-start.2) | collective-permute-done | bytes 524320 | tf_op jit(solution)/shard_map/ppermute | solution.py:233
  44.8 0.5 all-to-all-done.2
  45.3 0.0 copy-start.1
  45.3 1.6 %copy-done.1 = bf16[1024,1024]{1,0:T(8,128)(2,1)S(1)} copy-done((bf16[1024,1024]{1,0:T(8,128)(2,1)S(1)}, bf16[1024,1024]{1,0:T(8,128)(2,1)}, u32[]{:S(2)}) %copy-start.1) | copy-done | bytes 2097176
  46.9 0.0 copy-start.3
  46.9 0.0 copy-start.5
  46.9 2.4 %shard_map.58 = (bf16[256,1024]{1,0:T(8,128)(2,1)S(1)}, bf16[128,1024]{1,0:T(8,128)(2,1)S(1)}) custom-call(bf16[2,128,256]{2,1,0:T(8,128)(2,1)S(1)} %get-tuple-element.20.refs_0_, bf16[256,1024]{1,0:T(8,128)(2,1)S(1)} %get-tuple-element.21.refs_1_, bf16[128,256]{1,0:T(8,128)(2,1)S(1)} %get-tuple-element.22.refs_2_, bf16[128,1024]{1,0:T(8,128)(2,1)S(1)} %bitcast.8, ...), custom_call_target="tpu_custom_call" | custom-call | flops 738197504 | bytes 3670016 | tf_op jit(solution)/shard_map/pallas_call | solution.py:292
  49.3 10.8 %all_to_all.46 = bf16[8,16,1024]{2,1,0:T(8,128)(2,1)S(1)} all-to-all(bf16[8,16,1024]{2,1,0:T(8,128)(2,1)S(1)} %bitcast.13), channel_id=1, replica_groups={{5,0,2,3,6,1,4,7},{13,8,10,11,14,9,12,15},{21,16,18,19,22,17,20,23},{29..., dimensions={0} | all-to-all | bytes 524288 | tf_op jit(solution)/shard_map/all_to_all | solution.py:240
  60.1 0.0 copy-done.3
  60.1 0.0 copy-done.5
  60.1 1.1 %shard_map.59 = (bf16[256,1024]{1,0:T(8,128)(2,1)S(1)}, bf16[256,1024]{1,0:T(8,128)(2,1)S(1)}) custom-call(bf16[2,128,256]{2,1,0:T(8,128)(2,1)S(1)} %get-tuple-element.20.refs_0_, bf16[256,1024]{1,0:T(8,128)(2,1)S(1)} %get-tuple-element.21.refs_1_, bf16[128,256]{1,0:T(8,128)(2,1)S(1)} %get-tuple-element.22.refs_2_, bf16[128,1024]{1,0:T(8,128)(2,1)S(1)} %bitcast.9, ...), custom_call_target="tpu_custom_call" | custom-call | flops 738197504 | bytes 3670016 | tf_op jit(solution)/shard_map/pallas_call | solution.py:292
  61.3 5.8 %collective-permute-start.3 = (bf16[256,1024]{1,0:T(8,128)(2,1)S(1)}, bf16[256,1024]{1,0:T(8,128)(2,1)S(1)}, u32[]{:S(2)}, u32[]{:S(2)}) collective-permute-start(bf16[256,1024]{1,0:T(8,128)(2,1)S(1)} %get-tuple-element.33), channel_id=1, source_target_pairs={{0,8},{8,0},{16,24},{24,16},{1,9},{9,1},{17,25},{25,17},{2,10},{10... | collective-permute-start | bytes 1572872 | tf_op jit(solution)/shard_map/ppermute | solution.py:229
  67.0 0.8 %shard_map.60.refs_1_ = bf16[1,2,256,1024]{3,2,1,0:T(8,128)(2,1)} custom-call(bf16[256,1024]{1,0:T(8,128)(2,1)S(1)} %get-tuple-element.34.refs_0_), custom_call_target="tpu_custom_call" | custom-call | bytes 1048576 | tf_op jit(solution)/shard_map/pallas_call | solution.py:325
  67.9 0.7 %collective-permute-done.3.refs_0_ = bf16[256,1024]{1,0:T(8,128)(2,1)S(1)} collective-permute-done((bf16[256,1024]{1,0:T(8,128)(2,1)S(1)}, bf16[256,1024]{1,0:T(8,128)(2,1)S(1)}, u32[]{:S(2)}, u32[]{:S(2)}) %collective-permute-start.3) | collective-permute-done | bytes 524320 | tf_op jit(solution)/shard_map/ppermute | solution.py:229
  68.6 0.8 %shard_map.61 = bf16[1,2,256,1024]{3,2,1,0:T(8,128)(2,1)} custom-call(bf16[256,1024]{1,0:T(8,128)(2,1)S(1)} %collective-permute-done.3.refs_0_, bf16[1,2,256,1024]{3,2,1,0:T(8,128)(2,1)} %shard_map.60.refs_1_), custom_call_target="tpu_custom_call", output_to_operand_aliasing={{}: (1, {})} | custom-call | tf_op jit(solution)/shard_map/pallas_call | solution.py:335
Async XLA Ops:
  1.8 13.3 %collective-permute-start = (bf16[1024,1024]{1,0:T(8,128)(2,1)S(1)}, bf16[1024,1024]{1,0:T(8,128)(2,1)S(1)}, u32[]{:S(2)}, u32[]{:S(2)}) collective-permute-start(bf16[1024,1024]{1,0:T(8,128)(2,1)S(1)} %get-tuple-element.24.refs_4_), channel_id=1, source_target_pairs={{0,8},{8,0},{16,24},{24,16},{1,9},{9,1},{17,25},{25,17},{2,10},{10... | collective-permute-start | bytes 6291464 | tf_op jit(solution)/shard_map/ppermute | solution.py:229
  15.2 9.5 %copy-start = (bf16[1024,1024]{1,0:T(8,128)(2,1)}, bf16[1024,1024]{1,0:T(8,128)(2,1)S(1)}, u32[]{:S(2)}) copy-start(bf16[1024,1024]{1,0:T(8,128)(2,1)S(1)} %collective-permute-done.refs_5_) | copy-start | bytes 6291460
  26.8 0.8 %copy-start.2 = (bf16[256,1024]{1,0:T(8,128)(2,1)}, bf16[256,1024]{1,0:T(8,128)(2,1)S(1)}, u32[]{:S(2)}) copy-start(bf16[256,1024]{1,0:T(8,128)(2,1)S(1)} %get-tuple-element.31.refs_7_) | copy-start | bytes 1572868
  27.6 0.8 %copy-start.4 = (bf16[256,1024]{1,0:T(8,128)(2,1)}, bf16[256,1024]{1,0:T(8,128)(2,1)S(1)}, u32[]{:S(2)}) copy-start(bf16[256,1024]{1,0:T(8,128)(2,1)S(1)} %get-tuple-element.32.refs_8_) | copy-start | bytes 1572868
  28.4 6.4 %collective-permute-start.1 = (bf16[128,1024]{1,0:T(8,128)(2,1)S(1)}, bf16[128,1024]{1,0:T(8,128)(2,1)}, u32[]{:S(2)}, u32[]{:S(2)}) collective-permute-start(bf16[128,1024]{1,0:T(8,128)(2,1)S(1)} %get-tuple-element.27), channel_id=1, source_target_pairs={{0,16},{8,24},{1,17},{9,25},{2,18},{10,26},{3,19},{11,27},{4,20},{... | collective-permute-start | bytes 786440 | tf_op jit(solution)/shard_map/ppermute | solution.py:233
  32.3 12.6 %collective-permute-start.2 = (bf16[256,1024]{1,0:T(8,128)(2,1)}, bf16[256,1024]{1,0:T(8,128)(2,1)}, u32[]{:S(2)}, u32[]{:S(2)}) collective-permute-start(bf16[256,1024]{1,0:T(8,128)(2,1)} %get-tuple-element.28), channel_id=1, source_target_pairs={{0,16},{8,24},{1,17},{9,25},{2,18},{10,26},{3,19},{11,27},{4,20},{... | collective-permute-start | bytes 1572872 | tf_op jit(solution)/shard_map/ppermute | solution.py:233
  34.9 10.5 %all-to-all-start.2 = ((bf16[8,16,1024]{2,1,0:T(8,128)(2,1)}), bf16[8,16,1024]{2,1,0:T(8,128)(2,1)S(1)}, u32[]{:S(2)}, u32[]{:S(2)}) async-start(bf16[8,16,1024]{2,1,0:T(8,128)(2,1)} %bitcast.4), calls=%async_computation.2 | async-start | bytes 524288 | tf_op jit(solution)/shard_map/all_to_all | solution.py:240
  45.3 1.6 %copy-start.1 = (bf16[1024,1024]{1,0:T(8,128)(2,1)S(1)}, bf16[1024,1024]{1,0:T(8,128)(2,1)}, u32[]{:S(2)}) copy-start(bf16[1024,1024]{1,0:T(8,128)(2,1)} %copy-done) | copy-start | bytes 6291460
  46.9 13.2 %copy-start.3 = (bf16[256,1024]{1,0:T(8,128)(2,1)S(1)}, bf16[256,1024]{1,0:T(8,128)(2,1)}, u32[]{:S(2)}) copy-start(bf16[256,1024]{1,0:T(8,128)(2,1)} %copy-done.2) | copy-start | bytes 1572868
  46.9 13.2 %copy-start.5 = (bf16[256,1024]{1,0:T(8,128)(2,1)S(1)}, bf16[256,1024]{1,0:T(8,128)(2,1)}, u32[]{:S(2)}) copy-start(bf16[256,1024]{1,0:T(8,128)(2,1)} %copy-done.4) | copy-start | bytes 1572868
  61.3 7.3 %collective-permute-start.3 = (bf16[256,1024]{1,0:T(8,128)(2,1)S(1)}, bf16[256,1024]{1,0:T(8,128)(2,1)S(1)}, u32[]{:S(2)}, u32[]{:S(2)}) collective-permute-start(bf16[256,1024]{1,0:T(8,128)(2,1)S(1)} %get-tuple-element.33), channel_id=1, source_target_pairs={{0,8},{8,0},{16,24},{24,16},{1,9},{9,1},{17,25},{25,17},{2,10},{10... | collective-permute-start | bytes 1572872 | tf_op jit(solution)/shard_map/ppermute | solution.py:229

commit v4 on v3

--- a/solution.py
+++ b/solution.py
@@ -74,12 +74,10 @@
     block_hbm,
     init_hbm,
     tiles_hbm,
-    weight_hbm,
     out_ref,
     pick_ref,
     mix_ref,
     init_ref,
-    weight_ref,
     send_ref,
     block_ref,
     tiles_ref,
@@ -97,15 +95,6 @@
             ]
         )
     ]
-    count = sems.shape[0] - len(copies)
-    part = weight_ref.shape[0] // count
-    for i in range(count):
-        rows = pl.ds(i * part, part)
-        copies.append(
-            pltpu.make_async_copy(
-                weight_hbm.at[0, rows], weight_ref.at[rows], sems.at[4 + i]
-            )
-        )
     for copy in copies:
         copy.start()
     copies[0].wait()
@@ -128,8 +117,6 @@
             far = far_t if far is None else far + far_t
         far = jnp.dot(far.astype(bf16), arrival, preferred_element_type=f32)
         mix_ref[r] = jnp.concatenate([own, far], axis=1).astype(bf16)
-    for copy in copies[4:]:
-        copy.wait()
 
 
 def layer_kernel(group, stage, step, has_current, has_old, has_x, *refs):
@@ -152,32 +139,31 @@
     section = lax.axis_index("section")
     member = section % group
     row_blocks, side = mix_ref.shape[:2]
-    boundary = bound_ref[...]
-    for r in range(row_blocks):
-        rows = pl.ds(r * side, side)
-        both = jnp.concatenate([current_ref[rows, :], boundary], axis=0)
-        aggregate = jnp.dot(mix_ref[r], both, preferred_element_type=f32)
-        initial = init_ref[rows, :].astype(f32)
-        mixed_ref[rows, :] = ((1.0 - restart) * aggregate + restart * initial).astype(bf16)
 
     layer = (section // group) * group + step + 1
     beta = f32(0.0)
     for number in range(step + 1, lax.axis_size("section") + 1, group):
         beta = jnp.where(layer == number, f32(math.log(strength / number + 1.0)), beta)
 
+    def body(weight_ref):
+        boundary = bound_ref[...]
+        for r in range(row_blocks):
+            rows = pl.ds(r * side, side)
+            both = jnp.concatenate([current_ref[rows, :], boundary], axis=0)
+            aggregate = jnp.dot(mix_ref[r], both, preferred_element_type=f32)
+            initial = init_ref[rows, :].astype(f32)
+            mixed_ref[rows, :] = ((1.0 - restart) * aggregate + restart * initial).astype(bf16)
+        mixed = mixed_ref[...]
+        product = jnp.dot(mixed, weight_ref[...], preferred_element_type=f32)
+        x = (1.0 - beta) * mixed.astype(f32) + beta * product
+        x_ref[...] = jnp.maximum(x, 0.0).astype(bf16)
+        if out_ref is not None:
+            out_ref[...] = jnp.dot(
+                pick_ref[...], x_ref[...], preferred_element_type=f32
+            ).astype(bf16)
+
     for shift in range(group):
-
-        @pl.when((member + shift) % group == step)
-        def _(weight_ref=weights[shift]):
-            mixed = mixed_ref[...]
-            product = jnp.dot(mixed, weight_ref[...], preferred_element_type=f32)
-            x = (1.0 - beta) * mixed.astype(f32) + beta * product
-            x_ref[...] = jnp.maximum(x, 0.0).astype(bf16)
-
-    if out_ref is not None:
-        out_ref[...] = jnp.dot(
-            pick_ref[...], x_ref[...], preferred_element_type=f32
-        ).astype(bf16)
+        pl.when((member + shift) % group == step)(functools.partial(body, weights[shift]))
 
     if end:
         layers = earlier + ([current_ref] if group > 1 else []) + [x_ref]
@@ -247,7 +233,6 @@
         )
 
     def first():
-        chunks = 4
         return call(
             functools.partial(first_kernel, group),
             [
@@ -255,20 +240,19 @@
                 (sent, rows),
                 (row_blocks, side, 2 * side),
                 (rows, width),
-                layer_weight.shape[1:],
             ],
-            [HBM] * 5,
-            [VMEM] * 5,
+            [HBM] * 4,
+            [VMEM] * 4,
             [
                 pltpu.VMEM(send_rows.shape[2:], jnp.int32),
                 pltpu.SMEM((row_blocks, tiles), jnp.int32),
                 pltpu.VMEM(tile_values.shape[2:], bf16),
-                pltpu.SemaphoreType.DMA((4 + chunks,)),
+                pltpu.SemaphoreType.DMA((4,)),
             ],
         )(
             *[
                 pltpu.with_memory_space_constraint(x, pltpu.HBM)
-                for x in (send_rows, tile_column, initial_feat, tile_values, layer_weight)
+                for x in (send_rows, tile_column, initial_feat, tile_values)
             ]
         )
 
@@ -300,8 +284,8 @@
             cost=pl.CostEstimate(flops=flops, bytes_accessed=moved, transcendentals=0),
         )(*operands)
 
-    outgoing, pick, mix, init, own_weight = first()
-    weights = [own_weight] + [shifted(own_weight, by) for by in range(1, group)]
+    outgoing, pick, mix, init = first()
+    weights = [shifted(layer_weight[0], by) for by in range(group)]
     boundary = exchanged(outgoing)
     shared = [mix, init, pick]
     current = None

time: 70.4 us -> 71.1 us (level)
  starting transfers between devices: 18.1 us -> 19.7 us
  Pallas kernels: 10.4 us -> 9.56 us
    ppermute x2 -> x3, starting transfers between devices: 5.88 us -> 7.43 us  [shifted(): return lax.ppermute(x, 'section', pairs)]
  transfers between devices with their start and end apart: 5 -> 6, of which waited for: 4 -> 4; matrix products, arithmetic and copies ran while one was open for 0% -> 0% of each run, Pallas kernels for 1% -> 3%
where the time goes in v4:
time: 71.1 us; the launch traced here: 70.1 us
  blocking collectives  32.2 us (45%)
  starting transfers between devices  19.7 us (28%)
  Pallas kernels  9.56 us (13%)
  waiting for transfers between devices  5.38 us (8%)
  local copies, waits for them, and re-layouts  3.22 us (5%)
    all_to_all x3, blocking collectives, exchanged(): lax.all_to_all(x, ('section', 'dom'), split_axis=0, concat_axis=0, axis_i...  32.2 us
    ppermute x3, starting transfers between devices, shifted(): return lax.ppermute(x, 'section', pairs)  7.43 us
    pallas_call x4, Pallas kernels, layer(): call(functools.partial(layer_kernel, group, stage, step, has_current, end...  6.41 us
    all_to_all x1, starting transfers between devices, exchanged(): lax.all_to_all(x, ('section', 'dom'), split_axis=0, concat_axis=0, axis_i...  6.32 us
    ppermute x2, starting transfers between devices, crossed(): return lax.ppermute(x, 'section', pairs)  5.92 us
    ppermute x2, waiting for transfers between devices, crossed(): return lax.ppermute(x, 'section', pairs)  4.15 us
    unnamed x12, local copies, waits for them, and re-layouts  3.22 us
    pallas_call x1, Pallas kernels, first(): call(functools.partial(first_kernel, group), [(sent, width), (sent, rows)...  1.55 us
  transfers between devices with their start and end apart: 6, of which 4 were waited for; matrix products, arithmetic and copies ran while one was open for 0% of the time, Pallas kernels for 3%

profile of v4, /device:TPU:1, one launch (start us, length us, event | category | flops | bytes accessed | tf_op | source)
XLA Modules:
  0.0 70.1 jit_solution(16351515842386441988)
XLA Ops:
  0.0 0.0 collective-permute-start.1
  0.0 1.6 %collective-permute-start = (bf16[1024,1024]{1,0:T(8,128)(2,1)}, bf16[1024,1024]{1,0:T(8,128)(2,1)S(1)}, u32[]{:S(2)}, u32[]{:S(2)}) collective-permute-start(bf16[1024,1024]{1,0:T(8,128)(2,1)} %bitcast.17), channel_id=1, source_target_pairs={{0,0},{8,8},{16,16},{24,24},{1,1},{9,9},{17,17},{25,25},{2,2},{10,... | collective-permute-start | bytes 6291464 | tf_op jit(solution)/shard_map/ppermute | solution.py:215
  1.6 1.6 %shard_map.55 = (bf16[128,1024]{1,0:T(8,128)(2,1)S(1)}, bf16[128,256]{1,0:T(8,128)(2,1)S(1)}, bf16[2,128,256]{2,1,0:T(8,128)(2,1)S(1)}, bf16[256,1024]{1,0:T(8,128)(2,1)S(1)}) custom-call(s32[1,2,8,16]{3,2,1,0:T(8,128)} %send_hbm.1, s32[1,2,2,4]{3,2,1,0:T(2,128)} %block_hbm.1, bf16[2,256,1024]{2,1,0:T(8,128)(2,1)} %init_hbm.1, ...), custom_call_target="tpu_custom_call" | custom-call | tf_op jit(solution)/shard_map/pallas_call | solution.py:236
  3.2 13.3 %all_to_all.44 = bf16[8,16,1024]{2,1,0:T(8,128)(2,1)S(1)} all-to-all(bf16[8,16,1024]{2,1,0:T(8,128)(2,1)S(1)} %bitcast.13), channel_id=1, replica_groups={{5,0,2,3,6,1,4,7},{13,8,10,11,14,9,12,15},{21,16,18,19,22,17,20,23},{29..., dimensions={0} | all-to-all | bytes 524288 | tf_op jit(solution)/shard_map/all_to_all | solution.py:226
  16.4 0.0 collective-permute-done.1.refs_5_
  16.4 0.0 collective-permute-done.refs_4_
  16.4 0.0 copy-start
  16.4 1.2 %shard_map.56 = (bf16[256,1024]{1,0:T(8,128)(2,1)S(1)}, bf16[128,1024]{1,0:T(8,128)(2,1)S(1)}) custom-call(bf16[2,128,256]{2,1,0:T(8,128)(2,1)S(1)} %get-tuple-element.19.refs_0_, bf16[256,1024]{1,0:T(8,128)(2,1)S(1)} %get-tuple-element.20.refs_1_, bf16[128,256]{1,0:T(8,128)(2,1)S(1)} %get-tuple-element.21.refs_2_, bf16[128,1024]{1,0:T(8,128)(2,1)S(1)} %bitcast.11, ...), custom_call_target="tpu_custom_call" | custom-call | flops 738197504 | bytes 3670016 | tf_op jit(solution)/shard_map/pallas_call | solution.py:276
  17.6 8.2 %all_to_all.45 = bf16[8,16,1024]{2,1,0:T(8,128)(2,1)S(1)} all-to-all(bf16[8,16,1024]{2,1,0:T(8,128)(2,1)S(1)} %bitcast.15), channel_id=1, replica_groups={{5,0,2,3,6,1,4,7},{13,8,10,11,14,9,12,15},{21,16,18,19,22,17,20,23},{29..., dimensions={0} | all-to-all | bytes 524288 | tf_op jit(solution)/shard_map/all_to_all | solution.py:226
  25.8 0.0 copy-done
  25.8 2.0 %shard_map.57 = (bf16[256,1024]{1,0:T(8,128)(2,1)}, bf16[128,1024]{1,0:T(8,128)(2,1)S(1)}, bf16[256,1024]{1,0:T(8,128)(2,1)S(1)}, bf16[256,1024]{1,0:T(8,128)(2,1)S(1)}) custom-call(bf16[2,128,256]{2,1,0:T(8,128)(2,1)S(1)} %get-tuple-element.19.refs_0_, bf16[256,1024]{1,0:T(8,128)(2,1)S(1)} %get-tuple-element.20.refs_1_, ...), custom_call_target="tpu_custom_call" | custom-call | flops 738197504 | bytes 3670016 | tf_op jit(solution)/shard_map/pallas_call | solution.py:276
  27.8 0.0 copy-start.2
  27.8 0.8 %copy-done.2 = bf16[256,1024]{1,0:T(8,128)(2,1)} copy-done((bf16[256,1024]{1,0:T(8,128)(2,1)}, bf16[256,1024]{1,0:T(8,128)(2,1)S(1)}, u32[]{:S(2)}) %copy-start.2) | copy-done | bytes 524312
  28.6 0.0 copy-start.4
  28.6 0.8 %copy-done.4 = bf16[256,1024]{1,0:T(8,128)(2,1)} copy-done((bf16[256,1024]{1,0:T(8,128)(2,1)}, bf16[256,1024]{1,0:T(8,128)(2,1)S(1)}, u32[]{:S(2)}) %copy-start.4) | copy-done | bytes 524312
  29.4 3.8 %collective-permute-start.2 = (bf16[128,1024]{1,0:T(8,128)(2,1)S(1)}, bf16[128,1024]{1,0:T(8,128)(2,1)}, u32[]{:S(2)}, u32[]{:S(2)}) collective-permute-start(bf16[128,1024]{1,0:T(8,128)(2,1)S(1)} %get-tuple-element.25), channel_id=1, source_target_pairs={{0,16},{8,24},{1,17},{9,25},{2,18},{10,26},{3,19},{11,27},{4,20},{... | collective-permute-start | bytes 786440 | tf_op jit(solution)/shard_map/ppermute | solution.py:219
  33.2 2.1 %collective-permute-start.3 = (bf16[256,1024]{1,0:T(8,128)(2,1)}, bf16[256,1024]{1,0:T(8,128)(2,1)}, u32[]{:S(2)}, u32[]{:S(2)}) collective-permute-start(bf16[256,1024]{1,0:T(8,128)(2,1)} %get-tuple-element.26), channel_id=1, source_target_pairs={{0,16},{8,24},{1,17},{9,25},{2,18},{10,26},{3,19},{11,27},{4,20},{... | collective-permute-start | bytes 1572872 | tf_op jit(solution)/shard_map/ppermute | solution.py:219
  35.3 0.5 collective-permute-done.2
  35.8 6.3 %all-to-all-start.2 = ((bf16[8,16,1024]{2,1,0:T(8,128)(2,1)}), bf16[8,16,1024]{2,1,0:T(8,128)(2,1)S(1)}, u32[]{:S(2)}, u32[]{:S(2)}) async-start(bf16[8,16,1024]{2,1,0:T(8,128)(2,1)} %bitcast.5), calls=%async_computation.2 | async-start | bytes 524288 | tf_op jit(solution)/shard_map/all_to_all | solution.py:226
  42.2 3.6 %collective-permute-done.3.refs_6_ = bf16[256,1024]{1,0:T(8,128)(2,1)} collective-permute-done((bf16[256,1024]{1,0:T(8,128)(2,1)}, bf16[256,1024]{1,0:T(8,128)(2,1)}, u32[]{:S(2)}, u32[]{:S(2)}) %collective-permute-start.3) | collective-permute-done | bytes 524320 | tf_op jit(solution)/shard_map/ppermute | solution.py:219
  45.8 0.5 all-to-all-done.2
  46.3 0.0 copy-start.1
  46.3 1.6 %copy-done.1 = bf16[1024,1024]{1,0:T(8,128)(2,1)S(1)} copy-done((bf16[1024,1024]{1,0:T(8,128)(2,1)S(1)}, bf16[1024,1024]{1,0:T(8,128)(2,1)}, u32[]{:S(2)}) %copy-start.1) | copy-done | bytes 2097176
  47.9 0.0 copy-start.3
  47.9 0.0 copy-start.5
  47.9 2.2 %shard_map.58 = (bf16[256,1024]{1,0:T(8,128)(2,1)S(1)}, bf16[128,1024]{1,0:T(8,128)(2,1)S(1)}) custom-call(bf16[2,128,256]{2,1,0:T(8,128)(2,1)S(1)} %get-tuple-element.19.refs_0_, bf16[256,1024]{1,0:T(8,128)(2,1)S(1)} %get-tuple-element.20.refs_1_, bf16[128,256]{1,0:T(8,128)(2,1)S(1)} %get-tuple-element.21.refs_2_, bf16[128,1024]{1,0:T(8,128)(2,1)S(1)} %bitcast.9, ...), custom_call_target="tpu_custom_call" | custom-call | flops 738197504 | bytes 3670016 | tf_op jit(solution)/shard_map/pallas_call | solution.py:276
  50.1 10.8 %all_to_all.46 = bf16[8,16,1024]{2,1,0:T(8,128)(2,1)S(1)} all-to-all(bf16[8,16,1024]{2,1,0:T(8,128)(2,1)S(1)} %bitcast.14), channel_id=1, replica_groups={{5,0,2,3,6,1,4,7},{13,8,10,11,14,9,12,15},{21,16,18,19,22,17,20,23},{29..., dimensions={0} | all-to-all | bytes 524288 | tf_op jit(solution)/shard_map/all_to_all | solution.py:226
  60.9 0.0 copy-done.3
  60.9 0.0 copy-done.5
  60.9 1.0 %shard_map.59 = (bf16[256,1024]{1,0:T(8,128)(2,1)S(1)}, bf16[256,1024]{1,0:T(8,128)(2,1)S(1)}) custom-call(bf16[2,128,256]{2,1,0:T(8,128)(2,1)S(1)} %get-tuple-element.19.refs_0_, bf16[256,1024]{1,0:T(8,128)(2,1)S(1)} %get-tuple-element.20.refs_1_, bf16[128,256]{1,0:T(8,128)(2,1)S(1)} %get-tuple-element.21.refs_2_, bf16[128,1024]{1,0:T(8,128)(2,1)S(1)} %bitcast.10, ...), custom_call_target="tpu_custom_call" | custom-call | flops 738197504 | bytes 3670016 | tf_op jit(solution)/shard_map/pallas_call | solution.py:276
  61.9 5.8 %collective-permute-start.4 = (bf16[256,1024]{1,0:T(8,128)(2,1)S(1)}, bf16[256,1024]{1,0:T(8,128)(2,1)S(1)}, u32[]{:S(2)}, u32[]{:S(2)}) collective-permute-start(bf16[256,1024]{1,0:T(8,128)(2,1)S(1)} %get-tuple-element.31), channel_id=1, source_target_pairs={{0,8},{8,0},{16,24},{24,16},{1,9},{9,1},{17,25},{25,17},{2,10},{10... | collective-permute-start | bytes 1572872 | tf_op jit(solution)/shard_map/ppermute | solution.py:215
  67.8 0.8 %shard_map.60.refs_1_ = bf16[1,2,256,1024]{3,2,1,0:T(8,128)(2,1)} custom-call(bf16[256,1024]{1,0:T(8,128)(2,1)S(1)} %get-tuple-element.32.refs_0_), custom_call_target="tpu_custom_call" | custom-call | bytes 1048576 | tf_op jit(solution)/shard_map/pallas_call | solution.py:309
  68.6 0.7 %collective-permute-done.4.refs_0_ = bf16[256,1024]{1,0:T(8,128)(2,1)S(1)} collective-permute-done((bf16[256,1024]{1,0:T(8,128)(2,1)S(1)}, bf16[256,1024]{1,0:T(8,128)(2,1)S(1)}, u32[]{:S(2)}, u32[]{:S(2)}) %collective-permute-start.4) | collective-permute-done | bytes 524320 | tf_op jit(solution)/shard_map/ppermute | solution.py:215
  69.3 0.8 %shard_map.61 = bf16[1,2,256,1024]{3,2,1,0:T(8,128)(2,1)} custom-call(bf16[256,1024]{1,0:T(8,128)(2,1)S(1)} %collective-permute-done.4.refs_0_, bf16[1,2,256,1024]{3,2,1,0:T(8,128)(2,1)} %shard_map.60.refs_1_), custom_call_target="tpu_custom_call", output_to_operand_aliasing={{}: (1, {})} | custom-call | tf_op jit(solution)/shard_map/pallas_call | solution.py:319
Async XLA Ops:
  0.0 16.4 %collective-permute-start.1 = (bf16[1024,1024]{1,0:T(8,128)(2,1)}, bf16[1024,1024]{1,0:T(8,128)(2,1)S(1)}, u32[]{:S(2)}, u32[]{:S(2)}) collective-permute-start(bf16[1024,1024]{1,0:T(8,128)(2,1)} %bitcast.16), channel_id=1, source_target_pairs={{0,8},{8,0},{16,24},{24,16},{1,9},{9,1},{17,25},{25,17},{2,10},{10... | collective-permute-start | bytes 6291464 | tf_op jit(solution)/shard_map/ppermute | solution.py:215
  0.0 16.4 %collective-permute-start = (bf16[1024,1024]{1,0:T(8,128)(2,1)}, bf16[1024,1024]{1,0:T(8,128)(2,1)S(1)}, u32[]{:S(2)}, u32[]{:S(2)}) collective-permute-start(bf16[1024,1024]{1,0:T(8,128)(2,1)} %bitcast.17), channel_id=1, source_target_pairs={{0,0},{8,8},{16,16},{24,24},{1,1},{9,9},{17,17},{25,25},{2,2},{10,... | collective-permute-start | bytes 6291464 | tf_op jit(solution)/shard_map/ppermute | solution.py:215
  16.4 9.4 %copy-start = (bf16[1024,1024]{1,0:T(8,128)(2,1)}, bf16[1024,1024]{1,0:T(8,128)(2,1)S(1)}, u32[]{:S(2)}) copy-start(bf16[1024,1024]{1,0:T(8,128)(2,1)S(1)} %collective-permute-done.refs_4_) | copy-start | bytes 6291460
  27.8 0.8 %copy-start.2 = (bf16[256,1024]{1,0:T(8,128)(2,1)}, bf16[256,1024]{1,0:T(8,128)(2,1)S(1)}, u32[]{:S(2)}) copy-start(bf16[256,1024]{1,0:T(8,128)(2,1)S(1)} %get-tuple-element.29.refs_7_) | copy-start | bytes 1572868
  28.6 0.8 %copy-start.4 = (bf16[256,1024]{1,0:T(8,128)(2,1)}, bf16[256,1024]{1,0:T(8,128)(2,1)S(1)}, u32[]{:S(2)}) copy-start(bf16[256,1024]{1,0:T(8,128)(2,1)S(1)} %get-tuple-element.30.refs_8_) | copy-start | bytes 1572868
  29.4 6.4 %collective-permute-start.2 = (bf16[128,1024]{1,0:T(8,128)(2,1)S(1)}, bf16[128,1024]{1,0:T(8,128)(2,1)}, u32[]{:S(2)}, u32[]{:S(2)}) collective-permute-start(bf16[128,1024]{1,0:T(8,128)(2,1)S(1)} %get-tuple-element.25), channel_id=1, source_target_pairs={{0,16},{8,24},{1,17},{9,25},{2,18},{10,26},{3,19},{11,27},{4,20},{... | collective-permute-start | bytes 786440 | tf_op jit(solution)/shard_map/ppermute | solution.py:219
  33.2 12.6 %collective-permute-start.3 = (bf16[256,1024]{1,0:T(8,128)(2,1)}, bf16[256,1024]{1,0:T(8,128)(2,1)}, u32[]{:S(2)}, u32[]{:S(2)}) collective-permute-start(bf16[256,1024]{1,0:T(8,128)(2,1)} %get-tuple-element.26), channel_id=1, source_target_pairs={{0,16},{8,24},{1,17},{9,25},{2,18},{10,26},{3,19},{11,27},{4,20},{... | collective-permute-start | bytes 1572872 | tf_op jit(solution)/shard_map/ppermute | solution.py:219
  35.8 10.4 %all-to-all-start.2 = ((bf16[8,16,1024]{2,1,0:T(8,128)(2,1)}), bf16[8,16,1024]{2,1,0:T(8,128)(2,1)S(1)}, u32[]{:S(2)}, u32[]{:S(2)}) async-start(bf16[8,16,1024]{2,1,0:T(8,128)(2,1)} %bitcast.5), calls=%async_computation.2 | async-start | bytes 524288 | tf_op jit(solution)/shard_map/all_to_all | solution.py:226
  46.3 1.6 %copy-start.1 = (bf16[1024,1024]{1,0:T(8,128)(2,1)S(1)}, bf16[1024,1024]{1,0:T(8,128)(2,1)}, u32[]{:S(2)}) copy-start(bf16[1024,1024]{1,0:T(8,128)(2,1)} %copy-done) | copy-start | bytes 6291460
  47.9 13.0 %copy-start.3 = (bf16[256,1024]{1,0:T(8,128)(2,1)S(1)}, bf16[256,1024]{1,0:T(8,128)(2,1)}, u32[]{:S(2)}) copy-start(bf16[256,1024]{1,0:T(8,128)(2,1)} %copy-done.2) | copy-start | bytes 1572868
  47.9 13.0 %copy-start.5 = (bf16[256,1024]{1,0:T(8,128)(2,1)S(1)}, bf16[256,1024]{1,0:T(8,128)(2,1)}, u32[]{:S(2)}) copy-start(bf16[256,1024]{1,0:T(8,128)(2,1)} %copy-done.4) | copy-start | bytes 1572868
  61.9 7.4 %collective-permute-start.4 = (bf16[256,1024]{1,0:T(8,128)(2,1)S(1)}, bf16[256,1024]{1,0:T(8,128)(2,1)S(1)}, u32[]{:S(2)}, u32[]{:S(2)}) collective-permute-start(bf16[256,1024]{1,0:T(8,128)(2,1)S(1)} %get-tuple-element.31), channel_id=1, source_target_pairs={{0,8},{8,0},{16,24},{24,16},{1,9},{9,1},{17,25},{25,17},{2,10},{10... | collective-permute-start | bytes 1572872 | tf_op jit(solution)/shard_map/ppermute | solution.py:215

commit v5 on v4

--- a/solution.py
+++ b/solution.py
@@ -74,10 +74,12 @@
     block_hbm,
     init_hbm,
     tiles_hbm,
+    weight_hbm,
     out_ref,
     pick_ref,
     mix_ref,
     init_ref,
+    weight_ref,
     send_ref,
     block_ref,
     tiles_ref,
@@ -95,6 +97,15 @@
             ]
         )
     ]
+    count = sems.shape[0] - len(copies)
+    part = weight_ref.shape[0] // count
+    for i in range(count):
+        rows = pl.ds(i * part, part)
+        copies.append(
+            pltpu.make_async_copy(
+                weight_hbm.at[0, rows], weight_ref.at[rows], sems.at[4 + i]
+            )
+        )
     for copy in copies:
         copy.start()
     copies[0].wait()
@@ -117,6 +128,8 @@
             far = far_t if far is None else far + far_t
         far = jnp.dot(far.astype(bf16), arrival, preferred_element_type=f32)
         mix_ref[r] = jnp.concatenate([own, far], axis=1).astype(bf16)
+    for copy in copies[4:]:
+        copy.wait()
 
 
 def layer_kernel(group, stage, step, has_current, has_old, has_x, *refs):
@@ -162,8 +175,10 @@
                 pick_ref[...], x_ref[...], preferred_element_type=f32
             ).astype(bf16)
 
+    active = section // group == stage
     for shift in range(group):
-        pl.when((member + shift) % group == step)(functools.partial(body, weights[shift]))
+        needed = active & ((member + shift) % group == step)
+        pl.when(needed)(functools.partial(body, weights[shift]))
 
     if end:
         layers = earlier + ([current_ref] if group > 1 else []) + [x_ref]
@@ -233,6 +248,7 @@
         )
 
     def first():
+        chunks = 4
         return call(
             functools.partial(first_kernel, group),
             [
@@ -240,19 +256,20 @@
                 (sent, rows),
                 (row_blocks, side, 2 * side),
                 (rows, width),
+                layer_weight.shape[1:],
             ],
-            [HBM] * 4,
-            [VMEM] * 4,
+            [HBM] * 5,
+            [VMEM] * 5,
             [
                 pltpu.VMEM(send_rows.shape[2:], jnp.int32),
                 pltpu.SMEM((row_blocks, tiles), jnp.int32),
                 pltpu.VMEM(tile_values.shape[2:], bf16),
-                pltpu.SemaphoreType.DMA((4,)),
+                pltpu.SemaphoreType.DMA((4 + chunks,)),
             ],
         )(
             *[
                 pltpu.with_memory_space_constraint(x, pltpu.HBM)
-                for x in (send_rows, tile_column, initial_feat, tile_values)
+                for x in (send_rows, tile_column, initial_feat, tile_values, layer_weight)
             ]
         )
 
@@ -284,8 +301,8 @@
             cost=pl.CostEstimate(flops=flops, bytes_accessed=moved, transcendentals=0),
         )(*operands)
 
-    outgoing, pick, mix, init = first()
-    weights = [shifted(layer_weight[0], by) for by in range(group)]
+    outgoing, pick, mix, init, own_weight = first()
+    weights = [own_weight] + [shifted(own_weight, by) for by in range(1, group)]
     boundary = exchanged(outgoing)
     shared = [mix, init, pick]
     current = None

time: 71.1 us -> 67.7 us (0.952)
  the two profiles are of different devices: /device:TPU:1 before, /device:TPU:7 now
where the time goes in v5:
time: 67.7 us; the launch traced here: 67.2 us
  blocking collectives  30.5 us (45%)
  starting transfers between devices  14.3 us (21%)
  waiting for transfers between devices  11.6 us (17%)
  Pallas kernels  7.56 us (11%)
  local copies, waits for them, and re-layouts  3.23 us (5%)
    all_to_all x3, blocking collectives, exchanged(): lax.all_to_all(x, ('section', 'dom'), split_axis=0, concat_axis=0, axis_i...  30.5 us
    ppermute x2, waiting for transfers between devices, crossed(): return lax.ppermute(x, 'section', pairs)  10.9 us
    ppermute x2, starting transfers between devices, shifted(): return lax.ppermute(x, 'section', pairs)  6.12 us
    all_to_all x1, starting transfers between devices, exchanged(): lax.all_to_all(x, ('section', 'dom'), split_axis=0, concat_axis=0, axis_i...  5.63 us
    pallas_call x4, Pallas kernels, layer(): call(functools.partial(layer_kernel, group, stage, step, has_current, end...  4.13 us
    unnamed x12, local copies, waits for them, and re-layouts  3.23 us
    ppermute x2, starting transfers between devices, crossed(): return lax.ppermute(x, 'section', pairs)  2.57 us
    pallas_call x1, Pallas kernels, first(): call(functools.partial(first_kernel, group), [(sent, width), (sent, rows)...  1.84 us
  transfers between devices with their start and end apart: 5, of which 3 were waited for; matrix products, arithmetic and copies ran while one was open for 0% of the time, Pallas kernels for 1%

profile of v5, /device:TPU:7, one launch (start us, length us, event | category | flops | bytes accessed | tf_op | source)
XLA Modules:
  0.0 67.2 jit_solution(8935799329624926654)
XLA Ops:
  0.0 1.8 %shard_map.55 = (bf16[128,1024]{1,0:T(8,128)(2,1)S(1)}, bf16[128,256]{1,0:T(8,128)(2,1)S(1)}, bf16[2,128,256]{2,1,0:T(8,128)(2,1)S(1)}, bf16[256,1024]{1,0:T(8,128)(2,1)S(1)}, bf16[1024,1024]{1,0:T(8,128)(2,1)S(1)}) custom-call(s32[1,2,8,16]{3,2,1,0:T(8,128)} %send_hbm.1, s32[1,2,2,4]{3,2,1,0:T(2,128)} %block_hbm.1, bf16[2,256,1024]{2,1,0:T(8,128)(2,1)} %init_hbm.1, ...), custom_call_target="tpu_custom_call" | custom-call | tf_op jit(solution)/shard_map/pallas_call | solution.py:252
  1.8 0.7 %collective-permute-start = (bf16[1024,1024]{1,0:T(8,128)(2,1)S(1)}, bf16[1024,1024]{1,0:T(8,128)(2,1)S(1)}, u32[]{:S(2)}, u32[]{:S(2)}) collective-permute-start(bf16[1024,1024]{1,0:T(8,128)(2,1)S(1)} %get-tuple-element.24.refs_4_), channel_id=1, source_target_pairs={{0,8},{8,0},{16,24},{24,16},{1,9},{9,1},{17,25},{25,17},{2,10},{10... | collective-permute-start | bytes 6291464 | tf_op jit(solution)/shard_map/ppermute | solution.py:230
  2.6 10.7 %all_to_all.44 = bf16[8,16,1024]{2,1,0:T(8,128)(2,1)S(1)} all-to-all(bf16[8,16,1024]{2,1,0:T(8,128)(2,1)S(1)} %bitcast.12), channel_id=1, replica_groups={{5,0,2,3,6,1,4,7},{13,8,10,11,14,9,12,15},{21,16,18,19,22,17,20,23},{29..., dimensions={0} | all-to-all | bytes 524288 | tf_op jit(solution)/shard_map/all_to_all | solution.py:241
  13.3 0.0 collective-permute-done.refs_5_
  13.3 0.0 copy-start
  13.3 9.6 %all_to_all.45 = bf16[8,16,1024]{2,1,0:T(8,128)(2,1)S(1)} all-to-all(bf16[8,16,1024]{2,1,0:T(8,128)(2,1)S(1)} %bitcast.14), channel_id=1, replica_groups={{5,0,2,3,6,1,4,7},{13,8,10,11,14,9,12,15},{21,16,18,19,22,17,20,23},{29..., dimensions={0} | all-to-all | bytes 524288 | tf_op jit(solution)/shard_map/all_to_all | solution.py:241
  22.9 0.0 copy-done
  22.9 0.9 %shard_map.57 = (bf16[256,1024]{1,0:T(8,128)(2,1)}, bf16[128,1024]{1,0:T(8,128)(2,1)S(1)}, bf16[256,1024]{1,0:T(8,128)(2,1)S(1)}, bf16[256,1024]{1,0:T(8,128)(2,1)S(1)}) custom-call(bf16[2,128,256]{2,1,0:T(8,128)(2,1)S(1)} %get-tuple-element.20.refs_0_, bf16[256,1024]{1,0:T(8,128)(2,1)S(1)} %get-tuple-element.21.refs_1_, ...), custom_call_target="tpu_custom_call" | custom-call | flops 738197504 | bytes 3670016 | tf_op jit(solution)/shard_map/pallas_call | solution.py:293
  23.8 0.0 copy-start.2
  23.8 0.8 %copy-done.2 = bf16[256,1024]{1,0:T(8,128)(2,1)} copy-done((bf16[256,1024]{1,0:T(8,128)(2,1)}, bf16[256,1024]{1,0:T(8,128)(2,1)S(1)}, u32[]{:S(2)}) %copy-start.2) | copy-done | bytes 524312
  24.6 0.0 copy-start.4
  24.6 0.8 %copy-done.4 = bf16[256,1024]{1,0:T(8,128)(2,1)} copy-done((bf16[256,1024]{1,0:T(8,128)(2,1)}, bf16[256,1024]{1,0:T(8,128)(2,1)S(1)}, u32[]{:S(2)}) %copy-start.4) | copy-done | bytes 524312
  25.4 1.3 %collective-permute-start.1 = (bf16[128,1024]{1,0:T(8,128)(2,1)S(1)}, bf16[128,1024]{1,0:T(8,128)(2,1)}, u32[]{:S(2)}, u32[]{:S(2)}) collective-permute-start(bf16[128,1024]{1,0:T(8,128)(2,1)S(1)} %get-tuple-element.27), channel_id=1, source_target_pairs={{0,16},{8,24},{1,17},{9,25},{2,18},{10,26},{3,19},{11,27},{4,20},{... | collective-permute-start | bytes 786440 | tf_op jit(solution)/shard_map/ppermute | solution.py:234
  26.7 1.3 %collective-permute-start.2 = (bf16[256,1024]{1,0:T(8,128)(2,1)}, bf16[256,1024]{1,0:T(8,128)(2,1)}, u32[]{:S(2)}, u32[]{:S(2)}) collective-permute-start(bf16[256,1024]{1,0:T(8,128)(2,1)} %get-tuple-element.28), channel_id=1, source_target_pairs={{0,16},{8,24},{1,17},{9,25},{2,18},{10,26},{3,19},{11,27},{4,20},{... | collective-permute-start | bytes 1572872 | tf_op jit(solution)/shard_map/ppermute | solution.py:234
  28.0 5.0 %collective-permute-done.1 = bf16[128,1024]{1,0:T(8,128)(2,1)} collective-permute-done((bf16[128,1024]{1,0:T(8,128)(2,1)S(1)}, bf16[128,1024]{1,0:T(8,128)(2,1)}, u32[]{:S(2)}, u32[]{:S(2)}) %collective-permute-start.1) | collective-permute-done | bytes 262176 | tf_op jit(solution)/shard_map/ppermute | solution.py:234
  33.0 5.6 %all-to-all-start.2 = ((bf16[8,16,1024]{2,1,0:T(8,128)(2,1)}), bf16[8,16,1024]{2,1,0:T(8,128)(2,1)S(1)}, u32[]{:S(2)}, u32[]{:S(2)}) async-start(bf16[8,16,1024]{2,1,0:T(8,128)(2,1)} %bitcast.4), calls=%async_computation.2 | async-start | bytes 524288 | tf_op jit(solution)/shard_map/all_to_all | solution.py:241
  38.6 5.9 %collective-permute-done.2.refs_6_ = bf16[256,1024]{1,0:T(8,128)(2,1)} collective-permute-done((bf16[256,1024]{1,0:T(8,128)(2,1)}, bf16[256,1024]{1,0:T(8,128)(2,1)}, u32[]{:S(2)}, u32[]{:S(2)}) %collective-permute-start.2) | collective-permute-done | bytes 524320 | tf_op jit(solution)/shard_map/ppermute | solution.py:234
  44.5 0.0 all-to-all-done.2
  44.5 0.0 copy-start.1
  44.5 1.6 %copy-done.1 = bf16[1024,1024]{1,0:T(8,128)(2,1)S(1)} copy-done((bf16[1024,1024]{1,0:T(8,128)(2,1)S(1)}, bf16[1024,1024]{1,0:T(8,128)(2,1)}, u32[]{:S(2)}) %copy-start.1) | copy-done | bytes 2097176
  46.1 0.0 copy-start.3
  46.1 0.0 copy-start.5
  46.1 2.2 %shard_map.58 = (bf16[256,1024]{1,0:T(8,128)(2,1)S(1)}, bf16[128,1024]{1,0:T(8,128)(2,1)S(1)}) custom-call(bf16[2,128,256]{2,1,0:T(8,128)(2,1)S(1)} %get-tuple-element.20.refs_0_, bf16[256,1024]{1,0:T(8,128)(2,1)S(1)} %get-tuple-element.21.refs_1_, bf16[128,256]{1,0:T(8,128)(2,1)S(1)} %get-tuple-element.22.refs_2_, bf16[128,1024]{1,0:T(8,128)(2,1)S(1)} %bitcast.8, ...), custom_call_target="tpu_custom_call" | custom-call | flops 738197504 | bytes 3670016 | tf_op jit(solution)/shard_map/pallas_call | solution.py:293
  48.3 10.2 %all_to_all.46 = bf16[8,16,1024]{2,1,0:T(8,128)(2,1)S(1)} all-to-all(bf16[8,16,1024]{2,1,0:T(8,128)(2,1)S(1)} %bitcast.13), channel_id=1, replica_groups={{5,0,2,3,6,1,4,7},{13,8,10,11,14,9,12,15},{21,16,18,19,22,17,20,23},{29..., dimensions={0} | all-to-all | bytes 524288 | tf_op jit(solution)/shard_map/all_to_all | solution.py:241
  58.5 0.0 copy-done.3
  58.5 0.0 copy-done.5
  58.5 1.0 %shard_map.59 = (bf16[256,1024]{1,0:T(8,128)(2,1)S(1)}, bf16[256,1024]{1,0:T(8,128)(2,1)S(1)}) custom-call(bf16[2,128,256]{2,1,0:T(8,128)(2,1)S(1)} %get-tuple-element.20.refs_0_, bf16[256,1024]{1,0:T(8,128)(2,1)S(1)} %get-tuple-element.21.refs_1_, bf16[128,256]{1,0:T(8,128)(2,1)S(1)} %get-tuple-element.22.refs_2_, bf16[128,1024]{1,0:T(8,128)(2,1)S(1)} %bitcast.9, ...), custom_call_target="tpu_custom_call" | custom-call | flops 738197504 | bytes 3670016 | tf_op jit(solution)/shard_map/pallas_call | solution.py:293
  59.5 5.4 %collective-permute-start.3 = (bf16[256,1024]{1,0:T(8,128)(2,1)S(1)}, bf16[256,1024]{1,0:T(8,128)(2,1)S(1)}, u32[]{:S(2)}, u32[]{:S(2)}) collective-permute-start(bf16[256,1024]{1,0:T(8,128)(2,1)S(1)} %get-tuple-element.33), channel_id=1, source_target_pairs={{0,8},{8,0},{16,24},{24,16},{1,9},{9,1},{17,25},{25,17},{2,10},{10... | collective-permute-start | bytes 1572872 | tf_op jit(solution)/shard_map/ppermute | solution.py:230
  64.9 0.8 %shard_map.60.refs_1_ = bf16[1,2,256,1024]{3,2,1,0:T(8,128)(2,1)} custom-call(bf16[256,1024]{1,0:T(8,128)(2,1)S(1)} %get-tuple-element.34.refs_0_), custom_call_target="tpu_custom_call" | custom-call | bytes 1048576 | tf_op jit(solution)/shard_map/pallas_call | solution.py:326
  65.7 0.7 %collective-permute-done.3.refs_0_ = bf16[256,1024]{1,0:T(8,128)(2,1)S(1)} collective-permute-done((bf16[256,1024]{1,0:T(8,128)(2,1)S(1)}, bf16[256,1024]{1,0:T(8,128)(2,1)S(1)}, u32[]{:S(2)}, u32[]{:S(2)}) %collective-permute-start.3) | collective-permute-done | bytes 524320 | tf_op jit(solution)/shard_map/ppermute | solution.py:230
  66.4 0.8 %shard_map.61 = bf16[1,2,256,1024]{3,2,1,0:T(8,128)(2,1)} custom-call(bf16[256,1024]{1,0:T(8,128)(2,1)S(1)} %collective-permute-done.3.refs_0_, bf16[1,2,256,1024]{3,2,1,0:T(8,128)(2,1)} %shard_map.60.refs_1_), custom_call_target="tpu_custom_call", output_to_operand_aliasing={{}: (1, {})} | custom-call | tf_op jit(solution)/shard_map/pallas_call | solution.py:336
  (1 shorter events, 0.0 us)
Async XLA Ops:
  1.8 11.5 %collective-permute-start = (bf16[1024,1024]{1,0:T(8,128)(2,1)S(1)}, bf16[1024,1024]{1,0:T(8,128)(2,1)S(1)}, u32[]{:S(2)}, u32[]{:S(2)}) collective-permute-start(bf16[1024,1024]{1,0:T(8,128)(2,1)S(1)} %get-tuple-element.24.refs_4_), channel_id=1, source_target_pairs={{0,8},{8,0},{16,24},{24,16},{1,9},{9,1},{17,25},{25,17},{2,10},{10... | collective-permute-start | bytes 6291464 | tf_op jit(solution)/shard_map/ppermute | solution.py:230
  13.3 9.6 %copy-start = (bf16[1024,1024]{1,0:T(8,128)(2,1)}, bf16[1024,1024]{1,0:T(8,128)(2,1)S(1)}, u32[]{:S(2)}) copy-start(bf16[1024,1024]{1,0:T(8,128)(2,1)S(1)} %collective-permute-done.refs_5_) | copy-start | bytes 6291460
  23.8 0.8 %copy-start.2 = (bf16[256,1024]{1,0:T(8,128)(2,1)}, bf16[256,1024]{1,0:T(8,128)(2,1)S(1)}, u32[]{:S(2)}) copy-start(bf16[256,1024]{1,0:T(8,128)(2,1)S(1)} %get-tuple-element.31.refs_7_) | copy-start | bytes 1572868
  24.6 0.8 %copy-start.4 = (bf16[256,1024]{1,0:T(8,128)(2,1)}, bf16[256,1024]{1,0:T(8,128)(2,1)S(1)}, u32[]{:S(2)}) copy-start(bf16[256,1024]{1,0:T(8,128)(2,1)S(1)} %get-tuple-element.32.refs_8_) | copy-start | bytes 1572868
  25.4 7.6 %collective-permute-start.1 = (bf16[128,1024]{1,0:T(8,128)(2,1)S(1)}, bf16[128,1024]{1,0:T(8,128)(2,1)}, u32[]{:S(2)}, u32[]{:S(2)}) collective-permute-start(bf16[128,1024]{1,0:T(8,128)(2,1)S(1)} %get-tuple-element.27), channel_id=1, source_target_pairs={{0,16},{8,24},{1,17},{9,25},{2,18},{10,26},{3,19},{11,27},{4,20},{... | collective-permute-start | bytes 786440 | tf_op jit(solution)/shard_map/ppermute | solution.py:234
  26.7 17.8 %collective-permute-start.2 = (bf16[256,1024]{1,0:T(8,128)(2,1)}, bf16[256,1024]{1,0:T(8,128)(2,1)}, u32[]{:S(2)}, u32[]{:S(2)}) collective-permute-start(bf16[256,1024]{1,0:T(8,128)(2,1)} %get-tuple-element.28), channel_id=1, source_target_pairs={{0,16},{8,24},{1,17},{9,25},{2,18},{10,26},{3,19},{11,27},{4,20},{... | collective-permute-start | bytes 1572872 | tf_op jit(solution)/shard_map/ppermute | solution.py:234
  33.0 11.5 %all-to-all-start.2 = ((bf16[8,16,1024]{2,1,0:T(8,128)(2,1)}), bf16[8,16,1024]{2,1,0:T(8,128)(2,1)S(1)}, u32[]{:S(2)}, u32[]{:S(2)}) async-start(bf16[8,16,1024]{2,1,0:T(8,128)(2,1)} %bitcast.4), calls=%async_computation.2 | async-start | bytes 524288 | tf_op jit(solution)/shard_map/all_to_all | solution.py:241
  44.5 1.6 %copy-start.1 = (bf16[1024,1024]{1,0:T(8,128)(2,1)S(1)}, bf16[1024,1024]{1,0:T(8,128)(2,1)}, u32[]{:S(2)}) copy-start(bf16[1024,1024]{1,0:T(8,128)(2,1)} %copy-done) | copy-start | bytes 6291460
  46.1 12.4 %copy-start.3 = (bf16[256,1024]{1,0:T(8,128)(2,1)S(1)}, bf16[256,1024]{1,0:T(8,128)(2,1)}, u32[]{:S(2)}) copy-start(bf16[256,1024]{1,0:T(8,128)(2,1)} %copy-done.2) | copy-start | bytes 1572868
  46.1 12.4 %copy-start.5 = (bf16[256,1024]{1,0:T(8,128)(2,1)S(1)}, bf16[256,1024]{1,0:T(8,128)(2,1)}, u32[]{:S(2)}) copy-start(bf16[256,1024]{1,0:T(8,128)(2,1)} %copy-done.4) | copy-start | bytes 1572868
  59.5 6.9 %collective-permute-start.3 = (bf16[256,1024]{1,0:T(8,128)(2,1)S(1)}, bf16[256,1024]{1,0:T(8,128)(2,1)S(1)}, u32[]{:S(2)}, u32[]{:S(2)}) collective-permute-start(bf16[256,1024]{1,0:T(8,128)(2,1)S(1)} %get-tuple-element.33), channel_id=1, source_target_pairs={{0,8},{8,0},{16,24},{24,16},{1,9},{9,1},{17,25},{25,17},{2,10},{10... | collective-permute-start | bytes 1572872 | tf_op jit(solution)/shard_map/ppermute | solution.py:230

commit v6 on v5

--- a/solution.py
+++ b/solution.py
@@ -40,6 +40,10 @@
     for i, value in enumerate(table):
         result = jnp.where(index == i, value, result)
     return result
+
+
+def batch_of(section, group):
+    return (section % group + section // group) % group
 
 
 def pick_matrix(send, rows):
@@ -85,7 +89,7 @@
     tiles_ref,
     sems,
 ):
-    batch = lax.axis_index("section") % group
+    batch = batch_of(lax.axis_index("section"), group)
     copies = [
         pltpu.make_async_copy(source, target, sems.at[i])
         for i, (source, target) in enumerate(
@@ -206,9 +210,9 @@
 def write_kernel(group, shifts, *refs):
     pieces = refs[: len(shifts)]
     target, sems = refs[-2:]
-    member = lax.axis_index("section") % group
+    batch = batch_of(lax.axis_index("section"), group)
     copies = [
-        pltpu.make_async_copy(piece, target.at[0, (member + by) % group], sems.at[i])
+        pltpu.make_async_copy(piece, target.at[0, (batch + by) % group], sems.at[i])
         for i, (by, piece) in enumerate(zip(shifts, pieces))
     ]
     for copy in copies:
@@ -230,7 +234,9 @@
         return lax.ppermute(x, "section", pairs)
 
     def crossed(x):
-        pairs = [(s, s + group) for s in range(section_count - group)]
+        pairs = [
+            (s, (s // group + 1) * group + (s - 1) % group) for s in range(section_count - group)
+        ]
         return lax.ppermute(x, "section", pairs)
 
     parts = lax.axis_size("dom")

time: 67.7 us -> 70.1 us (1.035)
  the two profiles are of different devices: /device:TPU:7 before, /device:TPU:5 now
where the time goes in v6:
time: 70.1 us; the launch traced here: 69.6 us
  blocking collectives  29.7 us (42%)
  waiting for transfers between devices  18.7 us (27%)
  starting transfers between devices  10.4 us (15%)
  Pallas kernels  7.56 us (11%)
  local copies, waits for them, and re-layouts  3.23 us (5%)
    all_to_all x3, blocking collectives, exchanged(): lax.all_to_all(x, ('section', 'dom'), split_axis=0, concat_axis=0, axis_i...  29.7 us
    ppermute x2, waiting for transfers between devices, crossed(): return lax.ppermute(x, 'section', pairs)  17.8 us
    all_to_all x1, starting transfers between devices, exchanged(): lax.all_to_all(x, ('section', 'dom'), split_axis=0, concat_axis=0, axis_i...  4.54 us
    pallas_call x4, Pallas kernels, layer(): call(functools.partial(layer_kernel, group, stage, step, has_current, end...  4.13 us
    ppermute x2, starting transfers between devices, shifted(): return lax.ppermute(x, 'section', pairs)  3.32 us
    unnamed x12, local copies, waits for them, and re-layouts  3.23 us
    ppermute x2, starting transfers between devices, crossed(): return lax.ppermute(x, 'section', pairs)  2.57 us
    pallas_call x1, Pallas kernels, first(): call(functools.partial(first_kernel, group), [(sent, width), (sent, rows)...  1.84 us
  transfers between devices with their start and end apart: 5, of which 4 were waited for; matrix products, arithmetic and copies ran while one was open for 0% of the time, Pallas kernels for 1%

profile of v6, /device:TPU:5, one launch (start us, length us, event | category | flops | bytes accessed | tf_op | source)
XLA Modules:
  0.0 69.6 jit_solution(9295391489174520297)
XLA Ops:
  0.0 1.8 %shard_map.55 = (bf16[128,1024]{1,0:T(8,128)(2,1)S(1)}, bf16[128,256]{1,0:T(8,128)(2,1)S(1)}, bf16[2,128,256]{2,1,0:T(8,128)(2,1)S(1)}, bf16[256,1024]{1,0:T(8,128)(2,1)S(1)}, bf16[1024,1024]{1,0:T(8,128)(2,1)S(1)}) custom-call(s32[1,2,8,16]{3,2,1,0:T(8,128)} %send_hbm.1, s32[1,2,2,4]{3,2,1,0:T(2,128)} %block_hbm.1, bf16[2,256,1024]{2,1,0:T(8,128)(2,1)} %init_hbm.1, ...), custom_call_target="tpu_custom_call" | custom-call | tf_op jit(solution)/shard_map/pallas_call | solution.py:258
  1.8 0.7 %collective-permute-start = (bf16[1024,1024]{1,0:T(8,128)(2,1)S(1)}, bf16[1024,1024]{1,0:T(8,128)(2,1)S(1)}, u32[]{:S(2)}, u32[]{:S(2)}) collective-permute-start(bf16[1024,1024]{1,0:T(8,128)(2,1)S(1)} %get-tuple-element.24.refs_4_), channel_id=1, source_target_pairs={{0,8},{8,0},{16,24},{24,16},{1,9},{9,1},{17,25},{25,17},{2,10},{10... | collective-permute-start | bytes 6291464 | tf_op jit(solution)/shard_map/ppermute | solution.py:234
  2.6 11.8 %all_to_all.44 = bf16[8,16,1024]{2,1,0:T(8,128)(2,1)S(1)} all-to-all(bf16[8,16,1024]{2,1,0:T(8,128)(2,1)S(1)} %bitcast.12), channel_id=1, replica_groups={{5,0,2,3,6,1,4,7},{13,8,10,11,14,9,12,15},{21,16,18,19,22,17,20,23},{29..., dimensions={0} | all-to-all | bytes 524288 | tf_op jit(solution)/shard_map/all_to_all | solution.py:247
  14.4 0.0 collective-permute-done.refs_5_
  14.4 0.0 copy-start
  14.4 8.2 %all_to_all.45 = bf16[8,16,1024]{2,1,0:T(8,128)(2,1)S(1)} all-to-all(bf16[8,16,1024]{2,1,0:T(8,128)(2,1)S(1)} %bitcast.14), channel_id=1, replica_groups={{5,0,2,3,6,1,4,7},{13,8,10,11,14,9,12,15},{21,16,18,19,22,17,20,23},{29..., dimensions={0} | all-to-all | bytes 524288 | tf_op jit(solution)/shard_map/all_to_all | solution.py:247
  22.5 0.0 copy-done
  22.5 0.9 %shard_map.57 = (bf16[256,1024]{1,0:T(8,128)(2,1)}, bf16[128,1024]{1,0:T(8,128)(2,1)S(1)}, bf16[256,1024]{1,0:T(8,128)(2,1)S(1)}, bf16[256,1024]{1,0:T(8,128)(2,1)S(1)}) custom-call(bf16[2,128,256]{2,1,0:T(8,128)(2,1)S(1)} %get-tuple-element.20.refs_0_, bf16[256,1024]{1,0:T(8,128)(2,1)S(1)} %get-tuple-element.21.refs_1_, ...), custom_call_target="tpu_custom_call" | custom-call | flops 738197504 | bytes 3670016 | tf_op jit(solution)/shard_map/pallas_call | solution.py:299
  23.4 0.0 copy-start.2
  23.4 0.8 %copy-done.2 = bf16[256,1024]{1,0:T(8,128)(2,1)} copy-done((bf16[256,1024]{1,0:T(8,128)(2,1)}, bf16[256,1024]{1,0:T(8,128)(2,1)S(1)}, u32[]{:S(2)}) %copy-start.2) | copy-done | bytes 524312
  24.2 0.0 copy-start.4
  24.2 0.8 %copy-done.4 = bf16[256,1024]{1,0:T(8,128)(2,1)} copy-done((bf16[256,1024]{1,0:T(8,128)(2,1)}, bf16[256,1024]{1,0:T(8,128)(2,1)S(1)}, u32[]{:S(2)}) %copy-start.4) | copy-done | bytes 524312
  25.0 1.3 %collective-permute-start.1 = (bf16[128,1024]{1,0:T(8,128)(2,1)S(1)}, bf16[128,1024]{1,0:T(8,128)(2,1)}, u32[]{:S(2)}, u32[]{:S(2)}) collective-permute-start(bf16[128,1024]{1,0:T(8,128)(2,1)S(1)} %get-tuple-element.27), channel_id=1, source_target_pairs={{0,24},{8,16},{1,25},{9,17},{2,26},{10,18},{3,27},{11,19},{4,28},{... | collective-permute-start | bytes 786440 | tf_op jit(solution)/shard_map/ppermute | solution.py:240
  26.3 1.3 %collective-permute-start.2 = (bf16[256,1024]{1,0:T(8,128)(2,1)}, bf16[256,1024]{1,0:T(8,128)(2,1)}, u32[]{:S(2)}, u32[]{:S(2)}) collective-permute-start(bf16[256,1024]{1,0:T(8,128)(2,1)} %get-tuple-element.28), channel_id=1, source_target_pairs={{0,24},{8,16},{1,25},{9,17},{2,26},{10,18},{3,27},{11,19},{4,28},{... | collective-permute-start | bytes 1572872 | tf_op jit(solution)/shard_map/ppermute | solution.py:240
  27.6 12.0 %collective-permute-done.1 = bf16[128,1024]{1,0:T(8,128)(2,1)} collective-permute-done((bf16[128,1024]{1,0:T(8,128)(2,1)S(1)}, bf16[128,1024]{1,0:T(8,128)(2,1)}, u32[]{:S(2)}, u32[]{:S(2)}) %collective-permute-start.1) | collective-permute-done | bytes 262176 | tf_op jit(solution)/shard_map/ppermute | solution.py:240
  39.7 4.5 %all-to-all-start.2 = ((bf16[8,16,1024]{2,1,0:T(8,128)(2,1)}), bf16[8,16,1024]{2,1,0:T(8,128)(2,1)S(1)}, u32[]{:S(2)}, u32[]{:S(2)}) async-start(bf16[8,16,1024]{2,1,0:T(8,128)(2,1)} %bitcast.4), calls=%async_computation.2 | async-start | bytes 524288 | tf_op jit(solution)/shard_map/all_to_all | solution.py:247
  44.2 5.7 %collective-permute-done.2.refs_6_ = bf16[256,1024]{1,0:T(8,128)(2,1)} collective-permute-done((bf16[256,1024]{1,0:T(8,128)(2,1)}, bf16[256,1024]{1,0:T(8,128)(2,1)}, u32[]{:S(2)}, u32[]{:S(2)}) %collective-permute-start.2) | collective-permute-done | bytes 524320 | tf_op jit(solution)/shard_map/ppermute | solution.py:240
  49.9 0.2 all-to-all-done.2
  50.1 0.0 copy-start.1
  50.1 1.6 %copy-done.1 = bf16[1024,1024]{1,0:T(8,128)(2,1)S(1)} copy-done((bf16[1024,1024]{1,0:T(8,128)(2,1)S(1)}, bf16[1024,1024]{1,0:T(8,128)(2,1)}, u32[]{:S(2)}) %copy-start.1) | copy-done | bytes 2097176
  51.7 0.0 copy-start.3
  51.7 0.0 copy-start.5
  51.7 2.2 %shard_map.58 = (bf16[256,1024]{1,0:T(8,128)(2,1)S(1)}, bf16[128,1024]{1,0:T(8,128)(2,1)S(1)}) custom-call(bf16[2,128,256]{2,1,0:T(8,128)(2,1)S(1)} %get-tuple-element.20.refs_0_, bf16[256,1024]{1,0:T(8,128)(2,1)S(1)} %get-tuple-element.21.refs_1_, bf16[128,256]{1,0:T(8,128)(2,1)S(1)} %get-tuple-element.22.refs_2_, bf16[128,1024]{1,0:T(8,128)(2,1)S(1)} %bitcast.8, ...), custom_call_target="tpu_custom_call" | custom-call | flops 738197504 | bytes 3670016 | tf_op jit(solution)/shard_map/pallas_call | solution.py:299
  53.9 9.7 %all_to_all.46 = bf16[8,16,1024]{2,1,0:T(8,128)(2,1)S(1)} all-to-all(bf16[8,16,1024]{2,1,0:T(8,128)(2,1)S(1)} %bitcast.13), channel_id=1, replica_groups={{5,0,2,3,6,1,4,7},{13,8,10,11,14,9,12,15},{21,16,18,19,22,17,20,23},{29..., dimensions={0} | all-to-all | bytes 524288 | tf_op jit(solution)/shard_map/all_to_all | solution.py:247
  63.7 0.0 copy-done.3
  63.7 0.0 copy-done.5
  63.7 1.0 %shard_map.59 = (bf16[256,1024]{1,0:T(8,128)(2,1)S(1)}, bf16[256,1024]{1,0:T(8,128)(2,1)S(1)}) custom-call(bf16[2,128,256]{2,1,0:T(8,128)(2,1)S(1)} %get-tuple-element.20.refs_0_, bf16[256,1024]{1,0:T(8,128)(2,1)S(1)} %get-tuple-element.21.refs_1_, bf16[128,256]{1,0:T(8,128)(2,1)S(1)} %get-tuple-element.22.refs_2_, bf16[128,1024]{1,0:T(8,128)(2,1)S(1)} %bitcast.9, ...), custom_call_target="tpu_custom_call" | custom-call | flops 738197504 | bytes 3670016 | tf_op jit(solution)/shard_map/pallas_call | solution.py:299
  64.7 2.6 %collective-permute-start.3 = (bf16[256,1024]{1,0:T(8,128)(2,1)S(1)}, bf16[256,1024]{1,0:T(8,128)(2,1)S(1)}, u32[]{:S(2)}, u32[]{:S(2)}) collective-permute-start(bf16[256,1024]{1,0:T(8,128)(2,1)S(1)} %get-tuple-element.33), channel_id=1, source_target_pairs={{0,8},{8,0},{16,24},{24,16},{1,9},{9,1},{17,25},{25,17},{2,10},{10... | collective-permute-start | bytes 1572872 | tf_op jit(solution)/shard_map/ppermute | solution.py:234
  67.3 0.8 %shard_map.60.refs_1_ = bf16[1,2,256,1024]{3,2,1,0:T(8,128)(2,1)} custom-call(bf16[256,1024]{1,0:T(8,128)(2,1)S(1)} %get-tuple-element.34.refs_0_), custom_call_target="tpu_custom_call" | custom-call | bytes 1048576 | tf_op jit(solution)/shard_map/pallas_call | solution.py:332
  68.1 0.7 %collective-permute-done.3.refs_0_ = bf16[256,1024]{1,0:T(8,128)(2,1)S(1)} collective-permute-done((bf16[256,1024]{1,0:T(8,128)(2,1)S(1)}, bf16[256,1024]{1,0:T(8,128)(2,1)S(1)}, u32[]{:S(2)}, u32[]{:S(2)}) %collective-permute-start.3) | collective-permute-done | bytes 524320 | tf_op jit(solution)/shard_map/ppermute | solution.py:234
  68.8 0.8 %shard_map.61 = bf16[1,2,256,1024]{3,2,1,0:T(8,128)(2,1)} custom-call(bf16[256,1024]{1,0:T(8,128)(2,1)S(1)} %collective-permute-done.3.refs_0_, bf16[1,2,256,1024]{3,2,1,0:T(8,128)(2,1)} %shard_map.60.refs_1_), custom_call_target="tpu_custom_call", output_to_operand_aliasing={{}: (1, {})} | custom-call | tf_op jit(solution)/shard_map/pallas_call | solution.py:342
  (1 shorter events, 0.0 us)
Async XLA Ops:
  1.8 12.5 %collective-permute-start = (bf16[1024,1024]{1,0:T(8,128)(2,1)S(1)}, bf16[1024,1024]{1,0:T(8,128)(2,1)S(1)}, u32[]{:S(2)}, u32[]{:S(2)}) collective-permute-start(bf16[1024,1024]{1,0:T(8,128)(2,1)S(1)} %get-tuple-element.24.refs_4_), channel_id=1, source_target_pairs={{0,8},{8,0},{16,24},{24,16},{1,9},{9,1},{17,25},{25,17},{2,10},{10... | collective-permute-start | bytes 6291464 | tf_op jit(solution)/shard_map/ppermute | solution.py:234
  14.4 8.2 %copy-start = (bf16[1024,1024]{1,0:T(8,128)(2,1)}, bf16[1024,1024]{1,0:T(8,128)(2,1)S(1)}, u32[]{:S(2)}) copy-start(bf16[1024,1024]{1,0:T(8,128)(2,1)S(1)} %collective-permute-done.refs_5_) | copy-start | bytes 6291460
  23.4 0.8 %copy-start.2 = (bf16[256,1024]{1,0:T(8,128)(2,1)}, bf16[256,1024]{1,0:T(8,128)(2,1)S(1)}, u32[]{:S(2)}) copy-start(bf16[256,1024]{1,0:T(8,128)(2,1)S(1)} %get-tuple-element.31.refs_7_) | copy-start | bytes 1572868
  24.2 0.8 %copy-start.4 = (bf16[256,1024]{1,0:T(8,128)(2,1)}, bf16[256,1024]{1,0:T(8,128)(2,1)S(1)}, u32[]{:S(2)}) copy-start(bf16[256,1024]{1,0:T(8,128)(2,1)S(1)} %get-tuple-element.32.refs_8_) | copy-start | bytes 1572868
  25.0 14.6 %collective-permute-start.1 = (bf16[128,1024]{1,0:T(8,128)(2,1)S(1)}, bf16[128,1024]{1,0:T(8,128)(2,1)}, u32[]{:S(2)}, u32[]{:S(2)}) collective-permute-start(bf16[128,1024]{1,0:T(8,128)(2,1)S(1)} %get-tuple-element.27), channel_id=1, source_target_pairs={{0,24},{8,16},{1,25},{9,17},{2,26},{10,18},{3,27},{11,19},{4,28},{... | collective-permute-start | bytes 786440 | tf_op jit(solution)/shard_map/ppermute | solution.py:240
  26.3 23.6 %collective-permute-start.2 = (bf16[256,1024]{1,0:T(8,128)(2,1)}, bf16[256,1024]{1,0:T(8,128)(2,1)}, u32[]{:S(2)}, u32[]{:S(2)}) collective-permute-start(bf16[256,1024]{1,0:T(8,128)(2,1)} %get-tuple-element.28), channel_id=1, source_target_pairs={{0,24},{8,16},{1,25},{9,17},{2,26},{10,18},{3,27},{11,19},{4,28},{... | collective-permute-start | bytes 1572872 | tf_op jit(solution)/shard_map/ppermute | solution.py:240
  39.7 10.4 %all-to-all-start.2 = ((bf16[8,16,1024]{2,1,0:T(8,128)(2,1)}), bf16[8,16,1024]{2,1,0:T(8,128)(2,1)S(1)}, u32[]{:S(2)}, u32[]{:S(2)}) async-start(bf16[8,16,1024]{2,1,0:T(8,128)(2,1)} %bitcast.4), calls=%async_computation.2 | async-start | bytes 524288 | tf_op jit(solution)/shard_map/all_to_all | solution.py:247
  50.1 1.6 %copy-start.1 = (bf16[1024,1024]{1,0:T(8,128)(2,1)S(1)}, bf16[1024,1024]{1,0:T(8,128)(2,1)}, u32[]{:S(2)}) copy-start(bf16[1024,1024]{1,0:T(8,128)(2,1)} %copy-done) | copy-start | bytes 6291460
  51.7 12.0 %copy-start.3 = (bf16[256,1024]{1,0:T(8,128)(2,1)S(1)}, bf16[256,1024]{1,0:T(8,128)(2,1)}, u32[]{:S(2)}) copy-start(bf16[256,1024]{1,0:T(8,128)(2,1)} %copy-done.2) | copy-start | bytes 1572868
  51.7 12.0 %copy-start.5 = (bf16[256,1024]{1,0:T(8,128)(2,1)S(1)}, bf16[256,1024]{1,0:T(8,128)(2,1)}, u32[]{:S(2)}) copy-start(bf16[256,1024]{1,0:T(8,128)(2,1)} %copy-done.4) | copy-start | bytes 1572868
  64.7 4.1 %collective-permute-start.3 = (bf16[256,1024]{1,0:T(8,128)(2,1)S(1)}, bf16[256,1024]{1,0:T(8,128)(2,1)S(1)}, u32[]{:S(2)}, u32[]{:S(2)}) collective-permute-start(bf16[256,1024]{1,0:T(8,128)(2,1)S(1)} %get-tuple-element.33), channel_id=1, source_target_pairs={{0,8},{8,0},{16,24},{24,16},{1,9},{9,1},{17,25},{25,17},{2,10},{10... | collective-permute-start | bytes 1572872 | tf_op jit(solution)/shard_map/ppermute | solution.py:234

commit v7 on v6

--- a/solution.py
+++ b/solution.py
@@ -136,65 +136,75 @@
         copy.wait()
 
 
-def layer_kernel(group, stage, step, has_current, has_old, has_x, *refs):
+def layer_kernel(group, stage, step, todo, has_current, has_old, *refs):
     refs = list(refs)
-    mix_ref, init_ref, pick_ref, bound_ref = refs[:4]
-    weights = refs[4 : 4 + group]
-    refs = refs[4 + group :]
-    current_ref = refs.pop(0) if has_current else init_ref
     end = step == group - 1
-    earlier = [refs.pop(0) for _ in range(group - 2)] if end else []
-    old = [refs.pop(0) for _ in range(group)] if has_old else []
-    mixed_ref = refs.pop()
-    spare = None if has_x else refs.pop()
-    picked = [refs.pop() for _ in range(group)][::-1] if end else []
-    if has_x:
-        x_ref, out_ref = refs
+    take = lambda count: [refs.pop(0) for _ in range(count)]
+    weights = take(group)
+    if todo == "rest":
+        (mixed_ref,) = take(1)
+        row_blocks = 0
     else:
-        x_ref, out_ref = spare, None
+        mix_ref, init_ref, bound_ref = take(3)
+        row_blocks, side = mix_ref.shape[:2]
+    pick_ref = take(1)[0] if todo == "rows" or not end else None
+    earlier = take(group - 1) if end and todo != "rows" else []
+    current_ref = take(1)[0] if has_current and todo != "rest" else None
+    old = take(group) if has_old else []
+    if todo == "rows":
+        mixed_ref, out_ref = take(2)
+    else:
+        x_ref = take(1)[0]
+        out_ref = take(1)[0] if not end else None
+        picked = take(group) if end else []
+        if todo == "all":
+            (mixed_ref,) = take(1)
 
     section = lax.axis_index("section")
     member = section % group
-    row_blocks, side = mix_ref.shape[:2]
-
     layer = (section // group) * group + step + 1
     beta = f32(0.0)
     for number in range(step + 1, lax.axis_size("section") + 1, group):
         beta = jnp.where(layer == number, f32(math.log(strength / number + 1.0)), beta)
 
+    def activated(mixed, weight_ref):
+        product = jnp.dot(mixed, weight_ref[...], preferred_element_type=f32)
+        x = (1.0 - beta) * mixed.astype(f32) + beta * product
+        return jnp.maximum(x, 0.0).astype(bf16)
+
+    def picked_rows(source_ref):
+        return jnp.dot(pick_ref[...], source_ref[...], preferred_element_type=f32).astype(bf16)
+
     def body(weight_ref):
-        boundary = bound_ref[...]
+        source_ref = current_ref if has_current else None
         for r in range(row_blocks):
             rows = pl.ds(r * side, side)
-            both = jnp.concatenate([current_ref[rows, :], boundary], axis=0)
+            own = init_ref[rows, :] if source_ref is None else source_ref[rows, :]
+            both = jnp.concatenate([own, bound_ref[...]], axis=0)
             aggregate = jnp.dot(mix_ref[r], both, preferred_element_type=f32)
             initial = init_ref[rows, :].astype(f32)
             mixed_ref[rows, :] = ((1.0 - restart) * aggregate + restart * initial).astype(bf16)
-        mixed = mixed_ref[...]
-        product = jnp.dot(mixed, weight_ref[...], preferred_element_type=f32)
-        x = (1.0 - beta) * mixed.astype(f32) + beta * product
-        x_ref[...] = jnp.maximum(x, 0.0).astype(bf16)
+        if todo == "rows":
+            out_ref[...] = activated(picked_rows(mixed_ref), weight_ref)
+            return
+        x_ref[...] = activated(mixed_ref[...], weight_ref)
         if out_ref is not None:
-            out_ref[...] = jnp.dot(
-                pick_ref[...], x_ref[...], preferred_element_type=f32
-            ).astype(bf16)
+            out_ref[...] = picked_rows(x_ref)
 
     active = section // group == stage
     for shift in range(group):
         needed = active & ((member + shift) % group == step)
         pl.when(needed)(functools.partial(body, weights[shift]))
 
-    if end:
-        layers = earlier + ([current_ref] if group > 1 else []) + [x_ref]
+    if end and todo != "rows":
+        layers = earlier + [x_ref]
 
         def pick_from(sources):
             for target, source in zip(picked, sources):
                 target[...] = source[...]
 
         for value in range(group):
-            here = member == value
-            if old:
-                here = here & (section // group == stage)
+            here = active & (member == value) if old else member == value
 
             @pl.when(here)
             def _(value=value):
@@ -202,7 +212,7 @@
 
         if old:
 
-            @pl.when(section // group != stage)
+            @pl.when(~active)
             def _():
                 pick_from(old)
 
@@ -279,27 +289,37 @@
             ]
         )
 
-    def layer(stage, step, shared, boundary, weights, currents, old):
+    def layer(stage, step, todo, weights, operands, earlier=(), current=None, old=()):
         end = step == group - 1
-        has_x = not (end and stage == stages - 1)
-        has_current = bool(currents)
-        operands = list(shared) + [boundary] + weights
-        if has_current:
-            operands.append(currents[-1])
-        if end:
-            operands += currents[-group + 1 : -1]
-            operands += old
-        outs = [(rows, width), (sent, width)] if has_x else []
-        if end:
-            outs += [(rows, width)] * group
-        scratch = [] if has_x else [pltpu.VMEM((rows, width), bf16)]
-        scratch.append(pltpu.VMEM((rows, width), bf16))
+        operands = weights + list(operands) + list(earlier)
+        if current is not None:
+            operands.append(current)
+        operands += list(old)
+        outs = [(rows, width), (sent, width)]
+        scratch = [] if todo == "rest" else [pltpu.VMEM((rows, width), bf16)]
+        if todo == "rows":
+            scratch = []
+        elif end:
+            last = stage == stages - 1
+            outs = ([] if last else [(rows, width)]) + [(rows, width)] * group
+            if last:
+                scratch = [pltpu.VMEM((rows, width), bf16)] + scratch
         flops = 2 * width * rows * (2 * side + width) + 2 * width * rows * sent
         moved = 2 * width * (width + 3 * rows)
+        kernel = functools.partial(
+            layer_kernel, group, stage, step, todo, current is not None, bool(old)
+        )
+
+        def reordered(*refs):
+            refs = list(refs)
+            if end and todo != "rows" and stage == stages - 1:
+                place = len(operands)
+                x_ref = refs.pop(place + group)
+                refs.insert(place, x_ref)
+            kernel(*refs)
+
         return call(
-            functools.partial(
-                layer_kernel, group, stage, step, has_current, end and bool(old), has_x
-            ),
+            reordered,
             outs,
             [VMEM] * len(operands),
             [VMEM] * len(outs),
@@ -307,25 +327,49 @@
             cost=pl.CostEstimate(flops=flops, bytes_accessed=moved, transcendentals=0),
         )(*operands)
 
+    def opening_exchanged(x):
+        x, choice = lax.optimization_barrier((x, opening))
+        return lax.cond(
+            choice > 0,
+            lambda x: exchanged(x),
+            jnp.negative,
+            x,
+        )
+
     outgoing, pick, mix, init, own_weight = first()
+    opening = (lax.axis_index("section") < group).astype(jnp.int32)
+    outgoing, opening = lax.optimization_barrier((outgoing, opening))
     weights = [own_weight] + [shifted(own_weight, by) for by in range(1, group)]
     boundary = exchanged(outgoing)
-    shared = [mix, init, pick]
     current = None
     picked = []
     for stage in range(stages):
-        currents = [] if stage == 0 else [current]
-        for step in range(group):
-            result = layer(stage, step, shared, boundary, weights, currents, picked)
-            if step < group - 1:
-                currents.append(result[0])
-                boundary = exchanged(result[1])
+        earlier = []
+        for step in range(group - 1):
+            x, outgoing = layer(
+                stage, step, "all", weights, [mix, init, boundary, pick], current=current
+            )
+            earlier.append(x)
+            current = x
+            if stage == 0:
+                boundary = opening_exchanged(outgoing)
             else:
-                picked = result[-group:]
-        if stage < stages - 1:
-            rows_sent = crossed(result[1])
-            current = crossed(result[0])
-            boundary = exchanged(rows_sent)
+                boundary = exchanged(outgoing)
+        step = group - 1
+        if stage == stages - 1:
+            picked = layer(
+                stage, step, "all", weights, [mix, init, boundary], earlier, current, picked
+            )
+            break
+        mixed, outgoing = layer(
+            stage, step, "rows", weights, [mix, init, boundary, pick], current=current
+        )
+        rows_sent = crossed(outgoing)
+        x, *picked = layer(
+            stage, step, "rest", weights, [mixed], earlier, old=picked
+        )
+        current = crossed(x)
+        boundary = exchanged(rows_sent)
 
     pieces = [shifted(picked[by], by) for by in range(1, group)]
     shape = (1, batches, rows, width)

time: 70.1 us -> 70.2 us (level)
  the two profiles are of different devices: /device:TPU:5 before, /device:TPU:7 now
where the time goes in v7:
time: 70.2 us; the launch traced here: 69.6 us
  blocking collectives  21.6 us (31%)
  waiting for transfers between devices  21.3 us (30%)
  Pallas kernels  15.3 us (22%)
  starting transfers between devices  7.98 us (11%)
  other arithmetic  1.72 us (2%)
  local copies, waits for them, and re-layouts  1.63 us (2%)
    all_to_all x2, blocking collectives, exchanged(): lax.all_to_all(x, ('section', 'dom'), split_axis=0, concat_axis=0, axis_i...  21.6 us
    ppermute x2, waiting for transfers between devices, crossed(): return lax.ppermute(x, 'section', pairs)  20.2 us
    pallas_call x5, Pallas kernels, layer(): call(reordered, outs, [VMEM] * len(operands), [VMEM] * len(outs), scratch...  11.8 us
    all_to_all x1, starting transfers between devices, exchanged(): lax.all_to_all(x, ('section', 'dom'), split_axis=0, concat_axis=0, axis_i...  4.6 us
    ppermute x2, starting transfers between devices, crossed(): return lax.ppermute(x, 'section', pairs)  2.56 us
    pallas_call x1, Pallas kernels, first(): call(functools.partial(first_kernel, group), [(sent, width), (sent, rows)...  1.84 us
    neg x1, other arithmetic, opening_exchanged(): return lax.cond(choice > 0, lambda x: exchanged(x), jnp.negative, x)  1.72 us
    unnamed x8, local copies, waits for them, and re-layouts  1.63 us
  transfers between devices with their start and end apart: 5, of which 3 were waited for; matrix products, arithmetic and copies ran while one was open for 0% of the time, Pallas kernels for 5%

profile of v7, /device:TPU:7, one launch (start us, length us, event | category | flops | bytes accessed | tf_op | source)
XLA Modules:
  0.0 69.6 jit_solution(12709168286106251709)
XLA Ops:
  0.0 1.8 %shard_map.55 = (bf16[128,1024]{1,0:T(8,128)(2,1)S(1)}, bf16[128,256]{1,0:T(8,128)(2,1)S(1)}, bf16[2,128,256]{2,1,0:T(8,128)(2,1)S(1)}, bf16[256,1024]{1,0:T(8,128)(2,1)S(1)}, bf16[1024,1024]{1,0:T(8,128)(2,1)S(1)}) custom-call(s32[1,2,8,16]{3,2,1,0:T(8,128)} %send_hbm.1, s32[1,2,2,4]{3,2,1,0:T(2,128)} %block_hbm.1, bf16[2,256,1024]{2,1,0:T(8,128)(2,1)} %init_hbm.1, ...), custom_call_target="tpu_custom_call" | custom-call | tf_op jit(solution)/shard_map/pallas_call | solution.py:268
  1.8 0.7 %collective-permute-start = (bf16[1024,1024]{1,0:T(8,128)(2,1)S(1)}, bf16[1024,1024]{1,0:T(8,128)(2,1)}, u32[]{:S(2)}, u32[]{:S(2)}) collective-permute-start(bf16[1024,1024]{1,0:T(8,128)(2,1)S(1)} %get-tuple-element.30.refs_0_), channel_id=1, source_target_pairs={{0,8},{8,0},{16,24},{24,16},{1,9},{9,1},{17,25},{25,17},{2,10},{10... | collective-permute-start | bytes 6291464 | tf_op jit(solution)/shard_map/ppermute | solution.py:244
  2.6 10.7 %all_to_all.43 = bf16[8,16,1024]{2,1,0:T(8,128)(2,1)S(1)} all-to-all(bf16[8,16,1024]{2,1,0:T(8,128)(2,1)S(1)} %bitcast.11), channel_id=1, replica_groups={{5,0,2,3,6,1,4,7},{13,8,10,11,14,9,12,15},{21,16,18,19,22,17,20,23},{29..., dimensions={0} | all-to-all | bytes 524288 | tf_op jit(solution)/shard_map/all_to_all | solution.py:257
  13.3 0.0 collective-permute-done.refs_1_
  13.3 2.3 %shard_map.56 = (bf16[256,1024]{1,0:T(8,128)(2,1)S(1)}, bf16[128,1024]{1,0:T(8,128)(2,1)}) custom-call(bf16[1024,1024]{1,0:T(8,128)(2,1)S(1)} %get-tuple-element.30.refs_0_, bf16[1024,1024]{1,0:T(8,128)(2,1)} %collective-permute-done.refs_1_, bf16[2,128,256]{2,1,0:T(8,128)(2,1)S(1)} %get-tuple-element.31.refs_2_, ...), custom_call_target="tpu_custom_call" | custom-call | flops 738197504 | bytes 3670016 | tf_op jit(solution)/shard_map/pallas_call | solution.py:321
  15.6 1.7 %conditional.1 = (bf16[128,1024]{1,0:T(8,128)(2,1)}) conditional(s32[]{:T(128)} %convert_element_type.7, bf16[128,1024]{1,0:T(8,128)(2,1)} %get-tuple-element.39, bf16[128,1024]{1,0:T(8,128)(2,1)} %get-tuple-element.39), branch_computations={%region_0.0_spmd, %region_1.0_spmd} | conditional | flops 131072 | bytes 524296 | solution.py:332
  15.6 1.7 %neg.2 = bf16[128,1024]{1,0:T(8,128)(2,1)} negate(bf16[128,1024]{1,0:T(8,128)(2,1)} %param) | non-fusion elementwise | flops 131072 | bytes 524288 | tf_op jit(solution)/shard_map/cond/branch_0_fun/neg | solution.py:332
  17.3 1.6 %shard_map.57 = (bf16[256,1024]{1,0:T(8,128)(2,1)S(1)}, bf16[128,1024]{1,0:T(8,128)(2,1)S(1)}) custom-call(bf16[1024,1024]{1,0:T(8,128)(2,1)S(1)} %get-tuple-element.30.refs_0_, bf16[1024,1024]{1,0:T(8,128)(2,1)} %collective-permute-done.refs_1_, bf16[2,128,256]{2,1,0:T(8,128)(2,1)S(1)} %get-tuple-element.31.refs_2_, ...), custom_call_target="tpu_custom_call" | custom-call | flops 738197504 | bytes 3670016 | tf_op jit(solution)/shard_map/pallas_call | solution.py:321
  18.9 1.3 %collective-permute-start.1 = (bf16[128,1024]{1,0:T(8,128)(2,1)S(1)}, bf16[128,1024]{1,0:T(8,128)(2,1)}, u32[]{:S(2)}, u32[]{:S(2)}) collective-permute-start(bf16[128,1024]{1,0:T(8,128)(2,1)S(1)} %get-tuple-element.41), channel_id=1, source_target_pairs={{0,24},{8,16},{1,25},{9,17},{2,26},{10,18},{3,27},{11,19},{4,28},{... | collective-permute-start | bytes 786440 | tf_op jit(solution)/shard_map/ppermute | solution.py:250
  20.2 2.5 %shard_map.58 = (bf16[256,1024]{1,0:T(8,128)(2,1)}, bf16[256,1024]{1,0:T(8,128)(2,1)S(1)}, bf16[256,1024]{1,0:T(8,128)(2,1)S(1)}) custom-call(bf16[1024,1024]{1,0:T(8,128)(2,1)S(1)} %get-tuple-element.30.refs_0_, bf16[1024,1024]{1,0:T(8,128)(2,1)} %collective-permute-done.refs_1_, bf16[256,1024]{1,0:T(8,128)(2,1)S(1)} %get-tuple-element.42.refs_2_, ...), custom_call_target="tpu_custom_call" | custom-call | flops 738197504 | bytes 3670016 | tf_op jit(solution)/shard_map/pallas_call | solution.py:321
  22.6 0.0 copy-start
  22.6 0.8 %copy-done = bf16[256,1024]{1,0:T(8,128)(2,1)} copy-done((bf16[256,1024]{1,0:T(8,128)(2,1)}, bf16[256,1024]{1,0:T(8,128)(2,1)S(1)}, u32[]{:S(2)}) %copy-start) | copy-done | bytes 524312
  23.5 0.0 copy-start.2
  23.5 0.8 %copy-done.2 = bf16[256,1024]{1,0:T(8,128)(2,1)} copy-done((bf16[256,1024]{1,0:T(8,128)(2,1)}, bf16[256,1024]{1,0:T(8,128)(2,1)S(1)}, u32[]{:S(2)}) %copy-start.2) | copy-done | bytes 524312
  24.3 1.3 %collective-permute-start.2 = (bf16[256,1024]{1,0:T(8,128)(2,1)}, bf16[256,1024]{1,0:T(8,128)(2,1)}, u32[]{:S(2)}, u32[]{:S(2)}) collective-permute-start(bf16[256,1024]{1,0:T(8,128)(2,1)} %get-tuple-element.43), channel_id=1, source_target_pairs={{0,24},{8,16},{1,25},{9,17},{2,26},{10,18},{3,27},{11,19},{4,28},{... | collective-permute-start | bytes 1572872 | tf_op jit(solution)/shard_map/ppermute | solution.py:250
  25.6 12.2 %collective-permute-done.1 = bf16[128,1024]{1,0:T(8,128)(2,1)} collective-permute-done((bf16[128,1024]{1,0:T(8,128)(2,1)S(1)}, bf16[128,1024]{1,0:T(8,128)(2,1)}, u32[]{:S(2)}, u32[]{:S(2)}) %collective-permute-start.1) | collective-permute-done | bytes 262176 | tf_op jit(solution)/shard_map/ppermute | solution.py:250
  37.8 4.6 %all-to-all-start.2 = ((bf16[8,16,1024]{2,1,0:T(8,128)(2,1)}), bf16[8,16,1024]{2,1,0:T(8,128)(2,1)S(1)}, u32[]{:S(2)}, u32[]{:S(2)}) async-start(bf16[8,16,1024]{2,1,0:T(8,128)(2,1)} %bitcast.4), calls=%async_computation.2 | async-start | bytes 524288 | tf_op jit(solution)/shard_map/all_to_all | solution.py:257
  42.4 8.0 %collective-permute-done.2.refs_6_ = bf16[256,1024]{1,0:T(8,128)(2,1)} collective-permute-done((bf16[256,1024]{1,0:T(8,128)(2,1)}, bf16[256,1024]{1,0:T(8,128)(2,1)}, u32[]{:S(2)}, u32[]{:S(2)}) %collective-permute-start.2) | collective-permute-done | bytes 524320 | tf_op jit(solution)/shard_map/ppermute | solution.py:250
  50.4 0.0 all-to-all-done.2
  50.4 0.0 copy-start.1
  50.4 0.0 copy-start.3
  50.4 2.9 %shard_map.59 = (bf16[256,1024]{1,0:T(8,128)(2,1)S(1)}, bf16[128,1024]{1,0:T(8,128)(2,1)S(1)}) custom-call(bf16[1024,1024]{1,0:T(8,128)(2,1)S(1)} %get-tuple-element.30.refs_0_, bf16[1024,1024]{1,0:T(8,128)(2,1)} %collective-permute-done.refs_1_, bf16[2,128,256]{2,1,0:T(8,128)(2,1)S(1)} %get-tuple-element.31.refs_2_, ...), custom_call_target="tpu_custom_call" | custom-call | flops 738197504 | bytes 3670016 | tf_op jit(solution)/shard_map/pallas_call | solution.py:321
  53.3 10.9 %all_to_all.44 = bf16[8,16,1024]{2,1,0:T(8,128)(2,1)S(1)} all-to-all(bf16[8,16,1024]{2,1,0:T(8,128)(2,1)S(1)} %bitcast.12), channel_id=1, replica_groups={{5,0,2,3,6,1,4,7},{13,8,10,11,14,9,12,15},{21,16,18,19,22,17,20,23},{29..., dimensions={0} | all-to-all | bytes 524288 | tf_op jit(solution)/shard_map/all_to_all | solution.py:257
  64.2 0.0 copy-done.1
  64.2 0.0 copy-done.3
  64.2 2.6 %shard_map.60 = (bf16[256,1024]{1,0:T(8,128)(2,1)S(1)}, bf16[256,1024]{1,0:T(8,128)(2,1)S(1)}) custom-call(bf16[1024,1024]{1,0:T(8,128)(2,1)S(1)} %get-tuple-element.30.refs_0_, bf16[1024,1024]{1,0:T(8,128)(2,1)} %collective-permute-done.refs_1_, bf16[2,128,256]{2,1,0:T(8,128)(2,1)S(1)} %get-tuple-element.31.refs_2_, ...), custom_call_target="tpu_custom_call" | custom-call | flops 738197504 | bytes 3670016 | tf_op jit(solution)/shard_map/pallas_call | solution.py:321
  66.9 0.1 collective-permute-start.3
  66.9 0.8 %shard_map.61.refs_1_ = bf16[1,2,256,1024]{3,2,1,0:T(8,128)(2,1)} custom-call(bf16[256,1024]{1,0:T(8,128)(2,1)S(1)} %get-tuple-element.49.refs_0_), custom_call_target="tpu_custom_call" | custom-call | bytes 1048576 | tf_op jit(solution)/shard_map/pallas_call | solution.py:376
  67.8 1.1 %collective-permute-done.3.refs_0_ = bf16[256,1024]{1,0:T(8,128)(2,1)S(1)} collective-permute-done((bf16[256,1024]{1,0:T(8,128)(2,1)S(1)}, bf16[256,1024]{1,0:T(8,128)(2,1)S(1)}, u32[]{:S(2)}, u32[]{:S(2)}) %collective-permute-start.3) | collective-permute-done | bytes 524320 | tf_op jit(solution)/shard_map/ppermute | solution.py:244
  68.8 0.8 %shard_map.62 = bf16[1,2,256,1024]{3,2,1,0:T(8,128)(2,1)} custom-call(bf16[256,1024]{1,0:T(8,128)(2,1)S(1)} %collective-permute-done.3.refs_0_, bf16[1,2,256,1024]{3,2,1,0:T(8,128)(2,1)} %shard_map.61.refs_1_), custom_call_target="tpu_custom_call", output_to_operand_aliasing={{}: (1, {})} | custom-call | tf_op jit(solution)/shard_map/pallas_call | solution.py:386
Async XLA Ops:
  1.8 11.5 %collective-permute-start = (bf16[1024,1024]{1,0:T(8,128)(2,1)S(1)}, bf16[1024,1024]{1,0:T(8,128)(2,1)}, u32[]{:S(2)}, u32[]{:S(2)}) collective-permute-start(bf16[1024,1024]{1,0:T(8,128)(2,1)S(1)} %get-tuple-element.30.refs_0_), channel_id=1, source_target_pairs={{0,8},{8,0},{16,24},{24,16},{1,9},{9,1},{17,25},{25,17},{2,10},{10... | collective-permute-start | bytes 6291464 | tf_op jit(solution)/shard_map/ppermute | solution.py:244
  18.9 18.9 %collective-permute-start.1 = (bf16[128,1024]{1,0:T(8,128)(2,1)S(1)}, bf16[128,1024]{1,0:T(8,128)(2,1)}, u32[]{:S(2)}, u32[]{:S(2)}) collective-permute-start(bf16[128,1024]{1,0:T(8,128)(2,1)S(1)} %get-tuple-element.41), channel_id=1, source_target_pairs={{0,24},{8,16},{1,25},{9,17},{2,26},{10,18},{3,27},{11,19},{4,28},{... | collective-permute-start | bytes 786440 | tf_op jit(solution)/shard_map/ppermute | solution.py:250
  22.6 0.8 %copy-start = (bf16[256,1024]{1,0:T(8,128)(2,1)}, bf16[256,1024]{1,0:T(8,128)(2,1)S(1)}, u32[]{:S(2)}) copy-start(bf16[256,1024]{1,0:T(8,128)(2,1)S(1)} %get-tuple-element.46.refs_7_) | copy-start | bytes 1572868
  23.5 0.8 %copy-start.2 = (bf16[256,1024]{1,0:T(8,128)(2,1)}, bf16[256,1024]{1,0:T(8,128)(2,1)S(1)}, u32[]{:S(2)}) copy-start(bf16[256,1024]{1,0:T(8,128)(2,1)S(1)} %get-tuple-element.47.refs_8_) | copy-start | bytes 1572868
  24.3 26.1 %collective-permute-start.2 = (bf16[256,1024]{1,0:T(8,128)(2,1)}, bf16[256,1024]{1,0:T(8,128)(2,1)}, u32[]{:S(2)}, u32[]{:S(2)}) collective-permute-start(bf16[256,1024]{1,0:T(8,128)(2,1)} %get-tuple-element.43), channel_id=1, source_target_pairs={{0,24},{8,16},{1,25},{9,17},{2,26},{10,18},{3,27},{11,19},{4,28},{... | collective-permute-start | bytes 1572872 | tf_op jit(solution)/shard_map/ppermute | solution.py:250
  37.8 12.6 %all-to-all-start.2 = ((bf16[8,16,1024]{2,1,0:T(8,128)(2,1)}), bf16[8,16,1024]{2,1,0:T(8,128)(2,1)S(1)}, u32[]{:S(2)}, u32[]{:S(2)}) async-start(bf16[8,16,1024]{2,1,0:T(8,128)(2,1)} %bitcast.4), calls=%async_computation.2 | async-start | bytes 524288 | tf_op jit(solution)/shard_map/all_to_all | solution.py:257
  50.4 13.8 %copy-start.1 = (bf16[256,1024]{1,0:T(8,128)(2,1)S(1)}, bf16[256,1024]{1,0:T(8,128)(2,1)}, u32[]{:S(2)}) copy-start(bf16[256,1024]{1,0:T(8,128)(2,1)} %copy-done) | copy-start | bytes 1572868
  50.4 13.8 %copy-start.3 = (bf16[256,1024]{1,0:T(8,128)(2,1)S(1)}, bf16[256,1024]{1,0:T(8,128)(2,1)}, u32[]{:S(2)}) copy-start(bf16[256,1024]{1,0:T(8,128)(2,1)} %copy-done.2) | copy-start | bytes 1572868
  66.9 2.0 %collective-permute-start.3 = (bf16[256,1024]{1,0:T(8,128)(2,1)S(1)}, bf16[256,1024]{1,0:T(8,128)(2,1)S(1)}, u32[]{:S(2)}, u32[]{:S(2)}) collective-permute-start(bf16[256,1024]{1,0:T(8,128)(2,1)S(1)} %get-tuple-element.48), channel_id=1, source_target_pairs={{0,8},{8,0},{16,24},{24,16},{1,9},{9,1},{17,25},{25,17},{2,10},{10... | collective-permute-start | bytes 1572872 | tf_op jit(solution)/shard_map/ppermute | solution.py:244

commit v8 on v7

--- a/solution.py
+++ b/solution.py
@@ -32,7 +32,7 @@
 
 
 def partner_order(count):
-    return [int(i) for i in np.random.RandomState(2756).permutation(count)]
+    return [int(i) for i in np.random.RandomState(10814).permutation(count)]
 
 
 def looked_up(index, table):
@@ -40,10 +40,6 @@
     for i, value in enumerate(table):
         result = jnp.where(index == i, value, result)
     return result
-
-
-def batch_of(section, group):
-    return (section % group + section // group) % group
 
 
 def pick_matrix(send, rows):
@@ -89,7 +85,7 @@
     tiles_ref,
     sems,
 ):
-    batch = batch_of(lax.axis_index("section"), group)
+    batch = lax.axis_index("section") % group
     copies = [
         pltpu.make_async_copy(source, target, sems.at[i])
         for i, (source, target) in enumerate(
@@ -220,9 +216,9 @@
 def write_kernel(group, shifts, *refs):
     pieces = refs[: len(shifts)]
     target, sems = refs[-2:]
-    batch = batch_of(lax.axis_index("section"), group)
+    member = lax.axis_index("section") % group
     copies = [
-        pltpu.make_async_copy(piece, target.at[0, (batch + by) % group], sems.at[i])
+        pltpu.make_async_copy(piece, target.at[0, (member + by) % group], sems.at[i])
         for i, (by, piece) in enumerate(zip(shifts, pieces))
     ]
     for copy in copies:
@@ -244,9 +240,7 @@
         return lax.ppermute(x, "section", pairs)
 
     def crossed(x):
-        pairs = [
-            (s, (s // group + 1) * group + (s - 1) % group) for s in range(section_count - group)
-        ]
+        pairs = [(s, s + group) for s in range(section_count - group)]
         return lax.ppermute(x, "section", pairs)
 
     parts = lax.axis_size("dom")
@@ -264,7 +258,7 @@
         )
 
     def first():
-        chunks = 4
+        chunks = 8
         return call(
             functools.partial(first_kernel, group),
             [
@@ -327,18 +321,7 @@
             cost=pl.CostEstimate(flops=flops, bytes_accessed=moved, transcendentals=0),
         )(*operands)
 
-    def opening_exchanged(x):
-        x, choice = lax.optimization_barrier((x, opening))
-        return lax.cond(
-            choice > 0,
-            lambda x: exchanged(x),
-            jnp.negative,
-            x,
-        )
-
     outgoing, pick, mix, init, own_weight = first()
-    opening = (lax.axis_index("section") < group).astype(jnp.int32)
-    outgoing, opening = lax.optimization_barrier((outgoing, opening))
     weights = [own_weight] + [shifted(own_weight, by) for by in range(1, group)]
     boundary = exchanged(outgoing)
     current = None
@@ -351,10 +334,7 @@
             )
             earlier.append(x)
             current = x
-            if stage == 0:
-                boundary = opening_exchanged(outgoing)
-            else:
-                boundary = exchanged(outgoing)
+            boundary = exchanged(outgoing)
         step = group - 1
         if stage == stages - 1:
             picked = layer(

time: 70.2 us -> 62.9 us (0.90)
  waiting for transfers between devices: 21.3 us -> 11.6 us
  Pallas kernels: 15.3 us -> 7.63 us
  blocking collectives: 21.6 us -> 27.6 us
  starting transfers between devices: 7.98 us -> 12.4 us
  other arithmetic: 1.72 us -> 0 us
  local copies, waits for them, and re-layouts: 1.63 us -> 3.22 us
    ppermute x2, waiting for transfers between devices: 20.2 us -> 10.9 us  [crossed(): return lax.ppermute(x, 'section', pairs)]
    pallas_call x5, Pallas kernels: 11.8 us -> 4.17 us  [layer(): call(reordered, outs, [VMEM] * len(operands), [VMEM] * len(outs), scratch...]
    all_to_all x2 -> x3, blocking collectives: 21.6 us -> 27.6 us  [exchanged(): lax.all_to_all(x, ('section', 'dom'), split_axis=0, concat_axis=0, axis_i...]
    ppermute x2, starting transfers between devices: 0.81 us -> 5.47 us  [shifted(): return lax.ppermute(x, 'section', pairs)]
    neg x1 -> x0, other arithmetic: 1.72 us -> none  [opening_exchanged(): return lax.cond(choice > 0, lambda x: exchanged(x), jnp.negative, x)]
    unnamed x8 -> x12, local copies, waits for them, and re-layouts: 1.63 us -> 3.22 us
  transfers between devices with their start and end apart: 5 -> 5, of which waited for: 3 -> 3; matrix products, arithmetic and copies ran while one was open for 0% -> 0% of each run, Pallas kernels for 5% -> 3%
where the time goes in v8:
time: 62.9 us; the launch traced here: 62.4 us
  blocking collectives  27.6 us (44%)
  starting transfers between devices  12.4 us (20%)
  waiting for transfers between devices  11.6 us (18%)
  Pallas kernels  7.63 us (12%)
  local copies, waits for them, and re-layouts  3.22 us (5%)
    all_to_all x3, blocking collectives, exchanged(): lax.all_to_all(x, ('section', 'dom'), split_axis=0, concat_axis=0, axis_i...  27.6 us
    ppermute x2, waiting for transfers between devices, crossed(): return lax.ppermute(x, 'section', pairs)  10.9 us
    ppermute x2, starting transfers between devices, shifted(): return lax.ppermute(x, 'section', pairs)  5.47 us
    all_to_all x1, starting transfers between devices, exchanged(): lax.all_to_all(x, ('section', 'dom'), split_axis=0, concat_axis=0, axis_i...  4.33 us
    pallas_call x5, Pallas kernels, layer(): call(reordered, outs, [VMEM] * len(operands), [VMEM] * len(outs), scratch...  4.17 us
    unnamed x12, local copies, waits for them, and re-layouts  3.22 us
    ppermute x2, starting transfers between devices, crossed(): return lax.ppermute(x, 'section', pairs)  2.56 us
    pallas_call x1, Pallas kernels, first(): call(functools.partial(first_kernel, group), [(sent, width), (sent, rows)...  1.86 us
  transfers between devices with their start and end apart: 5, of which 3 were waited for; matrix products, arithmetic and copies ran while one was open for 0% of the time, Pallas kernels for 3%

profile of v8, /device:TPU:7, one launch (start us, length us, event | category | flops | bytes accessed | tf_op | source)
XLA Modules:
  0.0 62.4 jit_solution(9832893474360432461)
XLA Ops:
  0.0 1.9 %shard_map.55 = (bf16[128,1024]{1,0:T(8,128)(2,1)S(1)}, bf16[128,256]{1,0:T(8,128)(2,1)S(1)}, bf16[2,128,256]{2,1,0:T(8,128)(2,1)S(1)}, bf16[256,1024]{1,0:T(8,128)(2,1)S(1)}, bf16[1024,1024]{1,0:T(8,128)(2,1)S(1)}) custom-call(s32[1,2,8,16]{3,2,1,0:T(8,128)} %send_hbm.1, s32[1,2,2,4]{3,2,1,0:T(2,128)} %block_hbm.1, bf16[2,256,1024]{2,1,0:T(8,128)(2,1)} %init_hbm.1, ...), custom_call_target="tpu_custom_call" | custom-call | tf_op jit(solution)/shard_map/pallas_call | solution.py:262
  1.9 0.7 %collective-permute-start = (bf16[1024,1024]{1,0:T(8,128)(2,1)S(1)}, bf16[1024,1024]{1,0:T(8,128)(2,1)S(1)}, u32[]{:S(2)}, u32[]{:S(2)}) collective-permute-start(bf16[1024,1024]{1,0:T(8,128)(2,1)S(1)} %get-tuple-element.21.refs_0_), channel_id=1, source_target_pairs={{0,8},{8,0},{16,24},{24,16},{1,9},{9,1},{17,25},{25,17},{2,10},{10... | collective-permute-start | bytes 6291464 | tf_op jit(solution)/shard_map/ppermute | solution.py:240
  2.6 11.0 %all_to_all.44 = bf16[8,16,1024]{2,1,0:T(8,128)(2,1)S(1)} all-to-all(bf16[8,16,1024]{2,1,0:T(8,128)(2,1)S(1)} %bitcast.12), channel_id=1, replica_groups={{5,0,6,2,1,4,3,7},{13,8,14,10,9,12,11,15},{21,16,22,18,17,20,19,23},{29..., dimensions={0} | all-to-all | bytes 524288 | tf_op jit(solution)/shard_map/all_to_all | solution.py:251
  13.6 0.0 collective-permute-done.refs_1_
  13.6 0.0 copy-start
  13.6 8.1 %all_to_all.45 = bf16[8,16,1024]{2,1,0:T(8,128)(2,1)S(1)} all-to-all(bf16[8,16,1024]{2,1,0:T(8,128)(2,1)S(1)} %bitcast.14), channel_id=1, replica_groups={{5,0,6,2,1,4,3,7},{13,8,14,10,9,12,11,15},{21,16,22,18,17,20,19,23},{29..., dimensions={0} | all-to-all | bytes 524288 | tf_op jit(solution)/shard_map/all_to_all | solution.py:251
  21.7 1.3 %collective-permute-start.1 = (bf16[128,1024]{1,0:T(8,128)(2,1)S(1)}, bf16[128,1024]{1,0:T(8,128)(2,1)}, u32[]{:S(2)}, u32[]{:S(2)}) collective-permute-start(bf16[128,1024]{1,0:T(8,128)(2,1)S(1)} %get-tuple-element.28), channel_id=1, source_target_pairs={{0,16},{8,24},{1,17},{9,25},{2,18},{10,26},{3,19},{11,27},{4,20},{... | collective-permute-start | bytes 786440 | tf_op jit(solution)/shard_map/ppermute | solution.py:244
  23.0 0.0 copy-done
  23.0 0.9 %shard_map.58 = (bf16[256,1024]{1,0:T(8,128)(2,1)}, bf16[256,1024]{1,0:T(8,128)(2,1)S(1)}, bf16[256,1024]{1,0:T(8,128)(2,1)S(1)}) custom-call(bf16[1024,1024]{1,0:T(8,128)(2,1)S(1)} %get-tuple-element.21.refs_0_, bf16[1024,1024]{1,0:T(8,128)(2,1)S(1)} %collective-permute-done.refs_1_, bf16[256,1024]{1,0:T(8,128)(2,1)S(1)} %get-tuple-element.29.refs_2_, ...), custom_call_target="tpu_custom_call" | custom-call | flops 738197504 | bytes 3670016 | tf_op jit(solution)/shard_map/pallas_call | solution.py:315
  23.9 0.0 copy-start.2
  23.9 0.8 %copy-done.2 = bf16[256,1024]{1,0:T(8,128)(2,1)} copy-done((bf16[256,1024]{1,0:T(8,128)(2,1)}, bf16[256,1024]{1,0:T(8,128)(2,1)S(1)}, u32[]{:S(2)}) %copy-start.2) | copy-done | bytes 524312
  24.8 0.0 copy-start.4
  24.8 0.8 %copy-done.4 = bf16[256,1024]{1,0:T(8,128)(2,1)} copy-done((bf16[256,1024]{1,0:T(8,128)(2,1)}, bf16[256,1024]{1,0:T(8,128)(2,1)S(1)}, u32[]{:S(2)}) %copy-start.4) | copy-done | bytes 524312
  25.6 1.3 %collective-permute-start.2 = (bf16[256,1024]{1,0:T(8,128)(2,1)}, bf16[256,1024]{1,0:T(8,128)(2,1)}, u32[]{:S(2)}, u32[]{:S(2)}) collective-permute-start(bf16[256,1024]{1,0:T(8,128)(2,1)} %get-tuple-element.30), channel_id=1, source_target_pairs={{0,16},{8,24},{1,17},{9,25},{2,18},{10,26},{3,19},{11,27},{4,20},{... | collective-permute-start | bytes 1572872 | tf_op jit(solution)/shard_map/ppermute | solution.py:244
  26.9 2.3 %collective-permute-done.1 = bf16[128,1024]{1,0:T(8,128)(2,1)} collective-permute-done((bf16[128,1024]{1,0:T(8,128)(2,1)S(1)}, bf16[128,1024]{1,0:T(8,128)(2,1)}, u32[]{:S(2)}, u32[]{:S(2)}) %collective-permute-start.1) | collective-permute-done | bytes 262176 | tf_op jit(solution)/shard_map/ppermute | solution.py:244
  29.1 4.3 %all-to-all-start.2 = ((bf16[8,16,1024]{2,1,0:T(8,128)(2,1)}), bf16[8,16,1024]{2,1,0:T(8,128)(2,1)S(1)}, u32[]{:S(2)}, u32[]{:S(2)}) async-start(bf16[8,16,1024]{2,1,0:T(8,128)(2,1)} %bitcast.4), calls=%async_computation.2 | async-start | bytes 524288 | tf_op jit(solution)/shard_map/all_to_all | solution.py:251
  33.4 8.6 %collective-permute-done.2.refs_6_ = bf16[256,1024]{1,0:T(8,128)(2,1)} collective-permute-done((bf16[256,1024]{1,0:T(8,128)(2,1)}, bf16[256,1024]{1,0:T(8,128)(2,1)}, u32[]{:S(2)}, u32[]{:S(2)}) %collective-permute-start.2) | collective-permute-done | bytes 524320 | tf_op jit(solution)/shard_map/ppermute | solution.py:244
  42.1 0.0 all-to-all-done.2
  42.1 0.0 copy-start.1
  42.1 1.6 %copy-done.1 = bf16[1024,1024]{1,0:T(8,128)(2,1)S(1)} copy-done((bf16[1024,1024]{1,0:T(8,128)(2,1)S(1)}, bf16[1024,1024]{1,0:T(8,128)(2,1)}, u32[]{:S(2)}) %copy-start.1) | copy-done | bytes 2097176
  43.6 0.0 copy-start.3
  43.7 0.0 copy-start.5
  43.7 2.2 %shard_map.59 = (bf16[256,1024]{1,0:T(8,128)(2,1)S(1)}, bf16[128,1024]{1,0:T(8,128)(2,1)S(1)}) custom-call(bf16[1024,1024]{1,0:T(8,128)(2,1)S(1)} %get-tuple-element.21.refs_0_, bf16[1024,1024]{1,0:T(8,128)(2,1)S(1)} %copy-done.1, bf16[2,128,256]{2,1,0:T(8,128)(2,1)S(1)} %get-tuple-element.22.refs_2_, bf16[256,1024]{1,0:T(8,128)(2,1)S(1)} %get-tuple-element.23.refs_3_, ...), custom_call_target="tpu_custom_call" | custom-call | flops 738197504 | bytes 3670016 | tf_op jit(solution)/shard_map/pallas_call | solution.py:315
  45.9 8.4 %all_to_all.46 = bf16[8,16,1024]{2,1,0:T(8,128)(2,1)S(1)} all-to-all(bf16[8,16,1024]{2,1,0:T(8,128)(2,1)S(1)} %bitcast.13), channel_id=1, replica_groups={{5,0,6,2,1,4,3,7},{13,8,14,10,9,12,11,15},{21,16,22,18,17,20,19,23},{29..., dimensions={0} | all-to-all | bytes 524288 | tf_op jit(solution)/shard_map/all_to_all | solution.py:251
  54.3 0.0 copy-done.3
  54.3 0.0 copy-done.5
  54.3 1.0 %shard_map.60 = (bf16[256,1024]{1,0:T(8,128)(2,1)S(1)}, bf16[256,1024]{1,0:T(8,128)(2,1)S(1)}) custom-call(bf16[1024,1024]{1,0:T(8,128)(2,1)S(1)} %get-tuple-element.21.refs_0_, bf16[1024,1024]{1,0:T(8,128)(2,1)S(1)} %copy-done.1, bf16[2,128,256]{2,1,0:T(8,128)(2,1)S(1)} %get-tuple-element.22.refs_2_, bf16[256,1024]{1,0:T(8,128)(2,1)S(1)} %get-tuple-element.23.refs_3_, ...), custom_call_target="tpu_custom_call" | custom-call | flops 738197504 | bytes 3670016 | tf_op jit(solution)/shard_map/pallas_call | solution.py:315
  55.4 4.7 %collective-permute-start.3 = (bf16[256,1024]{1,0:T(8,128)(2,1)S(1)}, bf16[256,1024]{1,0:T(8,128)(2,1)S(1)}, u32[]{:S(2)}, u32[]{:S(2)}) collective-permute-start(bf16[256,1024]{1,0:T(8,128)(2,1)S(1)} %get-tuple-element.35), channel_id=1, source_target_pairs={{0,8},{8,0},{16,24},{24,16},{1,9},{9,1},{17,25},{25,17},{2,10},{10... | collective-permute-start | bytes 1572872 | tf_op jit(solution)/shard_map/ppermute | solution.py:240
  60.1 0.8 %shard_map.61.refs_1_ = bf16[1,2,256,1024]{3,2,1,0:T(8,128)(2,1)} custom-call(bf16[256,1024]{1,0:T(8,128)(2,1)S(1)} %get-tuple-element.36.refs_0_), custom_call_target="tpu_custom_call" | custom-call | bytes 1048576 | tf_op jit(solution)/shard_map/pallas_call | solution.py:356
  60.9 0.7 %collective-permute-done.3.refs_0_ = bf16[256,1024]{1,0:T(8,128)(2,1)S(1)} collective-permute-done((bf16[256,1024]{1,0:T(8,128)(2,1)S(1)}, bf16[256,1024]{1,0:T(8,128)(2,1)S(1)}, u32[]{:S(2)}, u32[]{:S(2)}) %collective-permute-start.3) | collective-permute-done | bytes 524320 | tf_op jit(solution)/shard_map/ppermute | solution.py:240
  61.6 0.8 %shard_map.62 = bf16[1,2,256,1024]{3,2,1,0:T(8,128)(2,1)} custom-call(bf16[256,1024]{1,0:T(8,128)(2,1)S(1)} %collective-permute-done.3.refs_0_, bf16[1,2,256,1024]{3,2,1,0:T(8,128)(2,1)} %shard_map.61.refs_1_), custom_call_target="tpu_custom_call", output_to_operand_aliasing={{}: (1, {})} | custom-call | tf_op jit(solution)/shard_map/pallas_call | solution.py:366
  (2 shorter events, 0.0 us)
Async XLA Ops:
  1.9 11.8 %collective-permute-start = (bf16[1024,1024]{1,0:T(8,128)(2,1)S(1)}, bf16[1024,1024]{1,0:T(8,128)(2,1)S(1)}, u32[]{:S(2)}, u32[]{:S(2)}) collective-permute-start(bf16[1024,1024]{1,0:T(8,128)(2,1)S(1)} %get-tuple-element.21.refs_0_), channel_id=1, source_target_pairs={{0,8},{8,0},{16,24},{24,16},{1,9},{9,1},{17,25},{25,17},{2,10},{10... | collective-permute-start | bytes 6291464 | tf_op jit(solution)/shard_map/ppermute | solution.py:240
  13.6 9.4 %copy-start = (bf16[1024,1024]{1,0:T(8,128)(2,1)}, bf16[1024,1024]{1,0:T(8,128)(2,1)S(1)}, u32[]{:S(2)}) copy-start(bf16[1024,1024]{1,0:T(8,128)(2,1)S(1)} %collective-permute-done.refs_1_) | copy-start | bytes 6291460
  21.7 7.4 %collective-permute-start.1 = (bf16[128,1024]{1,0:T(8,128)(2,1)S(1)}, bf16[128,1024]{1,0:T(8,128)(2,1)}, u32[]{:S(2)}, u32[]{:S(2)}) collective-permute-start(bf16[128,1024]{1,0:T(8,128)(2,1)S(1)} %get-tuple-element.28), channel_id=1, source_target_pairs={{0,16},{8,24},{1,17},{9,25},{2,18},{10,26},{3,19},{11,27},{4,20},{... | collective-permute-start | bytes 786440 | tf_op jit(solution)/shard_map/ppermute | solution.py:244
  23.9 0.8 %copy-start.2 = (bf16[256,1024]{1,0:T(8,128)(2,1)}, bf16[256,1024]{1,0:T(8,128)(2,1)S(1)}, u32[]{:S(2)}) copy-start(bf16[256,1024]{1,0:T(8,128)(2,1)S(1)} %get-tuple-element.33.refs_7_) | copy-start | bytes 1572868
  24.8 0.8 %copy-start.4 = (bf16[256,1024]{1,0:T(8,128)(2,1)}, bf16[256,1024]{1,0:T(8,128)(2,1)S(1)}, u32[]{:S(2)}) copy-start(bf16[256,1024]{1,0:T(8,128)(2,1)S(1)} %get-tuple-element.34.refs_8_) | copy-start | bytes 1572868
  25.6 16.5 %collective-permute-start.2 = (bf16[256,1024]{1,0:T(8,128)(2,1)}, bf16[256,1024]{1,0:T(8,128)(2,1)}, u32[]{:S(2)}, u32[]{:S(2)}) collective-permute-start(bf16[256,1024]{1,0:T(8,128)(2,1)} %get-tuple-element.30), channel_id=1, source_target_pairs={{0,16},{8,24},{1,17},{9,25},{2,18},{10,26},{3,19},{11,27},{4,20},{... | collective-permute-start | bytes 1572872 | tf_op jit(solution)/shard_map/ppermute | solution.py:244
  29.1 12.9 %all-to-all-start.2 = ((bf16[8,16,1024]{2,1,0:T(8,128)(2,1)}), bf16[8,16,1024]{2,1,0:T(8,128)(2,1)S(1)}, u32[]{:S(2)}, u32[]{:S(2)}) async-start(bf16[8,16,1024]{2,1,0:T(8,128)(2,1)} %bitcast.4), calls=%async_computation.2 | async-start | bytes 524288 | tf_op jit(solution)/shard_map/all_to_all | solution.py:251
  42.1 1.6 %copy-start.1 = (bf16[1024,1024]{1,0:T(8,128)(2,1)S(1)}, bf16[1024,1024]{1,0:T(8,128)(2,1)}, u32[]{:S(2)}) copy-start(bf16[1024,1024]{1,0:T(8,128)(2,1)} %copy-done) | copy-start | bytes 6291460
  43.6 10.7 %copy-start.3 = (bf16[256,1024]{1,0:T(8,128)(2,1)S(1)}, bf16[256,1024]{1,0:T(8,128)(2,1)}, u32[]{:S(2)}) copy-start(bf16[256,1024]{1,0:T(8,128)(2,1)} %copy-done.2) | copy-start | bytes 1572868
  43.7 10.7 %copy-start.5 = (bf16[256,1024]{1,0:T(8,128)(2,1)S(1)}, bf16[256,1024]{1,0:T(8,128)(2,1)}, u32[]{:S(2)}) copy-start(bf16[256,1024]{1,0:T(8,128)(2,1)} %copy-done.4) | copy-start | bytes 1572868
  55.4 6.3 %collective-permute-start.3 = (bf16[256,1024]{1,0:T(8,128)(2,1)S(1)}, bf16[256,1024]{1,0:T(8,128)(2,1)S(1)}, u32[]{:S(2)}, u32[]{:S(2)}) collective-permute-start(bf16[256,1024]{1,0:T(8,128)(2,1)S(1)} %get-tuple-element.35), channel_id=1, source_target_pairs={{0,8},{8,0},{16,24},{24,16},{1,9},{9,1},{17,25},{25,17},{2,10},{10... | collective-permute-start | bytes 1572872 | tf_op jit(solution)/shard_map/ppermute | solution.py:240

commit v9 on v8

--- a/solution.py
+++ b/solution.py
@@ -16,6 +16,7 @@
 bf16 = jnp.bfloat16
 f32 = jnp.float32
 MIB = 1024 * 1024
+LATE = 5
 
 
 def call(kernel, outs, in_specs, out_specs, scratch=(), aliases=None, cost=None):
@@ -40,6 +41,10 @@
     for i, value in enumerate(table):
         result = jnp.where(index == i, value, result)
     return result
+
+
+def batch_of(section, group):
+    return (section % group + section // group) % group
 
 
 def pick_matrix(send, rows):
@@ -85,7 +90,7 @@
     tiles_ref,
     sems,
 ):
-    batch = lax.axis_index("section") % group
+    batch = batch_of(lax.axis_index("section"), group)
     copies = [
         pltpu.make_async_copy(source, target, sems.at[i])
         for i, (source, target) in enumerate(
@@ -132,6 +137,18 @@
         copy.wait()
 
 
+def hold_kernel(group, rows_ref, weight_hbm, out_ref, room_ref, sem):
+    section = lax.axis_index("section")
+
+    @pl.when((section // group > 0) & (section % group == group - 1))
+    def _():
+        @pl.loop(0, LATE)
+        def _(step):
+            copy = pltpu.make_async_copy(weight_hbm.at[0, pl.ds(0, room_ref.shape[0])], room_ref, sem)
+            copy.start()
+            copy.wait()
+
+
 def layer_kernel(group, stage, step, todo, has_current, has_old, *refs):
     refs = list(refs)
     end = step == group - 1
@@ -216,9 +233,9 @@
 def write_kernel(group, shifts, *refs):
     pieces = refs[: len(shifts)]
     target, sems = refs[-2:]
-    member = lax.axis_index("section") % group
+    batch = batch_of(lax.axis_index("section"), group)
     copies = [
-        pltpu.make_async_copy(piece, target.at[0, (member + by) % group], sems.at[i])
+        pltpu.make_async_copy(piece, target.at[0, (batch + by) % group], sems.at[i])
         for i, (by, piece) in enumerate(zip(shifts, pieces))
     ]
     for copy in copies:
@@ -240,7 +257,9 @@
         return lax.ppermute(x, "section", pairs)
 
     def crossed(x):
-        pairs = [(s, s + group) for s in range(section_count - group)]
+        pairs = [
+            (s, (s // group + 1) * group + (s - 1) % group) for s in range(section_count - group)
+        ]
         return lax.ppermute(x, "section", pairs)
 
     parts = lax.axis_size("dom")
@@ -323,6 +342,14 @@
 
     outgoing, pick, mix, init, own_weight = first()
     weights = [own_weight] + [shifted(own_weight, by) for by in range(1, group)]
+    outgoing = call(
+        functools.partial(hold_kernel, group),
+        [(sent, width)],
+        [VMEM, HBM],
+        [VMEM],
+        [pltpu.VMEM((rows, width), bf16), pltpu.SemaphoreType.DMA(())],
+        aliases={0: 0},
+    )(outgoing, pltpu.with_memory_space_constraint(layer_weight, pltpu.HBM))[0]
     boundary = exchanged(outgoing)
     current = None
     picked = []

time: 62.9 us -> 63.5 us (level)
  the two profiles are of different devices: /device:TPU:7 before, /device:TPU:5 now
where the time goes in v9:
time: 63.5 us; the launch traced here: 62.9 us
  blocking collectives  28.4 us (45%)
  Pallas kernels  12.9 us (20%)
  waiting for transfers between devices  9.43 us (15%)
  starting transfers between devices  8.92 us (14%)
  local copies, waits for them, and re-layouts  3.22 us (5%)
    all_to_all x3, blocking collectives, exchanged(): lax.all_to_all(x, ('section', 'dom'), split_axis=0, concat_axis=0, axis_i...  28.4 us
    ppermute x2, waiting for transfers between devices, crossed(): return lax.ppermute(x, 'section', pairs)  8.36 us
    all_to_all x1, starting transfers between devices, exchanged(): lax.all_to_all(x, ('section', 'dom'), split_axis=0, concat_axis=0, axis_i...  5.55 us
    pallas_call x1, Pallas kernels, on_device(): call(functools.partial(hold_kernel, group), [(sent, width)], [VMEM, HBM],...  5.21 us
    pallas_call x5, Pallas kernels, layer(): call(reordered, outs, [VMEM] * len(operands), [VMEM] * len(outs), scratch...  4.17 us
    unnamed x12, local copies, waits for them, and re-layouts  3.22 us
    ppermute x2, starting transfers between devices, crossed(): return lax.ppermute(x, 'section', pairs)  2.56 us
    pallas_call x1, Pallas kernels, first(): call(functools.partial(first_kernel, group), [(sent, width), (sent, rows)...  1.86 us
  transfers between devices with their start and end apart: 5, of which 3 were waited for; matrix products, arithmetic and copies ran while one was open for 0% of the time, Pallas kernels for 11%

profile of v9, /device:TPU:5, one launch (start us, length us, event | category | flops | bytes accessed | tf_op | source)
XLA Modules:
  0.0 62.9 jit_solution(7831538299057540174)
XLA Ops:
  0.0 1.9 %shard_map.55 = (bf16[128,1024]{1,0:T(8,128)(2,1)S(1)}, bf16[128,256]{1,0:T(8,128)(2,1)S(1)}, bf16[2,128,256]{2,1,0:T(8,128)(2,1)S(1)}, bf16[256,1024]{1,0:T(8,128)(2,1)S(1)}, bf16[1024,1024]{1,0:T(8,128)(2,1)S(1)}) custom-call(s32[1,2,8,16]{3,2,1,0:T(8,128)} %send_hbm.1, s32[1,2,2,4]{3,2,1,0:T(2,128)} %block_hbm.1, bf16[2,256,1024]{2,1,0:T(8,128)(2,1)} %init_hbm.1, ...), custom_call_target="tpu_custom_call" | custom-call | tf_op jit(solution)/shard_map/pallas_call | solution.py:281
  1.9 0.7 %collective-permute-start = (bf16[1024,1024]{1,0:T(8,128)(2,1)S(1)}, bf16[1024,1024]{1,0:T(8,128)(2,1)S(1)}, u32[]{:S(2)}, u32[]{:S(2)}) collective-permute-start(bf16[1024,1024]{1,0:T(8,128)(2,1)S(1)} %get-tuple-element.21.refs_0_), channel_id=1, source_target_pairs={{0,8},{8,0},{16,24},{24,16},{1,9},{9,1},{17,25},{25,17},{2,10},{10... | collective-permute-start | bytes 6291464 | tf_op jit(solution)/shard_map/ppermute | solution.py:257
  2.6 5.2 %shard_map.56 = bf16[128,1024]{1,0:T(8,128)(2,1)S(1)} custom-call(bf16[128,1024]{1,0:T(8,128)(2,1)S(1)} %get-tuple-element.24.rows_ref, bf16[1,1024,1024]{2,1,0:T(8,128)(2,1)} %weight_hbm.3), custom_call_target="tpu_custom_call", output_to_operand_aliasing={{}: (0, {})} | custom-call | tf_op jit(solution)/shard_map/pallas_call | solution.py:345
  7.8 9.0 %all_to_all.44 = bf16[8,16,1024]{2,1,0:T(8,128)(2,1)S(1)} all-to-all(bf16[8,16,1024]{2,1,0:T(8,128)(2,1)S(1)} %bitcast.10), channel_id=1, replica_groups={{5,0,6,2,1,4,3,7},{13,8,14,10,9,12,11,15},{21,16,22,18,17,20,19,23},{29..., dimensions={0} | all-to-all | bytes 524288 | tf_op jit(solution)/shard_map/all_to_all | solution.py:270
  16.9 0.0 collective-permute-done.refs_1_
  16.9 0.0 copy-start
  16.9 8.4 %all_to_all.45 = bf16[8,16,1024]{2,1,0:T(8,128)(2,1)S(1)} all-to-all(bf16[8,16,1024]{2,1,0:T(8,128)(2,1)S(1)} %bitcast.14), channel_id=1, replica_groups={{5,0,6,2,1,4,3,7},{13,8,14,10,9,12,11,15},{21,16,22,18,17,20,19,23},{29..., dimensions={0} | all-to-all | bytes 524288 | tf_op jit(solution)/shard_map/all_to_all | solution.py:270
  25.3 1.3 %collective-permute-start.1 = (bf16[128,1024]{1,0:T(8,128)(2,1)S(1)}, bf16[128,1024]{1,0:T(8,128)(2,1)}, u32[]{:S(2)}, u32[]{:S(2)}) collective-permute-start(bf16[128,1024]{1,0:T(8,128)(2,1)S(1)} %get-tuple-element.28), channel_id=1, source_target_pairs={{0,24},{8,16},{1,25},{9,17},{2,26},{10,18},{3,27},{11,19},{4,28},{... | collective-permute-start | bytes 786440 | tf_op jit(solution)/shard_map/ppermute | solution.py:263
  26.6 0.0 copy-done
  26.6 0.9 %shard_map.59 = (bf16[256,1024]{1,0:T(8,128)(2,1)}, bf16[256,1024]{1,0:T(8,128)(2,1)S(1)}, bf16[256,1024]{1,0:T(8,128)(2,1)S(1)}) custom-call(bf16[1024,1024]{1,0:T(8,128)(2,1)S(1)} %get-tuple-element.21.refs_0_, bf16[1024,1024]{1,0:T(8,128)(2,1)S(1)} %collective-permute-done.refs_1_, bf16[256,1024]{1,0:T(8,128)(2,1)S(1)} %get-tuple-element.29.refs_2_, ...), custom_call_target="tpu_custom_call" | custom-call | flops 738197504 | bytes 3670016 | tf_op jit(solution)/shard_map/pallas_call | solution.py:334
  27.5 0.0 copy-start.2
  27.5 0.8 %copy-done.2 = bf16[256,1024]{1,0:T(8,128)(2,1)} copy-done((bf16[256,1024]{1,0:T(8,128)(2,1)}, bf16[256,1024]{1,0:T(8,128)(2,1)S(1)}, u32[]{:S(2)}) %copy-start.2) | copy-done | bytes 524312
  28.3 0.0 copy-start.4
  28.3 0.8 %copy-done.4 = bf16[256,1024]{1,0:T(8,128)(2,1)} copy-done((bf16[256,1024]{1,0:T(8,128)(2,1)}, bf16[256,1024]{1,0:T(8,128)(2,1)S(1)}, u32[]{:S(2)}) %copy-start.4) | copy-done | bytes 524312
  29.1 1.3 %collective-permute-start.2 = (bf16[256,1024]{1,0:T(8,128)(2,1)}, bf16[256,1024]{1,0:T(8,128)(2,1)}, u32[]{:S(2)}, u32[]{:S(2)}) collective-permute-start(bf16[256,1024]{1,0:T(8,128)(2,1)} %get-tuple-element.30), channel_id=1, source_target_pairs={{0,24},{8,16},{1,25},{9,17},{2,26},{10,18},{3,27},{11,19},{4,28},{... | collective-permute-start | bytes 1572872 | tf_op jit(solution)/shard_map/ppermute | solution.py:263
  30.4 3.4 %collective-permute-done.1 = bf16[128,1024]{1,0:T(8,128)(2,1)} collective-permute-done((bf16[128,1024]{1,0:T(8,128)(2,1)S(1)}, bf16[128,1024]{1,0:T(8,128)(2,1)}, u32[]{:S(2)}, u32[]{:S(2)}) %collective-permute-start.1) | collective-permute-done | bytes 262176 | tf_op jit(solution)/shard_map/ppermute | solution.py:263
  33.8 5.5 %all-to-all-start.2 = ((bf16[8,16,1024]{2,1,0:T(8,128)(2,1)}), bf16[8,16,1024]{2,1,0:T(8,128)(2,1)S(1)}, u32[]{:S(2)}, u32[]{:S(2)}) async-start(bf16[8,16,1024]{2,1,0:T(8,128)(2,1)} %bitcast.4), calls=%async_computation.2 | async-start | bytes 524288 | tf_op jit(solution)/shard_map/all_to_all | solution.py:270
  39.3 5.0 %collective-permute-done.2.refs_6_ = bf16[256,1024]{1,0:T(8,128)(2,1)} collective-permute-done((bf16[256,1024]{1,0:T(8,128)(2,1)}, bf16[256,1024]{1,0:T(8,128)(2,1)}, u32[]{:S(2)}, u32[]{:S(2)}) %collective-permute-start.2) | collective-permute-done | bytes 524320 | tf_op jit(solution)/shard_map/ppermute | solution.py:263
  44.3 0.0 all-to-all-done.2
  44.3 0.0 copy-start.1
  44.3 1.6 %copy-done.1 = bf16[1024,1024]{1,0:T(8,128)(2,1)S(1)} copy-done((bf16[1024,1024]{1,0:T(8,128)(2,1)S(1)}, bf16[1024,1024]{1,0:T(8,128)(2,1)}, u32[]{:S(2)}) %copy-start.1) | copy-done | bytes 2097176
  45.9 0.0 copy-start.3
  45.9 0.0 copy-start.5
  45.9 2.2 %shard_map.60 = (bf16[256,1024]{1,0:T(8,128)(2,1)S(1)}, bf16[128,1024]{1,0:T(8,128)(2,1)S(1)}) custom-call(bf16[1024,1024]{1,0:T(8,128)(2,1)S(1)} %get-tuple-element.21.refs_0_, bf16[1024,1024]{1,0:T(8,128)(2,1)S(1)} %copy-done.1, bf16[2,128,256]{2,1,0:T(8,128)(2,1)S(1)} %get-tuple-element.22.refs_2_, bf16[256,1024]{1,0:T(8,128)(2,1)S(1)} %get-tuple-element.23.refs_3_, ...), custom_call_target="tpu_custom_call" | custom-call | flops 738197504 | bytes 3670016 | tf_op jit(solution)/shard_map/pallas_call | solution.py:334
  48.1 10.9 %all_to_all.46 = bf16[8,16,1024]{2,1,0:T(8,128)(2,1)S(1)} all-to-all(bf16[8,16,1024]{2,1,0:T(8,128)(2,1)S(1)} %bitcast.13), channel_id=1, replica_groups={{5,0,6,2,1,4,3,7},{13,8,14,10,9,12,11,15},{21,16,22,18,17,20,19,23},{29..., dimensions={0} | all-to-all | bytes 524288 | tf_op jit(solution)/shard_map/all_to_all | solution.py:270
  59.1 0.0 copy-done.3
  59.1 0.0 copy-done.5
  59.1 1.0 %shard_map.61 = (bf16[256,1024]{1,0:T(8,128)(2,1)S(1)}, bf16[256,1024]{1,0:T(8,128)(2,1)S(1)}) custom-call(bf16[1024,1024]{1,0:T(8,128)(2,1)S(1)} %get-tuple-element.21.refs_0_, bf16[1024,1024]{1,0:T(8,128)(2,1)S(1)} %copy-done.1, bf16[2,128,256]{2,1,0:T(8,128)(2,1)S(1)} %get-tuple-element.22.refs_2_, bf16[256,1024]{1,0:T(8,128)(2,1)S(1)} %get-tuple-element.23.refs_3_, ...), custom_call_target="tpu_custom_call" | custom-call | flops 738197504 | bytes 3670016 | tf_op jit(solution)/shard_map/pallas_call | solution.py:334
  60.1 0.1 collective-permute-start.3
  60.2 0.8 %shard_map.62.refs_1_ = bf16[1,2,256,1024]{3,2,1,0:T(8,128)(2,1)} custom-call(bf16[256,1024]{1,0:T(8,128)(2,1)S(1)} %get-tuple-element.36.refs_0_), custom_call_target="tpu_custom_call" | custom-call | bytes 1048576 | tf_op jit(solution)/shard_map/pallas_call | solution.py:383
  61.0 1.1 %collective-permute-done.3.refs_0_ = bf16[256,1024]{1,0:T(8,128)(2,1)S(1)} collective-permute-done((bf16[256,1024]{1,0:T(8,128)(2,1)S(1)}, bf16[256,1024]{1,0:T(8,128)(2,1)S(1)}, u32[]{:S(2)}, u32[]{:S(2)}) %collective-permute-start.3) | collective-permute-done | bytes 524320 | tf_op jit(solution)/shard_map/ppermute | solution.py:257
  62.1 0.8 %shard_map.63 = bf16[1,2,256,1024]{3,2,1,0:T(8,128)(2,1)} custom-call(bf16[256,1024]{1,0:T(8,128)(2,1)S(1)} %collective-permute-done.3.refs_0_, bf16[1,2,256,1024]{3,2,1,0:T(8,128)(2,1)} %shard_map.62.refs_1_), custom_call_target="tpu_custom_call", output_to_operand_aliasing={{}: (1, {})} | custom-call | tf_op jit(solution)/shard_map/pallas_call | solution.py:393
  (2 shorter events, 0.0 us)
Async XLA Ops:
  1.9 15.0 %collective-permute-start = (bf16[1024,1024]{1,0:T(8,128)(2,1)S(1)}, bf16[1024,1024]{1,0:T(8,128)(2,1)S(1)}, u32[]{:S(2)}, u32[]{:S(2)}) collective-permute-start(bf16[1024,1024]{1,0:T(8,128)(2,1)S(1)} %get-tuple-element.21.refs_0_), channel_id=1, source_target_pairs={{0,8},{8,0},{16,24},{24,16},{1,9},{9,1},{17,25},{25,17},{2,10},{10... | collective-permute-start | bytes 6291464 | tf_op jit(solution)/shard_map/ppermute | solution.py:257
  16.9 9.7 %copy-start = (bf16[1024,1024]{1,0:T(8,128)(2,1)}, bf16[1024,1024]{1,0:T(8,128)(2,1)S(1)}, u32[]{:S(2)}) copy-start(bf16[1024,1024]{1,0:T(8,128)(2,1)S(1)} %collective-permute-done.refs_1_) | copy-start | bytes 6291460
  25.3 8.5 %collective-permute-start.1 = (bf16[128,1024]{1,0:T(8,128)(2,1)S(1)}, bf16[128,1024]{1,0:T(8,128)(2,1)}, u32[]{:S(2)}, u32[]{:S(2)}) collective-permute-start(bf16[128,1024]{1,0:T(8,128)(2,1)S(1)} %get-tuple-element.28), channel_id=1, source_target_pairs={{0,24},{8,16},{1,25},{9,17},{2,26},{10,18},{3,27},{11,19},{4,28},{... | collective-permute-start | bytes 786440 | tf_op jit(solution)/shard_map/ppermute | solution.py:263
  27.5 0.8 %copy-start.2 = (bf16[256,1024]{1,0:T(8,128)(2,1)}, bf16[256,1024]{1,0:T(8,128)(2,1)S(1)}, u32[]{:S(2)}) copy-start(bf16[256,1024]{1,0:T(8,128)(2,1)S(1)} %get-tuple-element.33.refs_7_) | copy-start | bytes 1572868
  28.3 0.8 %copy-start.4 = (bf16[256,1024]{1,0:T(8,128)(2,1)}, bf16[256,1024]{1,0:T(8,128)(2,1)S(1)}, u32[]{:S(2)}) copy-start(bf16[256,1024]{1,0:T(8,128)(2,1)S(1)} %get-tuple-element.34.refs_8_) | copy-start | bytes 1572868
  29.1 15.2 %collective-permute-start.2 = (bf16[256,1024]{1,0:T(8,128)(2,1)}, bf16[256,1024]{1,0:T(8,128)(2,1)}, u32[]{:S(2)}, u32[]{:S(2)}) collective-permute-start(bf16[256,1024]{1,0:T(8,128)(2,1)} %get-tuple-element.30), channel_id=1, source_target_pairs={{0,24},{8,16},{1,25},{9,17},{2,26},{10,18},{3,27},{11,19},{4,28},{... | collective-permute-start | bytes 1572872 | tf_op jit(solution)/shard_map/ppermute | solution.py:263
  33.8 10.5 %all-to-all-start.2 = ((bf16[8,16,1024]{2,1,0:T(8,128)(2,1)}), bf16[8,16,1024]{2,1,0:T(8,128)(2,1)S(1)}, u32[]{:S(2)}, u32[]{:S(2)}) async-start(bf16[8,16,1024]{2,1,0:T(8,128)(2,1)} %bitcast.4), calls=%async_computation.2 | async-start | bytes 524288 | tf_op jit(solution)/shard_map/all_to_all | solution.py:270
  44.3 1.6 %copy-start.1 = (bf16[1024,1024]{1,0:T(8,128)(2,1)S(1)}, bf16[1024,1024]{1,0:T(8,128)(2,1)}, u32[]{:S(2)}) copy-start(bf16[1024,1024]{1,0:T(8,128)(2,1)} %copy-done) | copy-start | bytes 6291460
  45.9 13.2 %copy-start.3 = (bf16[256,1024]{1,0:T(8,128)(2,1)S(1)}, bf16[256,1024]{1,0:T(8,128)(2,1)}, u32[]{:S(2)}) copy-start(bf16[256,1024]{1,0:T(8,128)(2,1)} %copy-done.2) | copy-start | bytes 1572868
  45.9 13.2 %copy-start.5 = (bf16[256,1024]{1,0:T(8,128)(2,1)S(1)}, bf16[256,1024]{1,0:T(8,128)(2,1)}, u32[]{:S(2)}) copy-start(bf16[256,1024]{1,0:T(8,128)(2,1)} %copy-done.4) | copy-start | bytes 1572868
  60.1 2.0 %collective-permute-start.3 = (bf16[256,1024]{1,0:T(8,128)(2,1)S(1)}, bf16[256,1024]{1,0:T(8,128)(2,1)S(1)}, u32[]{:S(2)}, u32[]{:S(2)}) collective-permute-start(bf16[256,1024]{1,0:T(8,128)(2,1)S(1)} %get-tuple-element.35), channel_id=1, source_target_pairs={{0,8},{8,0},{16,24},{24,16},{1,9},{9,1},{17,25},{25,17},{2,10},{10... | collective-permute-start | bytes 1572872 | tf_op jit(solution)/shard_map/ppermute | solution.py:257

commit v10 on v9

--- a/solution.py
+++ b/solution.py
@@ -169,8 +169,9 @@
     else:
         x_ref = take(1)[0]
         out_ref = take(1)[0] if not end else None
-        picked = take(group) if end else []
-        if todo == "all":
+        shifts = {"send": range(1, group), "keep": [0]}.get(todo, range(group))
+        picked = take(len(shifts)) if end else []
+        if todo != "rest":
             (mixed_ref,) = take(1)
 
     section = lax.axis_index("section")
@@ -207,6 +208,10 @@
     active = section // group == stage
     for shift in range(group):
         needed = active & ((member + shift) % group == step)
+        if todo == "send":
+            needed = needed & (member < group - 1)
+        if todo == "keep":
+            needed = needed & (member == group - 1)
         pl.when(needed)(functools.partial(body, weights[shift]))
 
     if end and todo != "rows":
@@ -221,13 +226,13 @@
 
             @pl.when(here)
             def _(value=value):
-                pick_from([layers[(value - by) % group] for by in range(group)])
+                pick_from([layers[(value - by) % group] for by in shifts])
 
         if old:
 
             @pl.when(~active)
             def _():
-                pick_from(old)
+                pick_from([old[by] for by in shifts])
 
 
 def write_kernel(group, shifts, *refs):
@@ -314,7 +319,8 @@
             scratch = []
         elif end:
             last = stage == stages - 1
-            outs = ([] if last else [(rows, width)]) + [(rows, width)] * group
+            count = {"send": group - 1, "keep": 1}.get(todo, group)
+            outs = ([] if last else [(rows, width)]) + [(rows, width)] * count
             if last:
                 scratch = [pltpu.VMEM((rows, width), bf16)] + scratch
         flops = 2 * width * rows * (2 * side + width) + 2 * width * rows * sent
@@ -327,7 +333,7 @@
             refs = list(refs)
             if end and todo != "rows" and stage == stages - 1:
                 place = len(operands)
-                x_ref = refs.pop(place + group)
+                x_ref = refs.pop(place + count)
                 refs.insert(place, x_ref)
             kernel(*refs)
 
@@ -364,9 +370,13 @@
             boundary = exchanged(outgoing)
         step = group - 1
         if stage == stages - 1:
-            picked = layer(
-                stage, step, "all", weights, [mix, init, boundary], earlier, current, picked
-            )
+            sending, keeping = [
+                functools.partial(
+                    layer, stage, step, todo, weights, [mix, init, boundary], earlier, current
+                )
+                for todo in ("send", "keep")
+            ]
+            to_send = sending(picked)
             break
         mixed, outgoing = layer(
             stage, step, "rows", weights, [mix, init, boundary, pick], current=current
@@ -378,28 +388,15 @@
         current = crossed(x)
         boundary = exchanged(rows_sent)
 
-    pieces = [shifted(picked[by], by) for by in range(1, group)]
-    shape = (1, batches, rows, width)
-    target = call(
-        functools.partial(write_kernel, group, [0]),
-        [shape],
-        [VMEM],
+    pieces = [shifted(piece, by) for by, piece in enumerate(to_send, 1)]
+    kept = keeping(picked)
+    return call(
+        functools.partial(write_kernel, group, range(group)),
+        [(1, batches, rows, width)],
+        [VMEM] * group,
         [HBM],
-        [pltpu.SemaphoreType.DMA((1,))],
-        cost=pl.CostEstimate(flops=0, bytes_accessed=4 * rows * width, transcendentals=0),
-    )(picked[0])[0]
-    if group == 1:
-        return target
-    return call(
-        lambda *refs: write_kernel(
-            group, range(1, group), *refs[: group - 1], *refs[group:]
-        ),
-        [shape],
-        [VMEM] * (group - 1) + [HBM],
-        [HBM],
-        [pltpu.SemaphoreType.DMA((group - 1,))],
-        aliases={group - 1: 0},
-    )(*pieces, target)[0]
+        [pltpu.SemaphoreType.DMA((group,))],
+    )(*kept, *pieces)[0]
 
 
 def solution(mesh):

time: 63.5 us -> 64.4 us (1.014)
  local copies, waits for them, and re-layouts: 3.22 us -> 3.96 us
  Pallas kernels: 12.9 us -> 12.2 us
    unnamed x12 -> x14, local copies, waits for them, and re-layouts: 3.22 us -> 3.96 us
    pallas_call x2 -> x1, Pallas kernels: 1.63 us -> 0.98 us  [on_device(): call(functools.partial(write_kernel, group, range(group)), [(1, batches,...]
    pallas_call x5 -> x6, Pallas kernels: 4.17 us -> 4.16 us  [layer(): call(reordered, outs, [VMEM] * len(operands), [VMEM] * len(outs), scratch...]
  transfers between devices with their start and end apart: 5 -> 5, of which waited for: 3 -> 4; matrix products, arithmetic and copies ran while one was open for 0% -> 0% of each run, Pallas kernels for 11% -> 11%
where the time goes in v10:
time: 64.4 us; the launch traced here: 63.7 us
  blocking collectives  28.6 us (44%)
  Pallas kernels  12.2 us (19%)
  waiting for transfers between devices  9.95 us (15%)
  starting transfers between devices  8.92 us (14%)
  local copies, waits for them, and re-layouts  3.96 us (6%)
    all_to_all x3, blocking collectives, exchanged(): lax.all_to_all(x, ('section', 'dom'), split_axis=0, concat_axis=0, axis_i...  28.6 us
    ppermute x2, waiting for transfers between devices, crossed(): return lax.ppermute(x, 'section', pairs)  8.47 us
    all_to_all x1, starting transfers between devices, exchanged(): lax.all_to_all(x, ('section', 'dom'), split_axis=0, concat_axis=0, axis_i...  5.55 us
    pallas_call x1, Pallas kernels, on_device(): call(functools.partial(hold_kernel, group), [(sent, width)], [VMEM, HBM],...  5.21 us
    pallas_call x6, Pallas kernels, layer(): call(reordered, outs, [VMEM] * len(operands), [VMEM] * len(outs), scratch...  4.16 us
    unnamed x14, local copies, waits for them, and re-layouts  3.96 us
    ppermute x2, starting transfers between devices, crossed(): return lax.ppermute(x, 'section', pairs)  2.56 us
    pallas_call x1, Pallas kernels, first(): call(functools.partial(first_kernel, group), [(sent, width), (sent, rows)...  1.86 us
  transfers between devices with their start and end apart: 5, of which 4 were waited for; matrix products, arithmetic and copies ran while one was open for 0% of the time, Pallas kernels for 11%

profile of v10, /device:TPU:5, one launch (start us, length us, event | category | flops | bytes accessed | tf_op | source)
XLA Modules:
  0.0 63.7 jit_solution(5596927739924813863)
XLA Ops:
  0.0 1.9 %shard_map.55 = (bf16[128,1024]{1,0:T(8,128)(2,1)S(1)}, bf16[128,256]{1,0:T(8,128)(2,1)S(1)}, bf16[2,128,256]{2,1,0:T(8,128)(2,1)S(1)}, bf16[256,1024]{1,0:T(8,128)(2,1)S(1)}, bf16[1024,1024]{1,0:T(8,128)(2,1)S(1)}) custom-call(s32[1,2,8,16]{3,2,1,0:T(8,128)} %send_hbm.1, s32[1,2,2,4]{3,2,1,0:T(2,128)} %block_hbm.1, bf16[2,256,1024]{2,1,0:T(8,128)(2,1)} %init_hbm.1, ...), custom_call_target="tpu_custom_call" | custom-call | tf_op jit(solution)/shard_map/pallas_call | solution.py:286
  1.9 0.0 copy-start.4
  1.9 0.7 %collective-permute-start = (bf16[1024,1024]{1,0:T(8,128)(2,1)S(1)}, bf16[1024,1024]{1,0:T(8,128)(2,1)S(1)}, u32[]{:S(2)}, u32[]{:S(2)}) collective-permute-start(bf16[1024,1024]{1,0:T(8,128)(2,1)S(1)} %get-tuple-element.19.refs_0_), channel_id=1, source_target_pairs={{0,8},{8,0},{16,24},{24,16},{1,9},{9,1},{17,25},{25,17},{2,10},{10... | collective-permute-start | bytes 6291464 | tf_op jit(solution)/shard_map/ppermute | solution.py:262
  2.6 5.2 %shard_map.56 = bf16[128,1024]{1,0:T(8,128)(2,1)S(1)} custom-call(bf16[128,1024]{1,0:T(8,128)(2,1)S(1)} %get-tuple-element.22.rows_ref, bf16[1,1024,1024]{2,1,0:T(8,128)(2,1)} %weight_hbm.3), custom_call_target="tpu_custom_call", output_to_operand_aliasing={{}: (0, {})} | custom-call | tf_op jit(solution)/shard_map/pallas_call | solution.py:351
  7.8 9.0 %all_to_all.44 = bf16[8,16,1024]{2,1,0:T(8,128)(2,1)S(1)} all-to-all(bf16[8,16,1024]{2,1,0:T(8,128)(2,1)S(1)} %bitcast.11), channel_id=1, replica_groups={{5,0,6,2,1,4,3,7},{13,8,14,10,9,12,11,15},{21,16,22,18,17,20,19,23},{29..., dimensions={0} | all-to-all | bytes 524288 | tf_op jit(solution)/shard_map/all_to_all | solution.py:275
  16.9 0.0 collective-permute-done.refs_1_
  16.9 0.0 copy-start
  16.9 8.4 %all_to_all.45 = bf16[8,16,1024]{2,1,0:T(8,128)(2,1)S(1)} all-to-all(bf16[8,16,1024]{2,1,0:T(8,128)(2,1)S(1)} %bitcast.15), channel_id=1, replica_groups={{5,0,6,2,1,4,3,7},{13,8,14,10,9,12,11,15},{21,16,22,18,17,20,19,23},{29..., dimensions={0} | all-to-all | bytes 524288 | tf_op jit(solution)/shard_map/all_to_all | solution.py:275
  25.3 0.0 copy-done.4
  25.3 1.3 %collective-permute-start.1 = (bf16[128,1024]{1,0:T(8,128)(2,1)S(1)}, bf16[128,1024]{1,0:T(8,128)(2,1)S(1)}, u32[]{:S(2)}, u32[]{:S(2)}) collective-permute-start(bf16[128,1024]{1,0:T(8,128)(2,1)S(1)} %get-tuple-element.26), channel_id=1, source_target_pairs={{0,24},{8,16},{1,25},{9,17},{2,26},{10,18},{3,27},{11,19},{4,28},{... | collective-permute-start | bytes 786440 | tf_op jit(solution)/shard_map/ppermute | solution.py:268
  26.6 0.0 copy-done
  26.6 0.9 %shard_map.59 = (bf16[256,1024]{1,0:T(8,128)(2,1)}, bf16[256,1024]{1,0:T(8,128)(2,1)S(1)}, bf16[256,1024]{1,0:T(8,128)(2,1)S(1)}) custom-call(bf16[1024,1024]{1,0:T(8,128)(2,1)S(1)} %get-tuple-element.19.refs_0_, bf16[1024,1024]{1,0:T(8,128)(2,1)S(1)} %collective-permute-done.refs_1_, bf16[256,1024]{1,0:T(8,128)(2,1)S(1)} %get-tuple-element.27.refs_2_, ...), custom_call_target="tpu_custom_call" | custom-call | flops 738197504 | bytes 3670016 | tf_op jit(solution)/shard_map/pallas_call | solution.py:340
  27.5 0.0 copy-start.2
  27.5 0.8 %copy-done.2 = bf16[256,1024]{1,0:T(8,128)(2,1)} copy-done((bf16[256,1024]{1,0:T(8,128)(2,1)}, bf16[256,1024]{1,0:T(8,128)(2,1)S(1)}, u32[]{:S(2)}) %copy-start.2) | copy-done | bytes 524312
  28.3 1.3 %collective-permute-start.2 = (bf16[256,1024]{1,0:T(8,128)(2,1)}, bf16[256,1024]{1,0:T(8,128)(2,1)}, u32[]{:S(2)}, u32[]{:S(2)}) collective-permute-start(bf16[256,1024]{1,0:T(8,128)(2,1)} %get-tuple-element.28), channel_id=1, source_target_pairs={{0,24},{8,16},{1,25},{9,17},{2,26},{10,18},{3,27},{11,19},{4,28},{... | collective-permute-start | bytes 1572872 | tf_op jit(solution)/shard_map/ppermute | solution.py:268
  29.6 5.6 %collective-permute-done.1 = bf16[128,1024]{1,0:T(8,128)(2,1)S(1)} collective-permute-done((bf16[128,1024]{1,0:T(8,128)(2,1)S(1)}, bf16[128,1024]{1,0:T(8,128)(2,1)S(1)}, u32[]{:S(2)}, u32[]{:S(2)}) %collective-permute-start.1) | collective-permute-done | bytes 262176 | tf_op jit(solution)/shard_map/ppermute | solution.py:268
  35.2 0.0 copy-start.6
  35.2 0.7 %copy-done.6 = bf16[128,1024]{1,0:T(8,128)(2,1)} copy-done((bf16[128,1024]{1,0:T(8,128)(2,1)}, bf16[128,1024]{1,0:T(8,128)(2,1)S(1)}, u32[]{:S(2)}) %copy-start.6) | copy-done | bytes 262168
  35.9 5.5 %all-to-all-start.2 = ((bf16[8,16,1024]{2,1,0:T(8,128)(2,1)}), bf16[8,16,1024]{2,1,0:T(8,128)(2,1)S(1)}, u32[]{:S(2)}, u32[]{:S(2)}) async-start(bf16[8,16,1024]{2,1,0:T(8,128)(2,1)} %bitcast.16), calls=%async_computation.2 | async-start | bytes 524288 | tf_op jit(solution)/shard_map/all_to_all | solution.py:275
  41.5 2.8 %collective-permute-done.2.refs_6_ = bf16[256,1024]{1,0:T(8,128)(2,1)} collective-permute-done((bf16[256,1024]{1,0:T(8,128)(2,1)}, bf16[256,1024]{1,0:T(8,128)(2,1)}, u32[]{:S(2)}, u32[]{:S(2)}) %collective-permute-start.2) | collective-permute-done | bytes 524320 | tf_op jit(solution)/shard_map/ppermute | solution.py:268
  44.3 0.6 all-to-all-done.2
  44.9 0.0 copy-start.1
  44.9 1.6 %copy-done.1 = bf16[1024,1024]{1,0:T(8,128)(2,1)S(1)} copy-done((bf16[1024,1024]{1,0:T(8,128)(2,1)S(1)}, bf16[1024,1024]{1,0:T(8,128)(2,1)}, u32[]{:S(2)}) %copy-start.1) | copy-done | bytes 2097176
  46.5 0.0 copy-start.5
  46.5 0.8 %copy-done.5 = bf16[128,256]{1,0:T(8,128)(2,1)S(1)} copy-done((bf16[128,256]{1,0:T(8,128)(2,1)S(1)}, bf16[128,256]{1,0:T(8,128)(2,1)}, u32[]{:S(2)}) %copy-start.5) | copy-done | bytes 65560
  47.3 0.0 copy-start.3
  47.3 2.2 %shard_map.60 = (bf16[256,1024]{1,0:T(8,128)(2,1)S(1)}, bf16[128,1024]{1,0:T(8,128)(2,1)S(1)}) custom-call(bf16[1024,1024]{1,0:T(8,128)(2,1)S(1)} %get-tuple-element.19.refs_0_, bf16[1024,1024]{1,0:T(8,128)(2,1)S(1)} %copy-done.1, bf16[2,128,256]{2,1,0:T(8,128)(2,1)S(1)} %get-tuple-element.20.refs_2_, bf16[256,1024]{1,0:T(8,128)(2,1)S(1)} %get-tuple-element.21.refs_3_, ...), custom_call_target="tpu_custom_call" | custom-call | flops 738197504 | bytes 3670016 | tf_op jit(solution)/shard_map/pallas_call | solution.py:340
  49.6 11.2 %all_to_all.46 = bf16[8,16,1024]{2,1,0:T(8,128)(2,1)S(1)} all-to-all(bf16[8,16,1024]{2,1,0:T(8,128)(2,1)S(1)} %bitcast.14), channel_id=1, replica_groups={{5,0,6,2,1,4,3,7},{13,8,14,10,9,12,11,15},{21,16,22,18,17,20,19,23},{29..., dimensions={0} | all-to-all | bytes 524288 | tf_op jit(solution)/shard_map/all_to_all | solution.py:275
  60.7 0.0 copy-done.3
  60.8 0.1 collective-permute-start.3
  60.8 1.0 %shard_map.61.refs_0_ = bf16[256,1024]{1,0:T(8,128)(2,1)S(1)} custom-call(bf16[1024,1024]{1,0:T(8,128)(2,1)S(1)} %get-tuple-element.19.refs_0_, bf16[1024,1024]{1,0:T(8,128)(2,1)S(1)} %copy-done.1, bf16[2,128,256]{2,1,0:T(8,128)(2,1)S(1)} %get-tuple-element.20.refs_2_, bf16[256,1024]{1,0:T(8,128)(2,1)S(1)} %get-tuple-element.21.refs_3_, ...), custom_call_target="tpu_custom_call" | custom-call | flops 738197504 | bytes 3670016 | tf_op jit(solution)/shard_map/pallas_call | solution.py:340
  61.9 0.9 %collective-permute-done.3.refs_1_ = bf16[256,1024]{1,0:T(8,128)(2,1)S(1)} collective-permute-done((bf16[256,1024]{1,0:T(8,128)(2,1)S(1)}, bf16[256,1024]{1,0:T(8,128)(2,1)S(1)}, u32[]{:S(2)}, u32[]{:S(2)}) %collective-permute-start.3) | collective-permute-done | bytes 524320 | tf_op jit(solution)/shard_map/ppermute | solution.py:262
  62.7 1.0 %shard_map.63 = bf16[1,2,256,1024]{3,2,1,0:T(8,128)(2,1)} custom-call(bf16[256,1024]{1,0:T(8,128)(2,1)S(1)} %shard_map.61.refs_0_, bf16[256,1024]{1,0:T(8,128)(2,1)S(1)} %collective-permute-done.3.refs_1_), custom_call_target="tpu_custom_call" | custom-call | tf_op jit(solution)/shard_map/pallas_call | solution.py:393
  (3 shorter events, 0.0 us)
Async XLA Ops:
  1.9 23.4 %copy-start.4 = (bf16[128,256]{1,0:T(8,128)(2,1)}, bf16[128,256]{1,0:T(8,128)(2,1)S(1)}, u32[]{:S(2)}) copy-start(bf16[128,256]{1,0:T(8,128)(2,1)S(1)} %get-tuple-element.23.refs_5_) | copy-start | bytes 196612
  1.9 15.0 %collective-permute-start = (bf16[1024,1024]{1,0:T(8,128)(2,1)S(1)}, bf16[1024,1024]{1,0:T(8,128)(2,1)S(1)}, u32[]{:S(2)}, u32[]{:S(2)}) collective-permute-start(bf16[1024,1024]{1,0:T(8,128)(2,1)S(1)} %get-tuple-element.19.refs_0_), channel_id=1, source_target_pairs={{0,8},{8,0},{16,24},{24,16},{1,9},{9,1},{17,25},{25,17},{2,10},{10... | collective-permute-start | bytes 6291464 | tf_op jit(solution)/shard_map/ppermute | solution.py:262
  16.9 9.7 %copy-start = (bf16[1024,1024]{1,0:T(8,128)(2,1)}, bf16[1024,1024]{1,0:T(8,128)(2,1)S(1)}, u32[]{:S(2)}) copy-start(bf16[1024,1024]{1,0:T(8,128)(2,1)S(1)} %collective-permute-done.refs_1_) | copy-start | bytes 6291460
  25.3 10.0 %collective-permute-start.1 = (bf16[128,1024]{1,0:T(8,128)(2,1)S(1)}, bf16[128,1024]{1,0:T(8,128)(2,1)S(1)}, u32[]{:S(2)}, u32[]{:S(2)}) collective-permute-start(bf16[128,1024]{1,0:T(8,128)(2,1)S(1)} %get-tuple-element.26), channel_id=1, source_target_pairs={{0,24},{8,16},{1,25},{9,17},{2,26},{10,18},{3,27},{11,19},{4,28},{... | collective-permute-start | bytes 786440 | tf_op jit(solution)/shard_map/ppermute | solution.py:268
  27.5 0.8 %copy-start.2 = (bf16[256,1024]{1,0:T(8,128)(2,1)}, bf16[256,1024]{1,0:T(8,128)(2,1)S(1)}, u32[]{:S(2)}) copy-start(bf16[256,1024]{1,0:T(8,128)(2,1)S(1)} %get-tuple-element.32.refs_8_) | copy-start | bytes 1572868
  28.3 16.0 %collective-permute-start.2 = (bf16[256,1024]{1,0:T(8,128)(2,1)}, bf16[256,1024]{1,0:T(8,128)(2,1)}, u32[]{:S(2)}, u32[]{:S(2)}) collective-permute-start(bf16[256,1024]{1,0:T(8,128)(2,1)} %get-tuple-element.28), channel_id=1, source_target_pairs={{0,24},{8,16},{1,25},{9,17},{2,26},{10,18},{3,27},{11,19},{4,28},{... | collective-permute-start | bytes 1572872 | tf_op jit(solution)/shard_map/ppermute | solution.py:268
  35.2 0.7 %copy-start.6 = (bf16[128,1024]{1,0:T(8,128)(2,1)}, bf16[128,1024]{1,0:T(8,128)(2,1)S(1)}, u32[]{:S(2)}) copy-start(bf16[128,1024]{1,0:T(8,128)(2,1)S(1)} %collective-permute-done.1) | copy-start | bytes 786436
  35.9 9.0 %all-to-all-start.2 = ((bf16[8,16,1024]{2,1,0:T(8,128)(2,1)}), bf16[8,16,1024]{2,1,0:T(8,128)(2,1)S(1)}, u32[]{:S(2)}, u32[]{:S(2)}) async-start(bf16[8,16,1024]{2,1,0:T(8,128)(2,1)} %bitcast.16), calls=%async_computation.2 | async-start | bytes 524288 | tf_op jit(solution)/shard_map/all_to_all | solution.py:275
  44.9 1.6 %copy-start.1 = (bf16[1024,1024]{1,0:T(8,128)(2,1)S(1)}, bf16[1024,1024]{1,0:T(8,128)(2,1)}, u32[]{:S(2)}) copy-start(bf16[1024,1024]{1,0:T(8,128)(2,1)} %copy-done) | copy-start | bytes 6291460
  46.5 0.8 %copy-start.5 = (bf16[128,256]{1,0:T(8,128)(2,1)S(1)}, bf16[128,256]{1,0:T(8,128)(2,1)}, u32[]{:S(2)}) copy-start(bf16[128,256]{1,0:T(8,128)(2,1)} %copy-done.4) | copy-start | bytes 196612
  47.3 13.4 %copy-start.3 = (bf16[256,1024]{1,0:T(8,128)(2,1)S(1)}, bf16[256,1024]{1,0:T(8,128)(2,1)}, u32[]{:S(2)}) copy-start(bf16[256,1024]{1,0:T(8,128)(2,1)} %copy-done.2) | copy-start | bytes 1572868
  60.8 2.0 %collective-permute-start.3 = (bf16[256,1024]{1,0:T(8,128)(2,1)S(1)}, bf16[256,1024]{1,0:T(8,128)(2,1)S(1)}, u32[]{:S(2)}, u32[]{:S(2)}) collective-permute-start(bf16[256,1024]{1,0:T(8,128)(2,1)S(1)} %shard_map.62), channel_id=1, source_target_pairs={{0,8},{8,0},{16,24},{24,16},{1,9},{9,1},{17,25},{25,17},{2,10},{10... | collective-permute-start | bytes 1572872 | tf_op jit(solution)/shard_map/ppermute | solution.py:262

commit v11 on v10

--- a/solution.py
+++ b/solution.py
@@ -390,13 +390,24 @@
 
     pieces = [shifted(piece, by) for by, piece in enumerate(to_send, 1)]
     kept = keeping(picked)
+    shape = (1, batches, rows, width)
+    target = call(
+        functools.partial(write_kernel, group, [0]),
+        [shape],
+        [VMEM],
+        [HBM],
+        [pltpu.SemaphoreType.DMA((1,))],
+    )(*kept)[0]
     return call(
-        functools.partial(write_kernel, group, range(group)),
-        [(1, batches, rows, width)],
-        [VMEM] * group,
+        lambda *refs: write_kernel(
+            group, range(1, group), *refs[: group - 1], *refs[group:]
+        ),
+        [shape],
+        [VMEM] * (group - 1) + [HBM],
         [HBM],
-        [pltpu.SemaphoreType.DMA((group,))],
-    )(*kept, *pieces)[0]
+        [pltpu.SemaphoreType.DMA((group - 1,))],
+        aliases={group - 1: 0},
+    )(*pieces, target)[0]
 
 
 def solution(mesh):

time: 64.4 us -> 64.2 us (level)
  waiting for transfers between devices: 9.95 us -> 9.12 us
  Pallas kernels: 12.2 us -> 12.9 us
    ppermute x2, waiting for transfers between devices: 0.87 us -> 0.04 us  [shifted(): return lax.ppermute(x, 'section', pairs)]
    pallas_call x1 -> x2, Pallas kernels: 0.98 us -> 1.63 us  [the longest x1 0.83 us: on_device(): call(functools.partial(write_kernel, group, [0]), [shape], [VMEM], [HBM],...]
  transfers between devices with their start and end apart: 5 -> 5, of which waited for: 4 -> 3; matrix products, arithmetic and copies ran while one was open for 0% -> 0% of each run, Pallas kernels for 11% -> 13%
where the time goes in v11:
time: 64.2 us; the launch traced here: 63.5 us
  blocking collectives  28.6 us (45%)
  Pallas kernels  12.9 us (20%)
  waiting for transfers between devices  9.12 us (14%)
  starting transfers between devices  8.92 us (14%)
  local copies, waits for them, and re-layouts  3.96 us (6%)
    all_to_all x3, blocking collectives, exchanged(): lax.all_to_all(x, ('section', 'dom'), split_axis=0, concat_axis=0, axis_i...  28.6 us
    ppermute x2, waiting for transfers between devices, crossed(): return lax.ppermute(x, 'section', pairs)  8.47 us
    all_to_all x1, starting transfers between devices, exchanged(): lax.all_to_all(x, ('section', 'dom'), split_axis=0, concat_axis=0, axis_i...  5.55 us
    pallas_call x1, Pallas kernels, on_device(): call(functools.partial(hold_kernel, group), [(sent, width)], [VMEM, HBM],...  5.21 us
    pallas_call x6, Pallas kernels, layer(): call(reordered, outs, [VMEM] * len(operands), [VMEM] * len(outs), scratch...  4.16 us
    unnamed x14, local copies, waits for them, and re-layouts  3.96 us
    ppermute x2, starting transfers between devices, crossed(): return lax.ppermute(x, 'section', pairs)  2.56 us
    pallas_call x1, Pallas kernels, first(): call(functools.partial(first_kernel, group), [(sent, width), (sent, rows)...  1.86 us
  transfers between devices with their start and end apart: 5, of which 3 were waited for; matrix products, arithmetic and copies ran while one was open for 0% of the time, Pallas kernels for 13%

profile of v11, /device:TPU:5, one launch (start us, length us, event | category | flops | bytes accessed | tf_op | source)
XLA Modules:
  0.0 63.5 jit_solution(8282661062299238472)
XLA Ops:
  0.0 1.9 %shard_map.55 = (bf16[128,1024]{1,0:T(8,128)(2,1)S(1)}, bf16[128,256]{1,0:T(8,128)(2,1)S(1)}, bf16[2,128,256]{2,1,0:T(8,128)(2,1)S(1)}, bf16[256,1024]{1,0:T(8,128)(2,1)S(1)}, bf16[1024,1024]{1,0:T(8,128)(2,1)S(1)}) custom-call(s32[1,2,8,16]{3,2,1,0:T(8,128)} %send_hbm.1, s32[1,2,2,4]{3,2,1,0:T(2,128)} %block_hbm.1, bf16[2,256,1024]{2,1,0:T(8,128)(2,1)} %init_hbm.1, ...), custom_call_target="tpu_custom_call" | custom-call | tf_op jit(solution)/shard_map/pallas_call | solution.py:286
  1.9 0.0 copy-start.4
  1.9 0.7 %collective-permute-start = (bf16[1024,1024]{1,0:T(8,128)(2,1)S(1)}, bf16[1024,1024]{1,0:T(8,128)(2,1)S(1)}, u32[]{:S(2)}, u32[]{:S(2)}) collective-permute-start(bf16[1024,1024]{1,0:T(8,128)(2,1)S(1)} %get-tuple-element.19.refs_0_), channel_id=1, source_target_pairs={{0,8},{8,0},{16,24},{24,16},{1,9},{9,1},{17,25},{25,17},{2,10},{10... | collective-permute-start | bytes 6291464 | tf_op jit(solution)/shard_map/ppermute | solution.py:262
  2.6 5.2 %shard_map.56 = bf16[128,1024]{1,0:T(8,128)(2,1)S(1)} custom-call(bf16[128,1024]{1,0:T(8,128)(2,1)S(1)} %get-tuple-element.22.rows_ref, bf16[1,1024,1024]{2,1,0:T(8,128)(2,1)} %weight_hbm.3), custom_call_target="tpu_custom_call", output_to_operand_aliasing={{}: (0, {})} | custom-call | tf_op jit(solution)/shard_map/pallas_call | solution.py:351
  7.8 9.0 %all_to_all.44 = bf16[8,16,1024]{2,1,0:T(8,128)(2,1)S(1)} all-to-all(bf16[8,16,1024]{2,1,0:T(8,128)(2,1)S(1)} %bitcast.11), channel_id=1, replica_groups={{5,0,6,2,1,4,3,7},{13,8,14,10,9,12,11,15},{21,16,22,18,17,20,19,23},{29..., dimensions={0} | all-to-all | bytes 524288 | tf_op jit(solution)/shard_map/all_to_all | solution.py:275
  16.9 0.0 collective-permute-done.refs_1_
  16.9 0.0 copy-start
  16.9 8.4 %all_to_all.45 = bf16[8,16,1024]{2,1,0:T(8,128)(2,1)S(1)} all-to-all(bf16[8,16,1024]{2,1,0:T(8,128)(2,1)S(1)} %bitcast.15), channel_id=1, replica_groups={{5,0,6,2,1,4,3,7},{13,8,14,10,9,12,11,15},{21,16,22,18,17,20,19,23},{29..., dimensions={0} | all-to-all | bytes 524288 | tf_op jit(solution)/shard_map/all_to_all | solution.py:275
  25.3 0.0 copy-done.4
  25.3 1.3 %collective-permute-start.1 = (bf16[128,1024]{1,0:T(8,128)(2,1)S(1)}, bf16[128,1024]{1,0:T(8,128)(2,1)S(1)}, u32[]{:S(2)}, u32[]{:S(2)}) collective-permute-start(bf16[128,1024]{1,0:T(8,128)(2,1)S(1)} %get-tuple-element.26), channel_id=1, source_target_pairs={{0,24},{8,16},{1,25},{9,17},{2,26},{10,18},{3,27},{11,19},{4,28},{... | collective-permute-start | bytes 786440 | tf_op jit(solution)/shard_map/ppermute | solution.py:268
  26.6 0.0 copy-done
  26.6 0.9 %shard_map.59 = (bf16[256,1024]{1,0:T(8,128)(2,1)}, bf16[256,1024]{1,0:T(8,128)(2,1)S(1)}, bf16[256,1024]{1,0:T(8,128)(2,1)S(1)}) custom-call(bf16[1024,1024]{1,0:T(8,128)(2,1)S(1)} %get-tuple-element.19.refs_0_, bf16[1024,1024]{1,0:T(8,128)(2,1)S(1)} %collective-permute-done.refs_1_, bf16[256,1024]{1,0:T(8,128)(2,1)S(1)} %get-tuple-element.27.refs_2_, ...), custom_call_target="tpu_custom_call" | custom-call | flops 738197504 | bytes 3670016 | tf_op jit(solution)/shard_map/pallas_call | solution.py:340
  27.5 0.0 copy-start.2
  27.5 0.8 %copy-done.2 = bf16[256,1024]{1,0:T(8,128)(2,1)} copy-done((bf16[256,1024]{1,0:T(8,128)(2,1)}, bf16[256,1024]{1,0:T(8,128)(2,1)S(1)}, u32[]{:S(2)}) %copy-start.2) | copy-done | bytes 524312
  28.3 1.3 %collective-permute-start.2 = (bf16[256,1024]{1,0:T(8,128)(2,1)}, bf16[256,1024]{1,0:T(8,128)(2,1)}, u32[]{:S(2)}, u32[]{:S(2)}) collective-permute-start(bf16[256,1024]{1,0:T(8,128)(2,1)} %get-tuple-element.28), channel_id=1, source_target_pairs={{0,24},{8,16},{1,25},{9,17},{2,26},{10,18},{3,27},{11,19},{4,28},{... | collective-permute-start | bytes 1572872 | tf_op jit(solution)/shard_map/ppermute | solution.py:268
  29.6 5.6 %collective-permute-done.1 = bf16[128,1024]{1,0:T(8,128)(2,1)S(1)} collective-permute-done((bf16[128,1024]{1,0:T(8,128)(2,1)S(1)}, bf16[128,1024]{1,0:T(8,128)(2,1)S(1)}, u32[]{:S(2)}, u32[]{:S(2)}) %collective-permute-start.1) | collective-permute-done | bytes 262176 | tf_op jit(solution)/shard_map/ppermute | solution.py:268
  35.2 0.0 copy-start.6
  35.2 0.7 %copy-done.6 = bf16[128,1024]{1,0:T(8,128)(2,1)} copy-done((bf16[128,1024]{1,0:T(8,128)(2,1)}, bf16[128,1024]{1,0:T(8,128)(2,1)S(1)}, u32[]{:S(2)}) %copy-start.6) | copy-done | bytes 262168
  35.9 5.5 %all-to-all-start.2 = ((bf16[8,16,1024]{2,1,0:T(8,128)(2,1)}), bf16[8,16,1024]{2,1,0:T(8,128)(2,1)S(1)}, u32[]{:S(2)}, u32[]{:S(2)}) async-start(bf16[8,16,1024]{2,1,0:T(8,128)(2,1)} %bitcast.16), calls=%async_computation.2 | async-start | bytes 524288 | tf_op jit(solution)/shard_map/all_to_all | solution.py:275
  41.5 2.8 %collective-permute-done.2.refs_6_ = bf16[256,1024]{1,0:T(8,128)(2,1)} collective-permute-done((bf16[256,1024]{1,0:T(8,128)(2,1)}, bf16[256,1024]{1,0:T(8,128)(2,1)}, u32[]{:S(2)}, u32[]{:S(2)}) %collective-permute-start.2) | collective-permute-done | bytes 524320 | tf_op jit(solution)/shard_map/ppermute | solution.py:268
  44.3 0.6 all-to-all-done.2
  44.9 0.0 copy-start.1
  44.9 1.6 %copy-done.1 = bf16[1024,1024]{1,0:T(8,128)(2,1)S(1)} copy-done((bf16[1024,1024]{1,0:T(8,128)(2,1)S(1)}, bf16[1024,1024]{1,0:T(8,128)(2,1)}, u32[]{:S(2)}) %copy-start.1) | copy-done | bytes 2097176
  46.5 0.0 copy-start.5
  46.5 0.8 %copy-done.5 = bf16[128,256]{1,0:T(8,128)(2,1)S(1)} copy-done((bf16[128,256]{1,0:T(8,128)(2,1)S(1)}, bf16[128,256]{1,0:T(8,128)(2,1)}, u32[]{:S(2)}) %copy-start.5) | copy-done | bytes 65560
  47.3 0.0 copy-start.3
  47.3 2.2 %shard_map.60 = (bf16[256,1024]{1,0:T(8,128)(2,1)S(1)}, bf16[128,1024]{1,0:T(8,128)(2,1)S(1)}) custom-call(bf16[1024,1024]{1,0:T(8,128)(2,1)S(1)} %get-tuple-element.19.refs_0_, bf16[1024,1024]{1,0:T(8,128)(2,1)S(1)} %copy-done.1, bf16[2,128,256]{2,1,0:T(8,128)(2,1)S(1)} %get-tuple-element.20.refs_2_, bf16[256,1024]{1,0:T(8,128)(2,1)S(1)} %get-tuple-element.21.refs_3_, ...), custom_call_target="tpu_custom_call" | custom-call | flops 738197504 | bytes 3670016 | tf_op jit(solution)/shard_map/pallas_call | solution.py:340
  49.6 11.2 %all_to_all.46 = bf16[8,16,1024]{2,1,0:T(8,128)(2,1)S(1)} all-to-all(bf16[8,16,1024]{2,1,0:T(8,128)(2,1)S(1)} %bitcast.14), channel_id=1, replica_groups={{5,0,6,2,1,4,3,7},{13,8,14,10,9,12,11,15},{21,16,22,18,17,20,19,23},{29..., dimensions={0} | all-to-all | bytes 524288 | tf_op jit(solution)/shard_map/all_to_all | solution.py:275
  60.7 0.0 copy-done.3
  60.8 0.1 collective-permute-start.3
  60.8 1.0 %shard_map.62.refs_0_ = bf16[256,1024]{1,0:T(8,128)(2,1)S(1)} custom-call(bf16[1024,1024]{1,0:T(8,128)(2,1)S(1)} %get-tuple-element.19.refs_0_, bf16[1024,1024]{1,0:T(8,128)(2,1)S(1)} %copy-done.1, bf16[2,128,256]{2,1,0:T(8,128)(2,1)S(1)} %get-tuple-element.20.refs_2_, bf16[256,1024]{1,0:T(8,128)(2,1)S(1)} %get-tuple-element.21.refs_3_, ...), custom_call_target="tpu_custom_call" | custom-call | flops 738197504 | bytes 3670016 | tf_op jit(solution)/shard_map/pallas_call | solution.py:340
  61.9 0.8 %shard_map.63.refs_1_ = bf16[1,2,256,1024]{3,2,1,0:T(8,128)(2,1)} custom-call(bf16[256,1024]{1,0:T(8,128)(2,1)S(1)} %shard_map.62.refs_0_), custom_call_target="tpu_custom_call" | custom-call | tf_op jit(solution)/shard_map/pallas_call | solution.py:394
  62.7 0.0 collective-permute-done.3.refs_0_
  62.7 0.8 %shard_map.64 = bf16[1,2,256,1024]{3,2,1,0:T(8,128)(2,1)} custom-call(bf16[256,1024]{1,0:T(8,128)(2,1)S(1)} %collective-permute-done.3.refs_0_, bf16[1,2,256,1024]{3,2,1,0:T(8,128)(2,1)} %shard_map.63.refs_1_), custom_call_target="tpu_custom_call", output_to_operand_aliasing={{}: (1, {})} | custom-call | tf_op jit(solution)/shard_map/pallas_call | solution.py:401
  (3 shorter events, 0.0 us)
Async XLA Ops:
  1.9 23.4 %copy-start.4 = (bf16[128,256]{1,0:T(8,128)(2,1)}, bf16[128,256]{1,0:T(8,128)(2,1)S(1)}, u32[]{:S(2)}) copy-start(bf16[128,256]{1,0:T(8,128)(2,1)S(1)} %get-tuple-element.23.refs_5_) | copy-start | bytes 196612
  1.9 15.0 %collective-permute-start = (bf16[1024,1024]{1,0:T(8,128)(2,1)S(1)}, bf16[1024,1024]{1,0:T(8,128)(2,1)S(1)}, u32[]{:S(2)}, u32[]{:S(2)}) collective-permute-start(bf16[1024,1024]{1,0:T(8,128)(2,1)S(1)} %get-tuple-element.19.refs_0_), channel_id=1, source_target_pairs={{0,8},{8,0},{16,24},{24,16},{1,9},{9,1},{17,25},{25,17},{2,10},{10... | collective-permute-start | bytes 6291464 | tf_op jit(solution)/shard_map/ppermute | solution.py:262
  16.9 9.7 %copy-start = (bf16[1024,1024]{1,0:T(8,128)(2,1)}, bf16[1024,1024]{1,0:T(8,128)(2,1)S(1)}, u32[]{:S(2)}) copy-start(bf16[1024,1024]{1,0:T(8,128)(2,1)S(1)} %collective-permute-done.refs_1_) | copy-start | bytes 6291460
  25.3 10.0 %collective-permute-start.1 = (bf16[128,1024]{1,0:T(8,128)(2,1)S(1)}, bf16[128,1024]{1,0:T(8,128)(2,1)S(1)}, u32[]{:S(2)}, u32[]{:S(2)}) collective-permute-start(bf16[128,1024]{1,0:T(8,128)(2,1)S(1)} %get-tuple-element.26), channel_id=1, source_target_pairs={{0,24},{8,16},{1,25},{9,17},{2,26},{10,18},{3,27},{11,19},{4,28},{... | collective-permute-start | bytes 786440 | tf_op jit(solution)/shard_map/ppermute | solution.py:268
  27.5 0.8 %copy-start.2 = (bf16[256,1024]{1,0:T(8,128)(2,1)}, bf16[256,1024]{1,0:T(8,128)(2,1)S(1)}, u32[]{:S(2)}) copy-start(bf16[256,1024]{1,0:T(8,128)(2,1)S(1)} %get-tuple-element.32.refs_8_) | copy-start | bytes 1572868
  28.3 16.0 %collective-permute-start.2 = (bf16[256,1024]{1,0:T(8,128)(2,1)}, bf16[256,1024]{1,0:T(8,128)(2,1)}, u32[]{:S(2)}, u32[]{:S(2)}) collective-permute-start(bf16[256,1024]{1,0:T(8,128)(2,1)} %get-tuple-element.28), channel_id=1, source_target_pairs={{0,24},{8,16},{1,25},{9,17},{2,26},{10,18},{3,27},{11,19},{4,28},{... | collective-permute-start | bytes 1572872 | tf_op jit(solution)/shard_map/ppermute | solution.py:268
  35.2 0.7 %copy-start.6 = (bf16[128,1024]{1,0:T(8,128)(2,1)}, bf16[128,1024]{1,0:T(8,128)(2,1)S(1)}, u32[]{:S(2)}) copy-start(bf16[128,1024]{1,0:T(8,128)(2,1)S(1)} %collective-permute-done.1) | copy-start | bytes 786436
  35.9 9.0 %all-to-all-start.2 = ((bf16[8,16,1024]{2,1,0:T(8,128)(2,1)}), bf16[8,16,1024]{2,1,0:T(8,128)(2,1)S(1)}, u32[]{:S(2)}, u32[]{:S(2)}) async-start(bf16[8,16,1024]{2,1,0:T(8,128)(2,1)} %bitcast.16), calls=%async_computation.2 | async-start | bytes 524288 | tf_op jit(solution)/shard_map/all_to_all | solution.py:275
  44.9 1.6 %copy-start.1 = (bf16[1024,1024]{1,0:T(8,128)(2,1)S(1)}, bf16[1024,1024]{1,0:T(8,128)(2,1)}, u32[]{:S(2)}) copy-start(bf16[1024,1024]{1,0:T(8,128)(2,1)} %copy-done) | copy-start | bytes 6291460
  46.5 0.8 %copy-start.5 = (bf16[128,256]{1,0:T(8,128)(2,1)S(1)}, bf16[128,256]{1,0:T(8,128)(2,1)}, u32[]{:S(2)}) copy-start(bf16[128,256]{1,0:T(8,128)(2,1)} %copy-done.4) | copy-start | bytes 196612
  47.3 13.4 %copy-start.3 = (bf16[256,1024]{1,0:T(8,128)(2,1)S(1)}, bf16[256,1024]{1,0:T(8,128)(2,1)}, u32[]{:S(2)}) copy-start(bf16[256,1024]{1,0:T(8,128)(2,1)} %copy-done.2) | copy-start | bytes 1572868
  60.8 2.0 %collective-permute-start.3 = (bf16[256,1024]{1,0:T(8,128)(2,1)S(1)}, bf16[256,1024]{1,0:T(8,128)(2,1)S(1)}, u32[]{:S(2)}, u32[]{:S(2)}) collective-permute-start(bf16[256,1024]{1,0:T(8,128)(2,1)S(1)} %shard_map.61), channel_id=1, source_target_pairs={{0,8},{8,0},{16,24},{24,16},{1,9},{9,1},{17,25},{25,17},{2,10},{10... | collective-permute-start | bytes 1572872 | tf_op jit(solution)/shard_map/ppermute | solution.py:262
